TPU v7x, 256 devices: a whole 4x4x8 slice. The times are simulated.
256 devices in a mesh: grow: 32 (over y_hi, z, core), gy: 4 (over x), gz: 2 (over y_lo).
Axes of the slice: x: 4, y: 4 (y_hi: 2, y_lo: 2; y = y_hi * 2 + y_lo), z: 8, core: 2. Of those that a mesh axis runs over, the one named last changes fastest.
Arguments:
- labels: int32 [1024, 32, 256], P('grow', 'gy', 'gz'), may hold values from 0 to 3
- potential: float32 [2, 1024, 32, 256], P(None, 'grow', 'gy', 'gz'), may hold values from -3 to 3
- melt_codes: int32 [16, 32, 256], P(None, 'gy', 'gz'), may hold values from 0 to 7
- melt_table: float32 [2, 8], replicated, may hold values from -1 to 1
Outputs:
- phases: float32 [4, 1024, 32, 256], P(None, 'grow', 'gy', 'gz')
- potentials: float32 [2, 1024, 32, 256], P(None, 'grow', 'gy', 'gz')
All inputs are finite; a program needn't handle non-finite values.
Results may differ from a plain program's by a relative error of at most 0.0001.
Values sent between devices are 32-bit elements; how exact they have to be, the bound alone decides.
No kernel may reach another device: no remote copies, remote signals or barrier semaphores. Data moves between devices by JAX's collectives and lax.ppermute only.
A program may use at most 64 MiB of HBM per device.

v0:
```python
import jax
import jax.numpy as jnp
from jax import lax
from jax.sharding import PartitionSpec as P

SHIFT = 16
STEPS_BEFORE = 3


comp_table = ((0.8, 0.1), (0.1, 0.8), (0.1, 0.1), (0.35, 0.35))
free_energy = (-0.05, -0.05, -0.05, 0.0)
diffusivity = (0.05, 0.05, 0.05, 1.0)
grad_rate = 0.12
well_rate = 0.3
drive_rate = 0.5
diff_rate = 0.15


def extended(value, sides, width):
    edges = {}
    for axis, dim in sides:
        count, length = (lax.axis_size(axis), value.shape[dim])
        up = [(i, (i + 1) % count) for i in range(count)]
        last = lax.slice_in_dim(value, length - width, length, axis=dim)
        first = lax.slice_in_dim(value, 0, width, axis=dim)
        edges[dim] = (
            lax.ppermute(last, axis, up),
            lax.ppermute(first, axis, [(b, a) for a, b in up]),
        )
    done = []
    for _, dim in sides:
        low, high = edges[dim]
        around = [(width, width) if d in done else (0, 0) for d in range(value.ndim)]
        value = jnp.concatenate([jnp.pad(low, around), value, jnp.pad(high, around)], axis=dim)
        done.append(dim)
    return value


def shifted_2(value, axis, steps):
    count = lax.axis_size(axis)
    first, last = (max(0, -steps), min(count, count - steps))
    return lax.ppermute(value, axis, [(source, source + steps) for source in range(first, last)])


def laplacian(fields, grow_padded, side_padded):
    total = grow_padded[:, 2:] + grow_padded[:, :-2]
    total = total + (side_padded[:, :, 2:, 1:-1] + side_padded[:, :, :-2, 1:-1])
    total = total + (side_padded[:, :, 1:-1, 2:] + side_padded[:, :, 1:-1, :-2])
    return total - 6.0 * fields


def advance(fields, grow_padded, side_padded):
    phases = fields[:4]
    chem_pot = fields[4:]
    laplace = laplacian(fields, grow_padded, side_padded)
    comp = jnp.array(comp_table, jnp.float32)
    comp_first = comp[:, 0].reshape(4, 1, 1, 1)
    comp_second = comp[:, 1].reshape(4, 1, 1, 1)
    energy = jnp.array(free_energy, jnp.float32).reshape(4, 1, 1, 1)
    spread = jnp.array(diffusivity, jnp.float32).reshape(4, 1, 1, 1)
    grand_pot = energy - (chem_pot[0:1] * comp_first + chem_pot[1:2] * comp_second)
    squares = phases * phases
    others = jnp.sum(squares, axis=0, keepdims=True) - squares
    slope = 6.0 * phases * (1.0 - phases)
    increment = (
        grad_rate * laplace[:4] - 2.0 * well_rate * phases * others - drive_rate * slope * grand_pot
    )
    increment = increment - jnp.mean(increment, axis=0, keepdims=True)
    clipped = jnp.clip(phases + increment, 0.0, 1.0)
    new_phases = clipped / jnp.sum(clipped, axis=0, keepdims=True)
    change = new_phases * new_phases * (3.0 - 2.0 * new_phases) - phases * phases * (
        3.0 - 2.0 * phases
    )
    mobility = jnp.sum(phases * spread, axis=0, keepdims=True)
    release = jnp.concatenate(
        [
            jnp.sum(change * comp_first, axis=0, keepdims=True),
            jnp.sum(change * comp_second, axis=0, keepdims=True),
        ],
        axis=0,
    )
    new_chem = chem_pot + diff_rate * mobility * laplace[4:] - release
    return jnp.concatenate([new_phases, new_chem], axis=0)


def melt_planes(melt_codes, melt_table):
    levels = melt_table.shape[1]
    onehot = (
        melt_codes[None] == jnp.arange(levels, dtype=jnp.int32).reshape(levels, 1, 1, 1)
    ).astype(jnp.float32)
    chem_pot = jnp.einsum("ik,kabc->iabc", melt_table, onehot, precision=lax.Precision.HIGHEST)
    liquid = (jnp.arange(4, dtype=jnp.int32) == 3).astype(jnp.float32).reshape(4, 1, 1, 1)
    phases = jnp.broadcast_to(liquid, (4,) + melt_codes.shape)
    return jnp.concatenate([phases, chem_pot], axis=0)


def side_faces(fields):
    return extended(fields, (("gy", 2), ("gz", 3)), 1)


def on_device(labels, potential, melt_codes, melt_table):
    index_grow = lax.axis_index("grow")
    is_first = index_grow == 0
    is_last = index_grow == lax.axis_size("grow") - 1

    def faces(fields):
        padded_all = extended(fields, (("grow", 1), ("gy", 2), ("gz", 3)), 1)
        side_padded = padded_all[:, 1:-1]
        raw_grow = padded_all[:, :, 1:-1, 1:-1]
        low_ghost = jnp.where(is_first, fields[:, :1], raw_grow[:, :1])
        top_ghost = jnp.where(is_last, fields[:, -1:], raw_grow[:, -1:])
        return (jnp.concatenate([low_ghost, fields, top_ghost], axis=1), side_padded)

    phases = (labels[None] == jnp.arange(4, dtype=jnp.int32).reshape(4, 1, 1, 1)).astype(
        jnp.float32
    )
    fields = jnp.concatenate([phases, potential], axis=0)
    for iteration in range(STEPS_BEFORE):
        grow_padded, side_padded = faces(fields)
        fields = advance(fields, grow_padded, side_padded)
    melt_block = melt_planes(melt_codes, melt_table)
    arrived = shifted_2(fields[:, : SHIFT + 1], "grow", -1)
    incoming = jnp.where(is_last, melt_block, arrived[:, :SHIFT])
    shifted = jnp.concatenate([fields[:, SHIFT:], incoming], axis=1)
    low_ghost = jnp.where(is_first, shifted[:, :1], fields[:, SHIFT - 1 : SHIFT])
    top_ghost = jnp.where(is_last, incoming[:, -1:], arrived[:, SHIFT : SHIFT + 1])
    grow_padded = jnp.concatenate([low_ghost, shifted, top_ghost], axis=1)
    fields = advance(shifted, grow_padded, side_faces(shifted))
    grow_padded, side_padded = faces(fields)
    fields = advance(fields, grow_padded, side_padded)
    return (fields[:4], fields[4:])


def solution(mesh):
    return jax.shard_map(
        on_device,
        mesh=mesh,
        in_specs=(P("grow", "gy", "gz"), P(None, "grow", "gy", "gz"), P(None, "gy", "gz"), P()),
        out_specs=(P(None, "grow", "gy", "gz"), P(None, "grow", "gy", "gz")),
        check_vma=False,
    )
```

profile of v0, /device:TPU:24, one launch (start us, length us, event | category | flops | bytes accessed | tf_op | source)
XLA Modules:
  0.0 103.4 jit_solution(12901561835729121587)
XLA Ops:
  2.6 6.0 %collective-permute-start = (f32[6,1,8,128]{3,1,2,0:T(1,128)S(1)}, f32[6,1,8,128]{3,1,2,0:T(1,128)S(1)}, u32[]{:S(2)}, u32[]{:S(2)}) collective-permute-start(f32[6,1,8,128]{3,1,2,0:T(1,128)S(1)} %fusion.119), channel_id=1, source_target_pairs={{8,0},{16,8},{24,16},{32,24},{40,32},{48,40},{56,48},{64,56},{72,6... | collective-permute-start | bytes 73736 | tf_op jit(solution)/shard_map/ppermute | solution.py:28
  9.7 2.1 %collective-permute-start.5 = (f32[6,32,8,1]{1,2,3,0:T(8,128)S(1)}, f32[6,32,8,1]{1,2,3,0:T(8,128)S(1)}, u32[]{:S(2)}, u32[]{:S(2)}) collective-permute-start(f32[6,32,8,1]{1,2,3,0:T(8,128)S(1)} %copy.54), channel_id=1, source_target_pairs={{0,1},{1,0},{2,3},{3,2},{4,5},{5,4},{6,7},{7,6},{8,9},{9,8},{10,11... | collective-permute-start | bytes 18440 | tf_op jit(solution)/shard_map/ppermute | solution.py:27
  12.5 2.8 %collective-permute-start.2 = (f32[6,32,1,128]{3,1,2,0:T(8,128)}, f32[6,32,1,128]{3,1,2,0:T(8,128)}, u32[]{:S(2)}, u32[]{:S(2)}) collective-permute-start(f32[6,32,1,128]{3,1,2,0:T(8,128)} %get-tuple-element.70), channel_id=1, source_target_pairs={{2,0},{4,2},{6,4},{0,6},{3,1},{5,3},{7,5},{1,7},{10,8},{12,10},{14... | collective-permute-start | bytes 294920 | tf_op jit(solution)/shard_map/ppermute | solution.py:28
  16.4 6.0 %collective-permute-done.1 = f32[6,1,8,128]{3,1,2,0:T(1,128)S(1)} collective-permute-done((f32[6,1,8,128]{3,1,2,0:T(1,128)S(1)}, f32[6,1,8,128]{3,1,2,0:T(1,128)S(1)}, u32[]{:S(2)}, u32[]{:S(2)}) %collective-permute-start.1) | collective-permute-done | bytes 24608 | tf_op jit(solution)/shard_map/ppermute | solution.py:27
  23.3 2.0 %fusion.19 = f32[6,32,8,128]{3,1,2,0:T(8,128)S(1)} fusion(f32[2,32,8,128]{3,1,2,0:T(8,128)S(1)} %copy.51, f32[4,32,8,128]{3,1,2,0:T(8,128)S(1)} %fusion.76, f32[6,32,8,1]{3,1,2,0:T(8,128)S(1)} %copy.55, f32[6,34,1,128]{3,1,2,0:T(8,128)S(1)} %pad.57, f32[6,34,1,128]{3,1,2,0:T(8,128)S(1)} %pad.58, f32[6,1,8,128]{3,1,2,0:T(1,128)S(1)} %collective-permute-done, ...), kind=kLoop, calls=%fused_computation.95 | loop fusion | flops 7471104 | bytes 1892352 | tf_op jit(solution)/shard_map/sub | solution.py:49
  28.1 2.1 %collective-permute-start.11 = (f32[6,32,8,1]{1,2,3,0:T(8,128)S(1)}, f32[6,32,8,1]{1,2,3,0:T(8,128)S(1)}, u32[]{:S(2)}, u32[]{:S(2)}) collective-permute-start(f32[6,32,8,1]{1,2,3,0:T(8,128)S(1)} %copy.61), channel_id=1, source_target_pairs={{0,1},{1,0},{2,3},{3,2},{4,5},{5,4},{6,7},{7,6},{8,9},{9,8},{10,11... | collective-permute-start | bytes 18440 | tf_op jit(solution)/shard_map/ppermute | solution.py:27
  30.4 3.3 %collective-permute-start.8 = (f32[6,32,1,128]{3,1,2,0:T(8,128)S(1)}, f32[6,32,1,128]{3,1,2,0:T(8,128)S(1)}, u32[]{:S(2)}, u32[]{:S(2)}) collective-permute-start(f32[6,32,1,128]{3,1,2,0:T(8,128)S(1)} %get-tuple-element.66), channel_id=1, source_target_pairs={{2,0},{4,2},{6,4},{0,6},{3,1},{5,3},{7,5},{1,7},{10,8},{12,10},{14... | collective-permute-start | bytes 294920 | tf_op jit(solution)/shard_map/ppermute | solution.py:28
  34.4 2.8 %collective-permute-done.7 = f32[6,1,8,128]{3,1,2,0:T(1,128)S(1)} collective-permute-done((f32[6,1,8,128]{3,1,2,0:T(1,128)S(1)}, f32[6,1,8,128]{3,1,2,0:T(1,128)S(1)}, u32[]{:S(2)}, u32[]{:S(2)}) %collective-permute-start.7) | collective-permute-done | bytes 24608 | tf_op jit(solution)/shard_map/ppermute | solution.py:27
  37.2 2.3 %collective-permute-done.9 = f32[6,32,1,128]{3,1,2,0:T(8,128)S(1)} collective-permute-done((f32[6,32,1,128]{3,1,2,0:T(8,128)S(1)}, f32[6,32,1,128]{3,1,2,0:T(8,128)S(1)}, u32[]{:S(2)}, u32[]{:S(2)}) %collective-permute-start.9) | collective-permute-done | bytes 98336 | tf_op jit(solution)/shard_map/ppermute | solution.py:27
  39.5 2.0 %fusion.17 = f32[6,32,8,128]{3,1,2,0:T(8,128)S(1)} fusion(f32[2,32,8,128]{3,1,2,0:T(8,128)S(1)} %fusion.91, f32[4,32,8,128]{3,1,2,0:T(8,128)S(1)} %get-tuple-element.44, f32[6,32,8,1]{3,1,2,0:T(8,128)S(1)} %copy.62, f32[6,34,1,128]{3,1,2,0:T(8,128)S(1)} %pad.61, f32[6,34,1,128]{3,1,2,0:T(8,128)S(1)} %pad.62, f32[6,1,8,128]{3,1,2,0:T(1,128)S(1)} %collective-permute-done.6, ...), kind=kLoop, calls=%fused_computation.93 | loop fusion | flops 7471104 | bytes 1892352 | tf_op jit(solution)/shard_map/sub | solution.py:49
  42.5 4.6 %collective-permute-start.12 = (f32[6,1,8,128]{3,1,2,0:T(1,128)S(1)}, f32[6,1,8,128]{3,1,2,0:T(1,128)S(1)}, u32[]{:S(2)}, u32[]{:S(2)}) collective-permute-start(f32[6,1,8,128]{3,1,2,0:T(1,128)S(1)} %fusion.115), channel_id=1, source_target_pairs={{8,0},{16,8},{24,16},{32,24},{40,32},{48,40},{56,48},{64,56},{72,6... | collective-permute-start | bytes 73736 | tf_op jit(solution)/shard_map/ppermute | solution.py:28
  48.2 2.1 %collective-permute-start.17 = (f32[6,32,8,1]{1,2,3,0:T(8,128)S(1)}, f32[6,32,8,1]{1,2,3,0:T(8,128)S(1)}, u32[]{:S(2)}, u32[]{:S(2)}) collective-permute-start(f32[6,32,8,1]{1,2,3,0:T(8,128)S(1)} %copy.65), channel_id=1, source_target_pairs={{0,1},{1,0},{2,3},{3,2},{4,5},{5,4},{6,7},{7,6},{8,9},{9,8},{10,11... | collective-permute-start | bytes 18440 | tf_op jit(solution)/shard_map/ppermute | solution.py:27
  50.6 2.0 %collective-permute-start.15 = (f32[6,32,1,128]{3,1,2,0:T(8,128)S(1)}, f32[6,32,1,128]{3,1,2,0:T(8,128)S(1)}, u32[]{:S(2)}, u32[]{:S(2)}) collective-permute-start(f32[6,32,1,128]{3,1,2,0:T(8,128)S(1)} %get-tuple-element.61), channel_id=1, source_target_pairs={{0,2},{2,4},{4,6},{6,0},{1,3},{3,5},{5,7},{7,1},{8,10},{10,12},{12... | collective-permute-start | bytes 294920 | tf_op jit(solution)/shard_map/ppermute | solution.py:27
  53.3 4.0 %collective-permute-done.13 = f32[6,1,8,128]{3,1,2,0:T(1,128)S(1)} collective-permute-done((f32[6,1,8,128]{3,1,2,0:T(1,128)S(1)}, f32[6,1,8,128]{3,1,2,0:T(1,128)S(1)}, u32[]{:S(2)}, u32[]{:S(2)}) %collective-permute-start.13) | collective-permute-done | bytes 24608 | tf_op jit(solution)/shard_map/ppermute | solution.py:27
  57.4 2.0 %fusion.15 = f32[6,32,8,128]{3,1,2,0:T(8,128)S(1)} fusion(f32[2,32,8,128]{3,1,2,0:T(8,128)S(1)} %fusion.89, f32[4,32,8,128]{3,1,2,0:T(8,128)S(1)} %get-tuple-element.39, f32[6,32,8,1]{3,1,2,0:T(8,128)S(1)} %copy.66, f32[6,34,1,128]{3,1,2,0:T(8,128)S(1)} %pad.65, f32[6,34,1,128]{3,1,2,0:T(8,128)S(1)} %pad.66, ...), kind=kLoop, calls=%fused_computation.91 | loop fusion | flops 7471104 | bytes 1892352 | tf_op jit(solution)/shard_map/sub | solution.py:49
  60.5 5.6 %collective-permute-start.18 = (f32[6,17,8,128]{3,2,1,0:T(8,128)S(1)}, f32[6,17,8,128]{3,2,1,0:T(8,128)S(1)}, u32[]{:S(2)}, u32[]{:S(2)}) collective-permute-start(f32[6,17,8,128]{3,2,1,0:T(8,128)S(1)} %copy.68), channel_id=1, source_target_pairs={{8,0},{16,8},{24,16},{32,24},{40,32},{48,40},{56,48},{64,56},{72,6... | collective-permute-start | bytes 1253384 | tf_op jit(solution)/shard_map/ppermute | solution.py:42
  66.6 5.0 %collective-permute-done.18 = f32[6,17,8,128]{3,2,1,0:T(8,128)S(1)} collective-permute-done((f32[6,17,8,128]{3,2,1,0:T(8,128)S(1)}, f32[6,17,8,128]{3,2,1,0:T(8,128)S(1)}, u32[]{:S(2)}, u32[]{:S(2)}) %collective-permute-start.18) | collective-permute-done | bytes 417824 | tf_op jit(solution)/shard_map/ppermute | solution.py:42
  73.0 2.0 %collective-permute-start.20 = (f32[6,32,1,128]{3,1,2,0:T(8,128)}, f32[6,32,1,128]{3,1,2,0:T(8,128)S(1)}, u32[]{:S(2)}, u32[]{:S(2)}) collective-permute-start(f32[6,32,1,128]{3,1,2,0:T(8,128)} %get-tuple-element.55), channel_id=1, source_target_pairs={{0,2},{2,4},{4,6},{6,0},{1,3},{3,5},{5,7},{7,1},{8,10},{10,12},{12... | collective-permute-start | bytes 294920 | tf_op jit(solution)/shard_map/ppermute | solution.py:27
  76.3 2.1 %collective-permute-start.22 = (f32[6,32,8,1]{1,2,3,0:T(8,128)S(1)}, f32[6,32,8,1]{1,2,3,0:T(8,128)}, u32[]{:S(2)}, u32[]{:S(2)}) collective-permute-start(f32[6,32,8,1]{1,2,3,0:T(8,128)S(1)} %copy.73), channel_id=1, source_target_pairs={{0,1},{1,0},{2,3},{3,2},{4,5},{5,4},{6,7},{7,6},{8,9},{9,8},{10,11... | collective-permute-start | bytes 18440 | tf_op jit(solution)/shard_map/ppermute | solution.py:27
  78.4 1.6 %collective-permute-done.21 = f32[6,32,8,1]{1,2,3,0:T(8,128)S(1)} collective-permute-done((f32[6,32,8,1]{1,2,3,0:T(8,128)}, f32[6,32,8,1]{1,2,3,0:T(8,128)S(1)}, u32[]{:S(2)}, u32[]{:S(2)}) %collective-permute-start.21) | collective-permute-done | bytes 6176 | tf_op jit(solution)/shard_map/ppermute | solution.py:28
  83.2 4.3 %collective-permute-start.23 = (f32[6,1,8,128]{3,1,2,0:T(1,128)S(1)}, f32[6,1,8,128]{3,1,2,0:T(1,128)S(1)}, u32[]{:S(2)}, u32[]{:S(2)}) collective-permute-start(f32[6,1,8,128]{3,1,2,0:T(1,128)S(1)} %fusion.113), channel_id=1, source_target_pairs={{8,0},{16,8},{24,16},{32,24},{40,32},{48,40},{56,48},{64,56},{72,6... | collective-permute-start | bytes 73736 | tf_op jit(solution)/shard_map/ppermute | solution.py:28
  90.8 1.9 %collective-permute-start.25 = (f32[6,32,1,128]{3,1,2,0:T(8,128)S(1)}, f32[6,32,1,128]{3,1,2,0:T(8,128)S(1)}, u32[]{:S(2)}, u32[]{:S(2)}) collective-permute-start(f32[6,32,1,128]{3,1,2,0:T(8,128)S(1)} %get-tuple-element.52), channel_id=1, source_target_pairs={{2,0},{4,2},{6,4},{0,6},{3,1},{5,3},{7,5},{1,7},{10,8},{12,10},{14... | collective-permute-start | bytes 294920 | tf_op jit(solution)/shard_map/ppermute | solution.py:28
  93.6 4.0 %collective-permute-done.24 = f32[6,1,8,128]{3,1,2,0:T(1,128)S(1)} collective-permute-done((f32[6,1,8,128]{3,1,2,0:T(1,128)S(1)}, f32[6,1,8,128]{3,1,2,0:T(1,128)S(1)}, u32[]{:S(2)}, u32[]{:S(2)}) %collective-permute-start.24) | collective-permute-done | bytes 24608 | tf_op jit(solution)/shard_map/ppermute | solution.py:27
  98.5 2.0 %fusion.13 = f32[6,32,8,128]{3,1,2,0:T(8,128)S(1)} fusion(f32[2,32,8,128]{3,1,2,0:T(8,128)S(1)} %fusion.83, f32[4,32,8,128]{3,1,2,0:T(8,128)S(1)} %get-tuple-element.29, f32[6,32,8,1]{3,1,2,0:T(8,128)S(1)} %copy.78, f32[6,34,1,128]{3,1,2,0:T(8,128)S(1)} %pad.71, f32[6,34,1,128]{3,1,2,0:T(8,128)S(1)} %pad.72, ...), kind=kLoop, calls=%fused_computation.89 | loop fusion | flops 7471104 | bytes 1892352 | tf_op jit(solution)/shard_map/sub | solution.py:49
  (159 shorter events, 27.6 us)
Async XLA Ops:
  2.6 12.7 %collective-permute-start = (f32[6,1,8,128]{3,1,2,0:T(1,128)S(1)}, f32[6,1,8,128]{3,1,2,0:T(1,128)S(1)}, u32[]{:S(2)}, u32[]{:S(2)}) collective-permute-start(f32[6,1,8,128]{3,1,2,0:T(1,128)S(1)} %fusion.119), channel_id=1, source_target_pairs={{8,0},{16,8},{24,16},{32,24},{40,32},{48,40},{56,48},{64,56},{72,6... | collective-permute-start | bytes 73736 | tf_op jit(solution)/shard_map/ppermute | solution.py:28
  9.3 6.3 %collective-permute-start.4 = (f32[6,32,8,1]{1,2,3,0:T(8,128)S(1)}, f32[6,32,8,1]{1,2,3,0:T(8,128)S(1)}, u32[]{:S(2)}, u32[]{:S(2)}) collective-permute-start(f32[6,32,8,1]{1,2,3,0:T(8,128)S(1)} %copy.52), channel_id=1, source_target_pairs={{1,0},{0,1},{3,2},{2,3},{5,4},{4,5},{7,6},{6,7},{9,8},{8,9},{11,10... | collective-permute-start | bytes 18440 | tf_op jit(solution)/shard_map/ppermute | solution.py:28
  9.7 6.2 %collective-permute-start.5 = (f32[6,32,8,1]{1,2,3,0:T(8,128)S(1)}, f32[6,32,8,1]{1,2,3,0:T(8,128)S(1)}, u32[]{:S(2)}, u32[]{:S(2)}) collective-permute-start(f32[6,32,8,1]{1,2,3,0:T(8,128)S(1)} %copy.54), channel_id=1, source_target_pairs={{0,1},{1,0},{2,3},{3,2},{4,5},{5,4},{6,7},{7,6},{8,9},{9,8},{10,11... | collective-permute-start | bytes 18440 | tf_op jit(solution)/shard_map/ppermute | solution.py:27
  12.5 9.8 %collective-permute-start.2 = (f32[6,32,1,128]{3,1,2,0:T(8,128)}, f32[6,32,1,128]{3,1,2,0:T(8,128)}, u32[]{:S(2)}, u32[]{:S(2)}) collective-permute-start(f32[6,32,1,128]{3,1,2,0:T(8,128)} %get-tuple-element.70), channel_id=1, source_target_pairs={{2,0},{4,2},{6,4},{0,6},{3,1},{5,3},{7,5},{1,7},{10,8},{12,10},{14... | collective-permute-start | bytes 294920 | tf_op jit(solution)/shard_map/ppermute | solution.py:28
  15.3 8.0 %collective-permute-start.3 = (f32[6,32,1,128]{3,1,2,0:T(8,128)}, f32[6,32,1,128]{3,1,2,0:T(8,128)S(1)}, u32[]{:S(2)}, u32[]{:S(2)}) collective-permute-start(f32[6,32,1,128]{3,1,2,0:T(8,128)} %get-tuple-element.69), channel_id=1, source_target_pairs={{0,2},{2,4},{4,6},{6,0},{1,3},{3,5},{5,7},{7,1},{8,10},{10,12},{12... | collective-permute-start | bytes 294920 | tf_op jit(solution)/shard_map/ppermute | solution.py:27
  15.4 6.9 %collective-permute-start.1 = (f32[6,1,8,128]{3,1,2,0:T(1,128)S(1)}, f32[6,1,8,128]{3,1,2,0:T(1,128)S(1)}, u32[]{:S(2)}, u32[]{:S(2)}) collective-permute-start(f32[6,1,8,128]{3,1,2,0:T(1,128)S(1)} %get-tuple-element.48), channel_id=1, source_target_pairs={{0,8},{8,16},{16,24},{24,32},{32,40},{40,48},{48,56},{56,64},{64,7... | collective-permute-start | bytes 73736 | tf_op jit(solution)/shard_map/ppermute | solution.py:27
  27.7 6.0 %collective-permute-start.10 = (f32[6,32,8,1]{1,2,3,0:T(8,128)S(1)}, f32[6,32,8,1]{1,2,3,0:T(8,128)S(1)}, u32[]{:S(2)}, u32[]{:S(2)}) collective-permute-start(f32[6,32,8,1]{1,2,3,0:T(8,128)S(1)} %copy.59), channel_id=1, source_target_pairs={{1,0},{0,1},{3,2},{2,3},{5,4},{4,5},{7,6},{6,7},{9,8},{8,9},{11,10... | collective-permute-start | bytes 18440 | tf_op jit(solution)/shard_map/ppermute | solution.py:28
  28.1 5.9 %collective-permute-start.11 = (f32[6,32,8,1]{1,2,3,0:T(8,128)S(1)}, f32[6,32,8,1]{1,2,3,0:T(8,128)S(1)}, u32[]{:S(2)}, u32[]{:S(2)}) collective-permute-start(f32[6,32,8,1]{1,2,3,0:T(8,128)S(1)} %copy.61), channel_id=1, source_target_pairs={{0,1},{1,0},{2,3},{3,2},{4,5},{5,4},{6,7},{7,6},{8,9},{9,8},{10,11... | collective-permute-start | bytes 18440 | tf_op jit(solution)/shard_map/ppermute | solution.py:27
  30.3 6.9 %collective-permute-start.7 = (f32[6,1,8,128]{3,1,2,0:T(1,128)S(1)}, f32[6,1,8,128]{3,1,2,0:T(1,128)S(1)}, u32[]{:S(2)}, u32[]{:S(2)}) collective-permute-start(f32[6,1,8,128]{3,1,2,0:T(1,128)S(1)} %get-tuple-element.43), channel_id=1, source_target_pairs={{0,8},{8,16},{16,24},{24,32},{32,40},{40,48},{48,56},{56,64},{64,7... | collective-permute-start | bytes 73736 | tf_op jit(solution)/shard_map/ppermute | solution.py:27
  30.4 6.8 %collective-permute-start.8 = (f32[6,32,1,128]{3,1,2,0:T(8,128)S(1)}, f32[6,32,1,128]{3,1,2,0:T(8,128)S(1)}, u32[]{:S(2)}, u32[]{:S(2)}) collective-permute-start(f32[6,32,1,128]{3,1,2,0:T(8,128)S(1)} %get-tuple-element.66), channel_id=1, source_target_pairs={{2,0},{4,2},{6,4},{0,6},{3,1},{5,3},{7,5},{1,7},{10,8},{12,10},{14... | collective-permute-start | bytes 294920 | tf_op jit(solution)/shard_map/ppermute | solution.py:28
  33.7 5.8 %collective-permute-start.9 = (f32[6,32,1,128]{3,1,2,0:T(8,128)S(1)}, f32[6,32,1,128]{3,1,2,0:T(8,128)S(1)}, u32[]{:S(2)}, u32[]{:S(2)}) collective-permute-start(f32[6,32,1,128]{3,1,2,0:T(8,128)S(1)} %get-tuple-element.65), channel_id=1, source_target_pairs={{0,2},{2,4},{4,6},{6,0},{1,3},{3,5},{5,7},{7,1},{8,10},{10,12},{12... | collective-permute-start | bytes 294920 | tf_op jit(solution)/shard_map/ppermute | solution.py:27
  42.5 7.8 %collective-permute-start.12 = (f32[6,1,8,128]{3,1,2,0:T(1,128)S(1)}, f32[6,1,8,128]{3,1,2,0:T(1,128)S(1)}, u32[]{:S(2)}, u32[]{:S(2)}) collective-permute-start(f32[6,1,8,128]{3,1,2,0:T(1,128)S(1)} %fusion.115), channel_id=1, source_target_pairs={{8,0},{16,8},{24,16},{32,24},{40,32},{48,40},{56,48},{64,56},{72,6... | collective-permute-start | bytes 73736 | tf_op jit(solution)/shard_map/ppermute | solution.py:28
  47.8 4.8 %collective-permute-start.16 = (f32[6,32,8,1]{1,2,3,0:T(8,128)S(1)}, f32[6,32,8,1]{1,2,3,0:T(8,128)S(1)}, u32[]{:S(2)}, u32[]{:S(2)}) collective-permute-start(f32[6,32,8,1]{1,2,3,0:T(8,128)S(1)} %copy.63), channel_id=1, source_target_pairs={{1,0},{0,1},{3,2},{2,3},{5,4},{4,5},{7,6},{6,7},{9,8},{8,9},{11,10... | collective-permute-start | bytes 18440 | tf_op jit(solution)/shard_map/ppermute | solution.py:28
  50.4 6.9 %collective-permute-start.13 = (f32[6,1,8,128]{3,1,2,0:T(1,128)S(1)}, f32[6,1,8,128]{3,1,2,0:T(1,128)S(1)}, u32[]{:S(2)}, u32[]{:S(2)}) collective-permute-start(f32[6,1,8,128]{3,1,2,0:T(1,128)S(1)} %get-tuple-element.38), channel_id=1, source_target_pairs={{0,8},{8,16},{16,24},{24,32},{32,40},{40,48},{48,56},{56,64},{64,7... | collective-permute-start | bytes 73736 | tf_op jit(solution)/shard_map/ppermute | solution.py:27
  50.5 6.8 %collective-permute-start.14 = (f32[6,32,1,128]{3,1,2,0:T(8,128)S(1)}, f32[6,32,1,128]{3,1,2,0:T(8,128)S(1)}, u32[]{:S(2)}, u32[]{:S(2)}) collective-permute-start(f32[6,32,1,128]{3,1,2,0:T(8,128)S(1)} %get-tuple-element.62), channel_id=1, source_target_pairs={{2,0},{4,2},{6,4},{0,6},{3,1},{5,3},{7,5},{1,7},{10,8},{12,10},{14... | collective-permute-start | bytes 294920 | tf_op jit(solution)/shard_map/ppermute | solution.py:28
  50.6 6.8 %collective-permute-start.15 = (f32[6,32,1,128]{3,1,2,0:T(8,128)S(1)}, f32[6,32,1,128]{3,1,2,0:T(8,128)S(1)}, u32[]{:S(2)}, u32[]{:S(2)}) collective-permute-start(f32[6,32,1,128]{3,1,2,0:T(8,128)S(1)} %get-tuple-element.61), channel_id=1, source_target_pairs={{0,2},{2,4},{4,6},{6,0},{1,3},{3,5},{5,7},{7,1},{8,10},{10,12},{12... | collective-permute-start | bytes 294920 | tf_op jit(solution)/shard_map/ppermute | solution.py:27
  60.5 11.1 %collective-permute-start.18 = (f32[6,17,8,128]{3,2,1,0:T(8,128)S(1)}, f32[6,17,8,128]{3,2,1,0:T(8,128)S(1)}, u32[]{:S(2)}, u32[]{:S(2)}) collective-permute-start(f32[6,17,8,128]{3,2,1,0:T(8,128)S(1)} %copy.68), channel_id=1, source_target_pairs={{8,0},{16,8},{24,16},{32,24},{40,32},{48,40},{56,48},{64,56},{72,6... | collective-permute-start | bytes 1253384 | tf_op jit(solution)/shard_map/ppermute | solution.py:42
  72.9 8.6 %collective-permute-start.19 = (f32[6,32,1,128]{3,1,2,0:T(8,128)}, f32[6,32,1,128]{3,1,2,0:T(8,128)S(1)}, u32[]{:S(2)}, u32[]{:S(2)}) collective-permute-start(f32[6,32,1,128]{3,1,2,0:T(8,128)} %get-tuple-element.56), channel_id=1, source_target_pairs={{2,0},{4,2},{6,4},{0,6},{3,1},{5,3},{7,5},{1,7},{10,8},{12,10},{14... | collective-permute-start | bytes 294920 | tf_op jit(solution)/shard_map/ppermute | solution.py:28
  73.0 8.5 %collective-permute-start.20 = (f32[6,32,1,128]{3,1,2,0:T(8,128)}, f32[6,32,1,128]{3,1,2,0:T(8,128)S(1)}, u32[]{:S(2)}, u32[]{:S(2)}) collective-permute-start(f32[6,32,1,128]{3,1,2,0:T(8,128)} %get-tuple-element.55), channel_id=1, source_target_pairs={{0,2},{2,4},{4,6},{6,0},{1,3},{3,5},{5,7},{7,1},{8,10},{10,12},{12... | collective-permute-start | bytes 294920 | tf_op jit(solution)/shard_map/ppermute | solution.py:27
  83.2 7.4 %collective-permute-start.23 = (f32[6,1,8,128]{3,1,2,0:T(1,128)S(1)}, f32[6,1,8,128]{3,1,2,0:T(1,128)S(1)}, u32[]{:S(2)}, u32[]{:S(2)}) collective-permute-start(f32[6,1,8,128]{3,1,2,0:T(1,128)S(1)} %fusion.113), channel_id=1, source_target_pairs={{8,0},{16,8},{24,16},{32,24},{40,32},{48,40},{56,48},{64,56},{72,6... | collective-permute-start | bytes 73736 | tf_op jit(solution)/shard_map/ppermute | solution.py:28
  88.1 4.8 %collective-permute-start.27 = (f32[6,32,8,1]{1,2,3,0:T(8,128)S(1)}, f32[6,32,8,1]{1,2,3,0:T(8,128)S(1)}, u32[]{:S(2)}, u32[]{:S(2)}) collective-permute-start(f32[6,32,8,1]{1,2,3,0:T(8,128)S(1)} %copy.75), channel_id=1, source_target_pairs={{1,0},{0,1},{3,2},{2,3},{5,4},{4,5},{7,6},{6,7},{9,8},{8,9},{11,10... | collective-permute-start | bytes 18440 | tf_op jit(solution)/shard_map/ppermute | solution.py:28
  90.7 6.9 %collective-permute-start.24 = (f32[6,1,8,128]{3,1,2,0:T(1,128)S(1)}, f32[6,1,8,128]{3,1,2,0:T(1,128)S(1)}, u32[]{:S(2)}, u32[]{:S(2)}) collective-permute-start(f32[6,1,8,128]{3,1,2,0:T(1,128)S(1)} %get-tuple-element.28), channel_id=1, source_target_pairs={{0,8},{8,16},{16,24},{24,32},{32,40},{40,48},{48,56},{56,64},{64,7... | collective-permute-start | bytes 73736 | tf_op jit(solution)/shard_map/ppermute | solution.py:27
  90.8 6.8 %collective-permute-start.25 = (f32[6,32,1,128]{3,1,2,0:T(8,128)S(1)}, f32[6,32,1,128]{3,1,2,0:T(8,128)S(1)}, u32[]{:S(2)}, u32[]{:S(2)}) collective-permute-start(f32[6,32,1,128]{3,1,2,0:T(8,128)S(1)} %get-tuple-element.52), channel_id=1, source_target_pairs={{2,0},{4,2},{6,4},{0,6},{3,1},{5,3},{7,5},{1,7},{10,8},{12,10},{14... | collective-permute-start | bytes 294920 | tf_op jit(solution)/shard_map/ppermute | solution.py:28
  92.7 5.8 %collective-permute-start.26 = (f32[6,32,1,128]{3,1,2,0:T(8,128)S(1)}, f32[6,32,1,128]{3,1,2,0:T(8,128)S(1)}, u32[]{:S(2)}, u32[]{:S(2)}) collective-permute-start(f32[6,32,1,128]{3,1,2,0:T(8,128)S(1)} %get-tuple-element.51), channel_id=1, source_target_pairs={{0,2},{2,4},{4,6},{6,0},{1,3},{3,5},{5,7},{7,1},{8,10},{10,12},{12... | collective-permute-start | bytes 294920 | tf_op jit(solution)/shard_map/ppermute | solution.py:27
  (12 other events, 98.9 us)
where the time goes:
time: 104 us; the launch traced here: 103 us
  starting transfers between devices  44.1 us (42%)
  waiting for transfers between devices  26.5 us (25%)
  other arithmetic  16.9 us (16%)
  local copies, waits for them, and re-layouts  14.1 us (14%)
  between operations  1.41 us (1%)
    ppermute x14, starting transfers between devices, extended(): lax.ppermute(first, axis, [(b, a) for a, b in up])  24.3 us
    ppermute x14, waiting for transfers between devices, extended(): lax.ppermute(last, axis, up)  19.9 us
    ppermute x14, starting transfers between devices, extended(): lax.ppermute(last, axis, up)  14.2 us
    sub x5, other arithmetic, laplacian(): return total - 6.0 * fields  8.69 us
    ppermute x1, starting transfers between devices, shifted_2(): lax.ppermute(value, axis, [(source, source + steps) for source in range(f...  5.6 us
    ppermute x1, waiting for transfers between devices, shifted_2(): lax.ppermute(value, axis, [(source, source + steps) for source in range(f...  5 us
    unnamed x18, local copies, waits for them, and re-layouts  4.41 us
    ppermute x5, local copies, waits for them, and re-layouts, extended(): lax.ppermute(last, axis, up)  2.55 us
  transfers between devices with their start and end apart: 29, of which 8 were waited for; matrix products, arithmetic and copies ran while one was open for 12% of the time, Pallas kernels for 0%

commit v1 on v0

v1 whole, which is shorter than its diff:
```python
import jax
import jax.numpy as jnp
from jax import lax
from jax.experimental import pallas as pl
from jax.experimental.pallas import tpu as pltpu
from jax.sharding import PartitionSpec as P

K = 5.0**0.5
ALPHA = 5.0 * K**3
BETA = 2.5 / (K * ALPHA)
TOP = K / 0.12
DRIFT = 0.15 / (0.12 * K)
HALF = 0.5 * K**3

SHIFT = 16
OWN = 21
PLANES = 2 * OWN
PITCH = 32
ROW0 = 12
DEEP = 5
PACK = 11
AXES = ("grow", "gy", "gz")
VMEM = pl.BlockSpec(memory_space=pltpu.VMEM)
SMEM = pl.BlockSpec(memory_space=pltpu.SMEM)


def lanes():
    return lax.broadcasted_iota(jnp.int32, (8, 128), 1)


def first_pack(where_ref, labels, potential, codes, table, upper, edges):
    first = where_ref[0] == 0

    @pl.when(first)
    def _():
        for e in range(OWN):
            upper[0, e] = jnp.full((8, 128), 3.0, jnp.float32)
            for i in range(2):
                value = jnp.zeros((8, 128), jnp.float32)
                if e < SHIFT:
                    code = codes[e]
                    for level in range(8):
                        value = jnp.where(code == level, table[i, level], value)
                upper[1 + i, e] = value

    @pl.when(jnp.logical_not(first))
    def _():
        for e in range(OWN):
            upper[0, e] = labels[e].astype(jnp.float32)
            for i in range(2):
                upper[1 + i, e] = potential[i, e]

    lane = lanes()
    for f in range(3):

        def own(p, f=f):
            return labels[p].astype(jnp.float32) if f == 0 else potential[f - 1, p]

        groups = (
            [upper[f, e] for e in range(PACK)],
            [upper[f, e] for e in range(PACK, OWN)],
            [own(p) for p in range(11, 22)],
            [own(p) for p in range(22, 32)],
        )
        for q, group in enumerate(groups):
            total = jnp.zeros((8, 128), jnp.float32)
            for c, tile in enumerate(group):
                there = (lane >= 10 * c) & (lane < 10 * c + 10)
                total = jnp.where(there, pltpu.roll(tile, (10 * c + 5) % 128, 1), total)
            edges[f, q] = total


def second_pack(labels, potential, upper, across, grow, own_lo, own_hi, up_lo, up_hi):
    for f in range(3):
        for p in range(OWN + 2):
            n = 5 * (f * (OWN + 2) + p)
            tile = upper[f, p] if p < OWN else across[f, p - OWN]
            grow[f, p] = tile
            up_lo[n : n + 5] = tile[0:5]
            up_hi[n : n + 5] = tile[3:8]
            if p >= OWN:
                tile = across[f, p - OWN + 2]
            elif f == 0:
                tile = labels[p + 11].astype(jnp.float32)
            else:
                tile = potential[f - 1, p + 11]
            own_lo[n : n + 5] = tile[0:5]
            own_hi[n : n + 5] = tile[3:8]


def react(phases, sums, chem, chem_sums, held):
    p0, p1, p2 = phases
    p3 = K - ((p0 + p1) + p2)
    n3 = 6.0 * K - ((sums[0] + sums[1]) + sums[2])
    ps = (p0, p1, p2, p3)
    ns = (sums[0], sums[1], sums[2], n3)
    squares = [p * p for p in ps]
    base = (0.28 / 0.12) - ((squares[0] + squares[1]) + (squares[2] + squares[3]))
    m0, m1 = chem
    both = BETA * (m0 + m1)
    w2 = both + DRIFT
    ws = (w2 + (7.0 * BETA) * m0, w2 + (7.0 * BETA) * m1, w2, 3.5 * both)
    moved = [
        ns[a] + ps[a] * ((base + squares[a]) + ws[a] * (K - ps[a])) for a in range(4)
    ]
    excess = 0.25 * ((moved[0] + moved[1]) + (moved[2] + moved[3])) - 0.25 * TOP
    clipped = [jnp.minimum(jnp.maximum(u - excess, 0.0), TOP) for u in moved]
    scale = K / ((clipped[0] + clipped[1]) + (clipped[2] + clipped[3]))
    new = [s * scale for s in clipped]
    h = [x * x * (1.5 * K - x) for x in new]
    shared = (h[0] + h[1]) + (h[2] + 3.5 * h[3])
    solute = (shared + 7.0 * h[0], shared + 7.0 * h[1])
    mobility = 0.0075 + (0.1425 / K) * p3
    new_held = [held[i] + mobility * (chem_sums[i] - 6.0 * chem[i]) for i in range(2)]
    new_chem = [new_held[i] - solute[i] for i in range(2)]
    return new, new_chem, new_held


def evolve(
    where_ref, labels, potential, across, grow, own_lo, own_hi, up_lo, up_hi,
    phases_out, chem_out, one, two,
):
    first = where_ref[0] == 0
    last = where_ref[0] == where_ref[1] - 1
    lane = lanes()

    def start(dst, z, p, rows, label, m0, m1):
        solids = [jnp.where(label == a, K, 0.0) for a in range(3)]
        for a in range(3):
            dst[a, z, p, rows, :] = solids[a]
        melt = jnp.where(label == 3.0, 3.5 * HALF, HALF)
        for i, m in enumerate((m0, m1)):
            m = ALPHA * m
            dst[3 + i, z, p, rows, :] = m
            dst[5 + i, z, p, rows, :] = m + jnp.where(label == i, 8.0 * HALF, melt)

    def fill(dst, p):
        low = p < OWN
        s = p if low else p - OWN
        q, c = divmod(s, PACK)
        for z in range(2):

            def turned(x, z=z):
                return pltpu.roll(x, (123 - 10 * c) % 128, 1) if z else x

            body = []
            for f in range(3):
                if z:
                    tile = across[f, q + 2] if low else grow[f, OWN + q]
                elif not low:
                    tile = grow[f, s]
                elif f == 0:
                    tile = labels[s + 11].astype(jnp.float32)
                else:
                    tile = potential[f - 1, s + 11]
                body.append(turned(tile))
            start(dst, z, p, slice(ROW0, ROW0 + 8), *body)
            at = OWN + q if z else s
            for ref, row in ((own_lo if low else up_lo, 8), (own_hi if low else up_hi, -5)):
                body = []
                for f in range(3):
                    n = 5 * (f * (OWN + 2) + at)
                    body.append(turned(ref[n : n + 5]))
                start(dst, z, p, slice(ROW0 + row, ROW0 + row + 5), *body)

    def repeat(ref, p, source):
        for f in range(5):
            for z in range(2):
                ref[f, z, p, 7:25, :] = ref[f, z, source, 7:25, :]

    def gather(src, f, z, p, row):
        rows = slice(row, row + 8)
        here = src[f, z, p, rows, :]
        there = src[f, 1 - z, p, rows, :]
        total = src[f, z, p - 1, rows, :] + src[f, z, p + 1, rows, :]
        total = total + (
            src[f, z, p, row - 1 : row + 7, :] + src[f, z, p, row + 1 : row + 9, :]
        )
        left = pltpu.roll(jnp.where(lane == 127, there, here), 1, 1)
        right = pltpu.roll(jnp.where(lane == 0, there, here), 127, 1)
        return here, total + (left + right)

    def tile_step(src, z, p, row):
        pairs = [gather(src, f, z, p, row) for f in range(5)]
        held = [src[f, z, p, row : row + 8, :] for f in (5, 6)]
        here = [a for a, _ in pairs]
        sums = [b for _, b in pairs]
        return react(here[:3], sums[:3], here[3:], sums[3:], held)

    def sweep(src, dst, s):
        count = PLANES - 2 * s

        @pl.loop(s, PLANES - s, unroll=4 if count % 4 == 0 else 2)
        def _(p):
            for z in range(2):
                for row in (8, 16):
                    new, chem, held = tile_step(src, z, p, row)
                    for f, value in enumerate((*new[:3], *chem, *held)):
                        dst[f, z, p, row : row + 8, :] = value

    for p in range(PLANES):
        fill(one, p)
    src, dst = one, two
    for s in range(1, 4):

        @pl.when(last)
        def _(src=src):
            repeat(src, OWN, OWN - 1)

        sweep(src, dst, s)
        src, dst = dst, src

    @pl.when(last)
    def _(src=src):
        for p in range(OWN, OWN + SHIFT):
            fill(src, p)
        repeat(src, OWN + SHIFT, OWN + SHIFT - 1)

    @pl.when(first)
    def _(src=src):
        repeat(src, 4, 5)

    sweep(src, dst, 4)
    src, dst = dst, src

    @pl.when(last)
    def _(src=src):
        repeat(src, OWN + SHIFT, OWN + SHIFT - 1)

    @pl.when(first)
    def _(src=src):
        repeat(src, 4, 5)

    @pl.loop(5, PLANES - 5, unroll=4)
    def _(p):
        new, chem, _ = tile_step(src, 0, p, ROW0)
        for a in range(4):
            phases_out[a, p - 5] = new[a] * (1.0 / K)
        for i in range(2):
            chem_out[i, p - 5] = chem[i] * (1.0 / ALPHA)


def on_device(labels, potential, melt_codes, melt_table):
    n_grow, n_gy, n_gz = (lax.axis_size(a) for a in AXES)
    where = jnp.stack([lax.axis_index("grow"), n_grow]).astype(jnp.int32)

    def send(value, dg, dy, dz):
        pairs = []
        for g in range(n_grow):
            for y in range(n_gy):
                for z in range(n_gz):
                    to = ((g + dg) % n_grow * n_gy + (y + dy) % n_gy) * n_gz + (z + dz) % n_gz
                    pairs.append(((g * n_gy + y) * n_gz + z, to))
        return lax.ppermute(value, AXES, pairs)

    def f32(*shape):
        return jax.ShapeDtypeStruct(shape, jnp.float32)

    params = pltpu.CompilerParams(vmem_limit_bytes=48 << 20)
    upper, edges = pl.pallas_call(
        first_pack,
        in_specs=[SMEM, VMEM, VMEM, VMEM, SMEM],
        out_specs=[VMEM, VMEM],
        out_shape=[f32(3, OWN, 8, 128), f32(3, 4, 8, 128)],
        compiler_params=params,
        name="first_pack",
    )(where, labels, potential, melt_codes, melt_table)
    across = send(edges, 0, 0, 1)
    rows = 5 * 3 * (OWN + 2)
    grow, own_lo, own_hi, up_lo, up_hi = pl.pallas_call(
        second_pack,
        in_specs=[VMEM] * 4,
        out_specs=[VMEM] * 5,
        out_shape=[f32(3, OWN + 2, 8, 128)] + [f32(rows, 128)] * 4,
        compiler_params=params,
        name="second_pack",
    )(labels, potential, upper, across)
    own_lo = send(own_lo, 0, -1, 0)
    own_hi = send(own_hi, 0, 1, 0)
    grow = send(grow, -1, 0, 0)
    up_lo = send(up_lo, -1, -1, 0)
    up_hi = send(up_hi, -1, 1, 0)
    held = pltpu.VMEM((7, 2, PLANES, PITCH, 128), jnp.float32)
    return pl.pallas_call(
        evolve,
        in_specs=[SMEM] + [VMEM] * 8,
        out_specs=[VMEM, VMEM],
        out_shape=[f32(4, 32, 8, 128), f32(2, 32, 8, 128)],
        scratch_shapes=[held, held],
        compiler_params=params,
        name="evolve",
    )(where, labels, potential, across, grow, own_lo, own_hi, up_lo, up_hi)


def solution(mesh):
    return jax.shard_map(
        on_device,
        mesh=mesh,
        in_specs=(P("grow", "gy", "gz"), P(None, "grow", "gy", "gz"), P(None, "gy", "gz"), P()),
        out_specs=(P(None, "grow", "gy", "gz"), P(None, "grow", "gy", "gz")),
        check_vma=False,
    )
```

time: 104 us -> 46.6 us (0.45)
  the two profiles are of different devices: /device:TPU:24 before, /device:TPU:1 now
where the time goes in v1:
time: 46.6 us; the launch traced here: 46.4 us
  Pallas kernels  17.1 us (37%)
  starting transfers between devices  16.7 us (36%)
  waiting for transfers between devices  8.61 us (18%)
  local copies, waits for them, and re-layouts  3.29 us (7%)
  between operations  0.67 us (1%)
    ppermute x6, starting transfers between devices, send(): return lax.ppermute(value, AXES, pairs)  16.7 us
    pallas_call x1, Pallas kernels, on_device(): pl.pallas_call(evolve, in_specs=[SMEM] + [VMEM] * 8, out_specs=[VMEM, VME...  16.2 us
    ppermute x6, waiting for transfers between devices, send(): return lax.ppermute(value, AXES, pairs)  8.61 us
    unnamed x10, local copies, waits for them, and re-layouts  3.29 us
  transfers between devices with their start and end apart: 6, of which 3 were waited for; matrix products, arithmetic and copies ran while one was open for 0% of the time, Pallas kernels for 0%

profile of v1, /device:TPU:1, one launch (start us, length us, event | category | flops | bytes accessed | tf_op | source)
XLA Modules:
  0.0 46.4 jit_solution(3032751503223479393)
XLA Ops:
  0.6 0.0 copy-start.4
  0.6 0.1 pad_add_fusion.where_ref
  0.7 0.6 %copy-done.4 = f32[2,8]{1,0:T(2,128)S(1)} copy-done((f32[2,8]{1,0:T(2,128)S(1)}, f32[2,8]{1,0:T(2,128)}, u32[]{:S(2)}) %copy-start.4) | copy-done | bytes 88
  1.3 0.0 copy-start
  1.3 0.9 %copy-done = f32[2,32,8,128]{3,2,1,0:T(8,128)S(1)} copy-done((f32[2,32,8,128]{3,2,1,0:T(8,128)S(1)}, f32[2,32,8,128]{3,2,1,0:T(8,128)}, u32[]{:S(2)}) %copy-start) | copy-done | bytes 262168
  2.3 0.0 copy-start.2
  2.3 0.9 %copy-done.2 = s32[32,8,128]{2,1,0:T(8,128)S(1)} copy-done((s32[32,8,128]{2,1,0:T(8,128)S(1)}, s32[32,8,128]{2,1,0:T(8,128)}, u32[]{:S(2)}) %copy-start.2) | copy-done | bytes 131096
  3.2 0.8 %copy-done.3 = s32[16,8,128]{2,1,0:T(8,128)S(1)} copy-done((s32[16,8,128]{2,1,0:T(8,128)S(1)}, s32[16,8,128]{2,1,0:T(8,128)}, u32[]{:S(2)}) %copy-start.3) | copy-done | bytes 65560
  4.0 0.8 %first_pack.1 = (f32[3,21,8,128]{3,2,1,0:T(8,128)S(1)}, f32[3,4,8,128]{3,2,1,0:T(8,128)S(1)}) custom-call(s32[2]{0:T(128)S(1)} %pad_add_fusion.where_ref, s32[32,8,128]{2,1,0:T(8,128)S(1)} %copy-done.2, f32[2,32,8,128]{3,2,1,0:T(8,128)S(1)} %copy-done, s32[16,8,128]{2,1,0:T(8,128)S(1)} %copy-done.3, f32[2,8]{1,0:T(2,128)S(1)} %copy-done.4), custom_call_target="tpu_custom_call" | custom-call | tf_op jit(solution)/shard_map/first_pack/pallas_call | solution.py:260
  4.8 2.2 %collective-permute-start = (f32[3,4,8,128]{3,2,1,0:T(8,128)S(1)}, f32[3,4,8,128]{3,2,1,0:T(8,128)S(1)}, u32[]{:S(2)}, u32[]{:S(2)}) collective-permute-start(f32[3,4,8,128]{3,2,1,0:T(8,128)S(1)} %get-tuple-element.9), channel_id=1, source_target_pairs={{0,1},{1,0},{2,3},{3,2},{4,5},{5,4},{6,7},{7,6},{8,9},{9,8},{10,11... | collective-permute-start | bytes 147464 | tf_op jit(solution)/shard_map/ppermute | solution.py:254
  7.0 1.5 %collective-permute-done.across = f32[3,4,8,128]{3,2,1,0:T(8,128)S(1)} collective-permute-done((f32[3,4,8,128]{3,2,1,0:T(8,128)S(1)}, f32[3,4,8,128]{3,2,1,0:T(8,128)S(1)}, u32[]{:S(2)}, u32[]{:S(2)}) %collective-permute-start) | collective-permute-done | bytes 49184 | tf_op jit(solution)/shard_map/ppermute | solution.py:254
  8.5 0.0 copy-done.1
  8.5 0.1 second_pack.1
  8.6 3.8 %collective-permute-start.1 = (f32[3,23,8,128]{3,2,1,0:T(8,128)S(1)}, f32[3,23,8,128]{3,2,1,0:T(8,128)S(1)}, u32[]{:S(2)}, u32[]{:S(2)}) collective-permute-start(f32[3,23,8,128]{3,2,1,0:T(8,128)S(1)} %get-tuple-element.11), channel_id=1, source_target_pairs={{0,248},{1,249},{2,250},{3,251},{4,252},{5,253},{6,254},{7,255},{8... | collective-permute-start | bytes 847880 | tf_op jit(solution)/shard_map/ppermute | solution.py:254
  12.4 0.7 %collective-permute-start.2 = (f32[345,128]{1,0:T(8,128)S(1)}, f32[345,128]{1,0:T(8,128)S(1)}, u32[]{:S(2)}, u32[]{:S(2)}) collective-permute-start(f32[345,128]{1,0:T(8,128)S(1)} %get-tuple-element.12), channel_id=1, source_target_pairs={{0,6},{1,7},{2,0},{3,1},{4,2},{5,3},{6,4},{7,5},{8,14},{9,15},{10,... | collective-permute-start | bytes 529928 | tf_op jit(solution)/shard_map/ppermute | solution.py:254
  13.2 0.7 %collective-permute-start.3 = (f32[345,128]{1,0:T(8,128)S(1)}, f32[345,128]{1,0:T(8,128)S(1)}, u32[]{:S(2)}, u32[]{:S(2)}) collective-permute-start(f32[345,128]{1,0:T(8,128)S(1)} %get-tuple-element.13), channel_id=1, source_target_pairs={{0,2},{1,3},{2,4},{3,5},{4,6},{5,7},{6,0},{7,1},{8,10},{9,11},{10,... | collective-permute-start | bytes 529928 | tf_op jit(solution)/shard_map/ppermute | solution.py:254
  13.9 9.1 %collective-permute-start.4 = (f32[345,128]{1,0:T(8,128)S(1)}, f32[345,128]{1,0:T(8,128)S(1)}, u32[]{:S(2)}, u32[]{:S(2)}) collective-permute-start(f32[345,128]{1,0:T(8,128)S(1)} %get-tuple-element.14), channel_id=1, source_target_pairs={{0,254},{1,255},{2,248},{3,249},{4,250},{5,251},{6,252},{7,253},{8... | collective-permute-start | bytes 529928 | tf_op jit(solution)/shard_map/ppermute | solution.py:254
  23.0 0.0 collective-permute-start.5
  23.0 0.0 collective-permute-done.2.own_lo
  23.0 0.0 collective-permute-done.3.own_hi
  23.0 2.4 %collective-permute-done.4.up_lo = f32[345,128]{1,0:T(8,128)S(1)} collective-permute-done((f32[345,128]{1,0:T(8,128)S(1)}, f32[345,128]{1,0:T(8,128)S(1)}, u32[]{:S(2)}, u32[]{:S(2)}) %collective-permute-start.4) | collective-permute-done | bytes 176672 | tf_op jit(solution)/shard_map/ppermute | solution.py:254
  25.5 4.7 %collective-permute-done.5.up_hi = f32[345,128]{1,0:T(8,128)S(1)} collective-permute-done((f32[345,128]{1,0:T(8,128)S(1)}, f32[345,128]{1,0:T(8,128)S(1)}, u32[]{:S(2)}, u32[]{:S(2)}) %collective-permute-start.5) | collective-permute-done | bytes 176672 | tf_op jit(solution)/shard_map/ppermute | solution.py:254
  30.2 0.0 collective-permute-done.1.grow
  30.2 16.2 %evolve.1 = (f32[4,32,8,128]{3,2,1,0:T(8,128)}, f32[2,32,8,128]{3,2,1,0:T(8,128)}) custom-call(s32[2]{0:T(128)S(1)} %pad_add_fusion.where_ref, s32[32,8,128]{2,1,0:T(8,128)S(1)} %copy-done.2, f32[2,32,8,128]{3,2,1,0:T(8,128)S(1)} %copy-done.1, f32[3,4,8,128]{3,2,1,0:T(8,128)S(1)} %collective-permute-done.across, ...), custom_call_target="tpu_custom_call" | custom-call | tf_op jit(solution)/shard_map/evolve/pallas_call | solution.py:284
  (2 shorter events, 0.0 us)
Async XLA Ops:
  0.6 0.7 %copy-start.4 = (f32[2,8]{1,0:T(2,128)S(1)}, f32[2,8]{1,0:T(2,128)}, u32[]{:S(2)}) copy-start(f32[2,8]{1,0:T(2,128)} %table.1) | copy-start | bytes 196
  1.3 0.9 %copy-start = (f32[2,32,8,128]{3,2,1,0:T(8,128)S(1)}, f32[2,32,8,128]{3,2,1,0:T(8,128)}, u32[]{:S(2)}) copy-start(f32[2,32,8,128]{3,2,1,0:T(8,128)} %potential.5) | copy-start | bytes 786436
  2.3 0.9 %copy-start.2 = (s32[32,8,128]{2,1,0:T(8,128)S(1)}, s32[32,8,128]{2,1,0:T(8,128)}, u32[]{:S(2)}) copy-start(s32[32,8,128]{2,1,0:T(8,128)} %labels.5) | copy-start | bytes 393220
  3.2 0.8 %copy-start.3 = (s32[16,8,128]{2,1,0:T(8,128)S(1)}, s32[16,8,128]{2,1,0:T(8,128)}, u32[]{:S(2)}) copy-start(s32[16,8,128]{2,1,0:T(8,128)} %codes.1) | copy-start | bytes 196612
  4.0 4.5 %copy-start.1 = (f32[2,32,8,128]{3,2,1,0:T(8,128)S(1)}, f32[2,32,8,128]{3,2,1,0:T(8,128)}, u32[]{:S(2)}) copy-start(f32[2,32,8,128]{3,2,1,0:T(8,128)} %potential.5) | copy-start | bytes 786436
  4.8 3.7 %collective-permute-start = (f32[3,4,8,128]{3,2,1,0:T(8,128)S(1)}, f32[3,4,8,128]{3,2,1,0:T(8,128)S(1)}, u32[]{:S(2)}, u32[]{:S(2)}) collective-permute-start(f32[3,4,8,128]{3,2,1,0:T(8,128)S(1)} %get-tuple-element.9), channel_id=1, source_target_pairs={{0,1},{1,0},{2,3},{3,2},{4,5},{5,4},{6,7},{7,6},{8,9},{9,8},{10,11... | collective-permute-start | bytes 147464 | tf_op jit(solution)/shard_map/ppermute | solution.py:254
  8.6 21.6 %collective-permute-start.1 = (f32[3,23,8,128]{3,2,1,0:T(8,128)S(1)}, f32[3,23,8,128]{3,2,1,0:T(8,128)S(1)}, u32[]{:S(2)}, u32[]{:S(2)}) collective-permute-start(f32[3,23,8,128]{3,2,1,0:T(8,128)S(1)} %get-tuple-element.11), channel_id=1, source_target_pairs={{0,248},{1,249},{2,250},{3,251},{4,252},{5,253},{6,254},{7,255},{8... | collective-permute-start | bytes 847880 | tf_op jit(solution)/shard_map/ppermute | solution.py:254
  12.4 10.6 %collective-permute-start.2 = (f32[345,128]{1,0:T(8,128)S(1)}, f32[345,128]{1,0:T(8,128)S(1)}, u32[]{:S(2)}, u32[]{:S(2)}) collective-permute-start(f32[345,128]{1,0:T(8,128)S(1)} %get-tuple-element.12), channel_id=1, source_target_pairs={{0,6},{1,7},{2,0},{3,1},{4,2},{5,3},{6,4},{7,5},{8,14},{9,15},{10,... | collective-permute-start | bytes 529928 | tf_op jit(solution)/shard_map/ppermute | solution.py:254
  13.2 9.9 %collective-permute-start.3 = (f32[345,128]{1,0:T(8,128)S(1)}, f32[345,128]{1,0:T(8,128)S(1)}, u32[]{:S(2)}, u32[]{:S(2)}) collective-permute-start(f32[345,128]{1,0:T(8,128)S(1)} %get-tuple-element.13), channel_id=1, source_target_pairs={{0,2},{1,3},{2,4},{3,5},{4,6},{5,7},{6,0},{7,1},{8,10},{9,11},{10,... | collective-permute-start | bytes 529928 | tf_op jit(solution)/shard_map/ppermute | solution.py:254
  13.9 11.6 %collective-permute-start.4 = (f32[345,128]{1,0:T(8,128)S(1)}, f32[345,128]{1,0:T(8,128)S(1)}, u32[]{:S(2)}, u32[]{:S(2)}) collective-permute-start(f32[345,128]{1,0:T(8,128)S(1)} %get-tuple-element.14), channel_id=1, source_target_pairs={{0,254},{1,255},{2,248},{3,249},{4,250},{5,251},{6,252},{7,253},{8... | collective-permute-start | bytes 529928 | tf_op jit(solution)/shard_map/ppermute | solution.py:254
  23.0 7.1 %collective-permute-start.5 = (f32[345,128]{1,0:T(8,128)S(1)}, f32[345,128]{1,0:T(8,128)S(1)}, u32[]{:S(2)}, u32[]{:S(2)}) collective-permute-start(f32[345,128]{1,0:T(8,128)S(1)} %get-tuple-element.15), channel_id=1, source_target_pairs={{0,250},{1,251},{2,252},{3,253},{4,254},{5,255},{6,248},{7,249},{8... | collective-permute-start | bytes 529928 | tf_op jit(solution)/shard_map/ppermute | solution.py:254

commit v2 on v1

v2 whole, which is shorter than its diff:
```python
import jax
import jax.numpy as jnp
from jax import lax
from jax.experimental import pallas as pl
from jax.experimental.pallas import tpu as pltpu
from jax.sharding import PartitionSpec as P

K = 5.0**0.5
ALPHA = 5.0 * K**3
BETA = 2.5 / (K * ALPHA)
TOP = K / 0.12
DRIFT = 0.15 / (0.12 * K)
HALF = 0.5 * K**3

SHIFT = 16
OWN = 21
PLANES = 2 * OWN
PITCH = 32
ROW0 = 12
DEEP = 5
PACK = 11
AXES = ("grow", "gy", "gz")
VMEM = pl.BlockSpec(memory_space=pltpu.VMEM)
HBM = pl.BlockSpec(memory_space=pltpu.MemorySpace.HBM)
SMEM = pl.BlockSpec(memory_space=pltpu.SMEM)


def lanes():
    return lax.broadcasted_iota(jnp.int32, (8, 128), 1)


def reach(i, up):
    return min(DEEP, OWN - 1 - i if up else i)


def plan(up):
    places, at = {}, 0
    for f in range(3):
        for i in range(OWN):
            places["cell", f, i] = (at, reach(i, up))
            at += reach(i, up)
        for q in range(2):
            places["edge", f, q] = (at, DEEP)
            at += DEEP
    if not up:
        for e in range(SHIFT):
            places["code", 0, e] = (at, 2)
            at += 2
        places["code_edge", 0, 0] = (at, 2)
        at += 2
    return places, -(-at // 8) * 8


OWN_PLAN, OWN_ROWS = plan(False)
UP_PLAN, UP_ROWS = plan(True)


def first_pack(labels, potential, codes, cells, codes_out, edges, labels_in, codes_in, sems):
    copies = [
        pltpu.make_async_copy(labels, labels_in, sems.at[0]),
        pltpu.make_async_copy(potential, cells.at[1:3], sems.at[1]),
        pltpu.make_async_copy(codes, codes_in, sems.at[2]),
    ]
    for copy in copies:
        copy.start()
    lane = lanes()

    def packed(tiles, width, offset):
        total = jnp.zeros((8, 128), jnp.float32)
        for c, tile in enumerate(tiles):
            there = (lane >= width * c) & (lane < width * (c + 1))
            total = jnp.where(there, pltpu.roll(tile, (width * c + offset) % 128, 1), total)
        return total

    copies[0].wait()
    for p in range(32):
        cells[0, p] = labels_in[p].astype(jnp.float32)
    copies[2].wait()
    for e in range(SHIFT):
        codes_out[e] = codes_in[e].astype(jnp.float32)
    edges[9] = packed([codes_out[e] for e in range(SHIFT)], 8, 4)
    copies[1].wait()
    for f in range(3):
        for q in range(3):
            planes = range(PACK * q, min(PACK * q + PACK, 32))
            edges[3 * f + q] = packed([cells[f, p] for p in planes], 10, 5)


def second_pack(cells, codes, edges, across, own_lo, own_hi, up_lo, up_hi, grow):
    def put(lo, hi, place, tile):
        at, count = place
        if count:
            lo[at : at + count] = tile[0:count]
            hi[at : at + count] = tile[8 - count : 8]

    for f in range(3):
        for i in range(OWN):
            put(own_lo, own_hi, OWN_PLAN["cell", f, i], cells[f, i + 11])
            put(up_lo, up_hi, UP_PLAN["cell", f, i], cells[f, i])
            grow[f, i] = cells[f, i]
        for q in range(2):
            put(own_lo, own_hi, OWN_PLAN["edge", f, q], across[3 * f + q + 1])
            put(up_lo, up_hi, UP_PLAN["edge", f, q], across[3 * f + q])
            grow[f, OWN + q] = across[3 * f + q]
    for e in range(SHIFT):
        put(own_lo, own_hi, OWN_PLAN["code", 0, e], codes[e])
    put(own_lo, own_hi, OWN_PLAN["code_edge", 0, 0], across[9])
    for ref, rows, used in ((own_lo, OWN_ROWS, 334), (own_hi, OWN_ROWS, 334), (up_lo, UP_ROWS, 300), (up_hi, UP_ROWS, 300)):
        ref[used:rows] = jnp.zeros((rows - used, 128), jnp.float32)


def react(phases, sums, chem, chem_sums, held):
    p0, p1, p2 = phases
    p3 = K - ((p0 + p1) + p2)
    n3 = 6.0 * K - ((sums[0] + sums[1]) + sums[2])
    ps = (p0, p1, p2, p3)
    ns = (sums[0], sums[1], sums[2], n3)
    squares = [p * p for p in ps]
    base = (0.28 / 0.12) - ((squares[0] + squares[1]) + (squares[2] + squares[3]))
    m0, m1 = chem
    both = BETA * (m0 + m1)
    w2 = both + DRIFT
    ws = (w2 + (7.0 * BETA) * m0, w2 + (7.0 * BETA) * m1, w2, 3.5 * both)
    moved = [
        ns[a] + ps[a] * ((base + squares[a]) + ws[a] * (K - ps[a])) for a in range(4)
    ]
    excess = 0.25 * ((moved[0] + moved[1]) + (moved[2] + moved[3])) - 0.25 * TOP
    clipped = [jnp.minimum(jnp.maximum(u - excess, 0.0), TOP) for u in moved]
    scale = K / ((clipped[0] + clipped[1]) + (clipped[2] + clipped[3]))
    new = [s * scale for s in clipped]
    h = [x * x * (1.5 * K - x) for x in new]
    shared = (h[0] + h[1]) + (h[2] + 3.5 * h[3])
    solute = (shared + 7.0 * h[0], shared + 7.0 * h[1])
    mobility = 0.0075 + (0.1425 / K) * p3
    new_held = [held[i] + mobility * (chem_sums[i] - 6.0 * chem[i]) for i in range(2)]
    new_chem = [new_held[i] - solute[i] for i in range(2)]
    return new, new_chem, new_held


def evolve(
    where_ref, cells, codes, table_in, across, own_lo, own_hi, up_lo, up_hi, grow,
    phases_out, chem_out, one, two, table, sem,
):
    first = where_ref[0] == 0
    last = where_ref[0] == where_ref[1] - 1
    lane = lanes()

    def start(dst, z, p, rows, label, m0, m1):
        for a in range(3):
            dst[a, z, p, rows, :] = jnp.where(label == a, K, 0.0)
        melt = jnp.where(label == 3.0, 3.5 * HALF, HALF)
        for i, m in enumerate((m0, m1)):
            m = ALPHA * m
            dst[3 + i, z, p, rows, :] = m
            dst[5 + i, z, p, rows, :] = m + jnp.where(label == i, 8.0 * HALF, melt)

    def fill(dst, p):
        up = p >= OWN
        i = p - OWN if up else p
        q, c = divmod(i, PACK)
        places = UP_PLAN if up else OWN_PLAN
        for z in range(2):

            def turned(x, z=z):
                return pltpu.roll(x, (123 - 10 * c) % 128, 1) if z else x

            def inside(f, z=z):
                if up:
                    return grow[f, OWN + q] if z else grow[f, i]
                return across[3 * f + q + 1] if z else cells[f, i + 11]

            body = [turned(inside(f)) for f in range(3)]
            start(dst, z, p, slice(ROW0, ROW0 + 8), *body)
            for ref, hi in ((up_lo if up else own_lo, False), (up_hi if up else own_hi, True)):
                count = reach(i, up)
                if not count:
                    continue
                body = []
                for f in range(3):
                    at, held = places["edge", f, q] if z else places["cell", f, i]
                    skip = held - count if hi else 0
                    body.append(turned(ref[at + skip : at + skip + count]))
                row = ROW0 - count if hi else ROW0 + 8
                start(dst, z, p, slice(row, row + count), *body)

    def melt(dst, e):
        def chem(code, i):
            value = jnp.zeros_like(code)
            for level in range(8):
                value = jnp.where(code == level, table[i, level], value)
            return value

        for z in range(2):
            at, _ = OWN_PLAN["code_edge", 0, 0] if z else OWN_PLAN["code", 0, e]
            parts = (
                (across[9] if z else codes[e], ROW0, 8),
                (own_hi[at : at + 2], ROW0 - 2, 2),
                (own_lo[at : at + 2], ROW0 + 8, 2),
            )
            for code, row, count in parts:
                code = pltpu.roll(code, (124 - 8 * e) % 128, 1) if z else code
                label = jnp.full_like(code, 3.0)
                start(dst, z, OWN + e, slice(row, row + count), label, chem(code, 0), chem(code, 1))

    def repeat(ref, p, source):
        for f in range(5):
            for z in range(2):
                ref[f, z, p, 7:25, :] = ref[f, z, source, 7:25, :]

    def gather(src, f, z, p, row):
        rows = slice(row, row + 8)
        here = src[f, z, p, rows, :]
        there = src[f, 1 - z, p, rows, :]
        total = src[f, z, p - 1, rows, :] + src[f, z, p + 1, rows, :]
        total = total + (
            src[f, z, p, row - 1 : row + 7, :] + src[f, z, p, row + 1 : row + 9, :]
        )
        left = pltpu.roll(jnp.where(lane == 127, there, here), 1, 1)
        right = pltpu.roll(jnp.where(lane == 0, there, here), 127, 1)
        return here, total + (left + right)

    def tile_step(src, z, p, row):
        pairs = [gather(src, f, z, p, row) for f in range(5)]
        held = [src[f, z, p, row : row + 8, :] for f in (5, 6)]
        here = [a for a, _ in pairs]
        sums = [b for _, b in pairs]
        return react(here[:3], sums[:3], here[3:], sums[3:], held)

    def sweep(src, dst, s):
        count = PLANES - 2 * s

        @pl.loop(s, PLANES - s, unroll=4 if count % 4 == 0 else 2)
        def _(p):
            for z in range(2):
                for row in (8, 16):
                    new, chem, held = tile_step(src, z, p, row)
                    for f, value in enumerate((*new[:3], *chem, *held)):
                        dst[f, z, p, row : row + 8, :] = value

    for p in range(PLANES):
        fill(one, p)
    src, dst = one, two
    for s in range(1, 4):

        @pl.when(last)
        def _(src=src):
            repeat(src, OWN, OWN - 1)

        sweep(src, dst, s)
        src, dst = dst, src

    @pl.when(last)
    def _(src=src):
        copy = pltpu.make_async_copy(table_in, table, sem)
        copy.start()
        copy.wait()
        for e in range(SHIFT):
            melt(src, e)
        repeat(src, OWN + SHIFT, OWN + SHIFT - 1)

    @pl.when(first)
    def _(src=src):
        repeat(src, 4, 5)

    sweep(src, dst, 4)
    src, dst = dst, src

    @pl.when(last)
    def _(src=src):
        repeat(src, OWN + SHIFT, OWN + SHIFT - 1)

    @pl.when(first)
    def _(src=src):
        repeat(src, 4, 5)

    @pl.loop(5, PLANES - 5, unroll=4)
    def _(p):
        new, chem, _ = tile_step(src, 0, p, ROW0)
        for a in range(4):
            phases_out[a, p - 5] = new[a] * (1.0 / K)
        for i in range(2):
            chem_out[i, p - 5] = chem[i] * (1.0 / ALPHA)


def on_device(labels, potential, melt_codes, melt_table):
    n_grow, n_gy, n_gz = (lax.axis_size(a) for a in AXES)
    where = jnp.stack([lax.axis_index("grow"), n_grow]).astype(jnp.int32)

    def send(value, dg, dy, dz):
        pairs = []
        for g in range(max(0, -dg), n_grow):
            for y in range(n_gy):
                for z in range(n_gz):
                    to = ((g + dg) * n_gy + (y + dy) % n_gy) * n_gz + (z + dz) % n_gz
                    pairs.append(((g * n_gy + y) * n_gz + z, to))
        return lax.ppermute(value, AXES, pairs)

    def f32(*shape):
        return jax.ShapeDtypeStruct(shape, jnp.float32)

    params = pltpu.CompilerParams(vmem_limit_bytes=48 << 20)
    cells, codes, edges = pl.pallas_call(
        first_pack,
        in_specs=[HBM] * 3,
        out_specs=[VMEM] * 3,
        out_shape=[f32(3, 32, 8, 128), f32(SHIFT, 8, 128), f32(10, 8, 128)],
        scratch_shapes=[
            pltpu.VMEM((32, 8, 128), jnp.int32),
            pltpu.VMEM((SHIFT, 8, 128), jnp.int32),
            pltpu.SemaphoreType.DMA((3,)),
        ],
        compiler_params=params,
        name="first_pack",
    )(*(pltpu.with_memory_space_constraint(x, pltpu.MemorySpace.HBM) for x in (labels, potential, melt_codes)))
    across = send(edges, 0, 0, 1)
    own_lo, own_hi, up_lo, up_hi, grow = pl.pallas_call(
        second_pack,
        in_specs=[VMEM] * 4,
        out_specs=[VMEM] * 5,
        out_shape=[f32(OWN_ROWS, 128)] * 2 + [f32(UP_ROWS, 128)] * 2 + [f32(3, OWN + 2, 8, 128)],
        compiler_params=params,
        name="second_pack",
    )(cells, codes, edges, across)
    own_lo = send(own_lo, 0, -1, 0)
    own_hi = send(own_hi, 0, 1, 0)
    up_lo = send(up_lo, -1, -1, 0)
    up_hi = send(up_hi, -1, 1, 0)
    grow = send(grow, -1, 0, 0)
    held = pltpu.VMEM((7, 2, PLANES, PITCH, 128), jnp.float32)
    return pl.pallas_call(
        evolve,
        in_specs=[SMEM, VMEM, VMEM, HBM] + [VMEM] * 6,
        out_specs=[VMEM, VMEM],
        out_shape=[f32(4, 32, 8, 128), f32(2, 32, 8, 128)],
        scratch_shapes=[held, held, pltpu.SMEM((2, 8), jnp.float32), pltpu.SemaphoreType.DMA],
        compiler_params=params,
        name="evolve",
    )(where, cells, codes, pltpu.with_memory_space_constraint(melt_table, pltpu.MemorySpace.HBM), across, own_lo, own_hi, up_lo, up_hi, grow)


def solution(mesh):
    return jax.shard_map(
        on_device,
        mesh=mesh,
        in_specs=(P("grow", "gy", "gz"), P(None, "grow", "gy", "gz"), P(None, "gy", "gz"), P()),
        out_specs=(P(None, "grow", "gy", "gz"), P(None, "grow", "gy", "gz")),
        check_vma=False,
    )
```

time: 46.6 us -> 47.4 us (1.017)
  the two profiles are of different devices: /device:TPU:1 before, /device:TPU:24 now
where the time goes in v2:
time: 47.4 us; the launch traced here: 47.2 us
  starting transfers between devices  18.1 us (38%)
  Pallas kernels  17.6 us (37%)
  waiting for transfers between devices  10.7 us (23%)
  between operations  0.68 us (1%)
    ppermute x6, starting transfers between devices, send(): return lax.ppermute(value, AXES, pairs)  18.1 us
    pallas_call x1, Pallas kernels, on_device(): pl.pallas_call(evolve, in_specs=[SMEM, VMEM, VMEM, HBM] + [VMEM] * 6, out...  16.2 us
    ppermute x6, waiting for transfers between devices, send(): return lax.ppermute(value, AXES, pairs)  10.7 us
    pallas_call x1, Pallas kernels, on_device(): pl.pallas_call(first_pack, in_specs=[HBM] * 3, out_specs=[VMEM] * 3, out_...  1.26 us
  transfers between devices with their start and end apart: 6, of which 3 were waited for; matrix products, arithmetic and copies ran while one was open for 0% of the time, Pallas kernels for 0%

profile of v2, /device:TPU:24, one launch (start us, length us, event | category | flops | bytes accessed | tf_op | source)
XLA Modules:
  0.0 47.2 jit_solution(9646826969310411818)
XLA Ops:
  0.6 1.3 %first_pack.1 = (f32[3,32,8,128]{3,2,1,0:T(8,128)S(1)}, f32[16,8,128]{2,1,0:T(8,128)S(1)}, f32[10,8,128]{2,1,0:T(8,128)S(1)}) custom-call(s32[32,8,128]{2,1,0:T(8,128)} %labels.1, f32[2,32,8,128]{3,2,1,0:T(8,128)} %potential.1, s32[16,8,128]{2,1,0:T(8,128)} %codes.1), custom_call_target="tpu_custom_call" | custom-call | tf_op jit(solution)/shard_map/first_pack/pallas_call | solution.py:302
  1.9 0.8 %collective-permute-start = (f32[10,8,128]{2,1,0:T(8,128)S(1)}, f32[10,8,128]{2,1,0:T(8,128)S(1)}, u32[]{:S(2)}, u32[]{:S(2)}) collective-permute-start(f32[10,8,128]{2,1,0:T(8,128)S(1)} %get-tuple-element.12.edges), channel_id=1, source_target_pairs={{0,1},{1,0},{2,3},{3,2},{4,5},{5,4},{6,7},{7,6},{8,9},{9,8},{10,11... | collective-permute-start | bytes 122888 | tf_op jit(solution)/shard_map/ppermute | solution.py:296
  2.7 3.3 %collective-permute-done.across = f32[10,8,128]{2,1,0:T(8,128)S(1)} collective-permute-done((f32[10,8,128]{2,1,0:T(8,128)S(1)}, f32[10,8,128]{2,1,0:T(8,128)S(1)}, u32[]{:S(2)}, u32[]{:S(2)}) %collective-permute-start) | collective-permute-done | bytes 40992 | tf_op jit(solution)/shard_map/ppermute | solution.py:296
  6.0 0.1 second_pack.1
  6.1 6.7 %collective-permute-start.5 = (f32[3,23,8,128]{3,2,1,0:T(8,128)S(1)}, f32[3,23,8,128]{3,2,1,0:T(8,128)S(1)}, u32[]{:S(2)}, u32[]{:S(2)}) collective-permute-start(f32[3,23,8,128]{3,2,1,0:T(8,128)S(1)} %get-tuple-element.17), channel_id=1, source_target_pairs={{8,0},{9,1},{10,2},{11,3},{12,4},{13,5},{14,6},{15,7},{16,8},{17,9... | collective-permute-start | bytes 847880 | tf_op jit(solution)/shard_map/ppermute | solution.py:296
  12.8 2.8 %collective-permute-start.1 = (f32[336,128]{1,0:T(8,128)S(1)}, f32[336,128]{1,0:T(8,128)S(1)}, u32[]{:S(2)}, u32[]{:S(2)}) collective-permute-start(f32[336,128]{1,0:T(8,128)S(1)} %get-tuple-element.13), channel_id=1, source_target_pairs={{0,6},{1,7},{2,0},{3,1},{4,2},{5,3},{6,4},{7,5},{8,14},{9,15},{10,... | collective-permute-start | bytes 516104 | tf_op jit(solution)/shard_map/ppermute | solution.py:296
  15.7 0.0 collective-permute-start.2
  15.7 5.8 %collective-permute-start.3 = (f32[304,128]{1,0:T(8,128)S(1)}, f32[304,128]{1,0:T(8,128)S(1)}, u32[]{:S(2)}, u32[]{:S(2)}) collective-permute-start(f32[304,128]{1,0:T(8,128)S(1)} %get-tuple-element.15), channel_id=1, source_target_pairs={{8,6},{9,7},{10,0},{11,1},{12,2},{13,3},{14,4},{15,5},{16,14},{17,... | collective-permute-start | bytes 466952 | tf_op jit(solution)/shard_map/ppermute | solution.py:296
  21.5 1.9 %collective-permute-start.4 = (f32[304,128]{1,0:T(8,128)S(1)}, f32[304,128]{1,0:T(8,128)S(1)}, u32[]{:S(2)}, u32[]{:S(2)}) collective-permute-start(f32[304,128]{1,0:T(8,128)S(1)} %get-tuple-element.16), channel_id=1, source_target_pairs={{8,2},{9,3},{10,4},{11,5},{12,6},{13,7},{14,0},{15,1},{16,10},{17,... | collective-permute-start | bytes 466952 | tf_op jit(solution)/shard_map/ppermute | solution.py:296
  23.4 0.1 pad_add_fusion.where_ref
  23.5 0.7 %collective-permute-done.3.up_lo = f32[304,128]{1,0:T(8,128)S(1)} collective-permute-done((f32[304,128]{1,0:T(8,128)S(1)}, f32[304,128]{1,0:T(8,128)S(1)}, u32[]{:S(2)}, u32[]{:S(2)}) %collective-permute-start.3) | collective-permute-done | bytes 155680 | tf_op jit(solution)/shard_map/ppermute | solution.py:296
  24.2 6.7 %collective-permute-done.4.up_hi = f32[304,128]{1,0:T(8,128)S(1)} collective-permute-done((f32[304,128]{1,0:T(8,128)S(1)}, f32[304,128]{1,0:T(8,128)S(1)}, u32[]{:S(2)}, u32[]{:S(2)}) %collective-permute-start.4) | collective-permute-done | bytes 155680 | tf_op jit(solution)/shard_map/ppermute | solution.py:296
  30.9 0.0 collective-permute-done.1.own_lo
  30.9 0.0 collective-permute-done.2.own_hi
  30.9 0.0 collective-permute-done.5.grow
  30.9 16.2 %evolve.1 = (f32[4,32,8,128]{3,2,1,0:T(8,128)}, f32[2,32,8,128]{3,2,1,0:T(8,128)}) custom-call(s32[2]{0:T(128)S(1)} %pad_add_fusion.where_ref, f32[3,32,8,128]{3,2,1,0:T(8,128)S(1)} %get-tuple-element.10.cells, f32[16,8,128]{2,1,0:T(8,128)S(1)} %get-tuple-element.11.codes, f32[2,8]{1,0:T(2,128)} %table_in.1, f32[10,8,128]{2,1,0:T(8,128)S(1)} %collective-permute-done.across, ...), custom_call_target="tpu_custom_call" | custom-call | tf_op jit(solution)/shard_map/evolve/pallas_call | solution.py:330
Async XLA Ops:
  1.9 4.1 %collective-permute-start = (f32[10,8,128]{2,1,0:T(8,128)S(1)}, f32[10,8,128]{2,1,0:T(8,128)S(1)}, u32[]{:S(2)}, u32[]{:S(2)}) collective-permute-start(f32[10,8,128]{2,1,0:T(8,128)S(1)} %get-tuple-element.12.edges), channel_id=1, source_target_pairs={{0,1},{1,0},{2,3},{3,2},{4,5},{5,4},{6,7},{7,6},{8,9},{9,8},{10,11... | collective-permute-start | bytes 122888 | tf_op jit(solution)/shard_map/ppermute | solution.py:296
  6.1 24.8 %collective-permute-start.5 = (f32[3,23,8,128]{3,2,1,0:T(8,128)S(1)}, f32[3,23,8,128]{3,2,1,0:T(8,128)S(1)}, u32[]{:S(2)}, u32[]{:S(2)}) collective-permute-start(f32[3,23,8,128]{3,2,1,0:T(8,128)S(1)} %get-tuple-element.17), channel_id=1, source_target_pairs={{8,0},{9,1},{10,2},{11,3},{12,4},{13,5},{14,6},{15,7},{16,8},{17,9... | collective-permute-start | bytes 847880 | tf_op jit(solution)/shard_map/ppermute | solution.py:296
  12.8 18.1 %collective-permute-start.1 = (f32[336,128]{1,0:T(8,128)S(1)}, f32[336,128]{1,0:T(8,128)S(1)}, u32[]{:S(2)}, u32[]{:S(2)}) collective-permute-start(f32[336,128]{1,0:T(8,128)S(1)} %get-tuple-element.13), channel_id=1, source_target_pairs={{0,6},{1,7},{2,0},{3,1},{4,2},{5,3},{6,4},{7,5},{8,14},{9,15},{10,... | collective-permute-start | bytes 516104 | tf_op jit(solution)/shard_map/ppermute | solution.py:296
  15.7 15.3 %collective-permute-start.2 = (f32[336,128]{1,0:T(8,128)S(1)}, f32[336,128]{1,0:T(8,128)S(1)}, u32[]{:S(2)}, u32[]{:S(2)}) collective-permute-start(f32[336,128]{1,0:T(8,128)S(1)} %get-tuple-element.14), channel_id=1, source_target_pairs={{0,2},{1,3},{2,4},{3,5},{4,6},{5,7},{6,0},{7,1},{8,10},{9,11},{10,... | collective-permute-start | bytes 516104 | tf_op jit(solution)/shard_map/ppermute | solution.py:296
  15.7 8.6 %collective-permute-start.3 = (f32[304,128]{1,0:T(8,128)S(1)}, f32[304,128]{1,0:T(8,128)S(1)}, u32[]{:S(2)}, u32[]{:S(2)}) collective-permute-start(f32[304,128]{1,0:T(8,128)S(1)} %get-tuple-element.15), channel_id=1, source_target_pairs={{8,6},{9,7},{10,0},{11,1},{12,2},{13,3},{14,4},{15,5},{16,14},{17,... | collective-permute-start | bytes 466952 | tf_op jit(solution)/shard_map/ppermute | solution.py:296
  21.5 9.4 %collective-permute-start.4 = (f32[304,128]{1,0:T(8,128)S(1)}, f32[304,128]{1,0:T(8,128)S(1)}, u32[]{:S(2)}, u32[]{:S(2)}) collective-permute-start(f32[304,128]{1,0:T(8,128)S(1)} %get-tuple-element.16), channel_id=1, source_target_pairs={{8,2},{9,3},{10,4},{11,5},{12,6},{13,7},{14,0},{15,1},{16,10},{17,... | collective-permute-start | bytes 466952 | tf_op jit(solution)/shard_map/ppermute | solution.py:296

commit v3 on v2

v3 whole, which is shorter than its diff:
```python
import jax
import jax.numpy as jnp
from jax import lax
from jax.experimental import pallas as pl
from jax.experimental.pallas import tpu as pltpu
from jax.sharding import PartitionSpec as P

K = 5.0**0.5
ALPHA = 5.0 * K**3
BETA = 2.5 / (K * ALPHA)
TOP = K / 0.12
DRIFT = 0.15 / (0.12 * K)
HALF = 0.5 * K**3

SHIFT = 16
OWN = 21
PLANES = 2 * OWN
PITCH = 32
ROW0 = 12
DEEP = 5
PACK = 11
AXES = ("grow", "gy", "gz")
VMEM = pl.BlockSpec(memory_space=pltpu.VMEM)
HBM = pl.BlockSpec(memory_space=pltpu.MemorySpace.HBM)
SMEM = pl.BlockSpec(memory_space=pltpu.SMEM)


def lanes():
    return lax.broadcasted_iota(jnp.int32, (8, 128), 1)


def reach(i, up):
    return min(DEEP, OWN - 1 - i if up else i)


def plan(up):
    places, at = {}, 8
    for f in range(3):
        for i in range(OWN):
            places["cell", f, i] = (at, reach(i, up))
            at += reach(i, up)
        for q in range(2):
            places["edge", f, q] = (at, DEEP)
            at += DEEP
    if not up:
        for e in range(SHIFT):
            places["code", 0, e] = (at, 2)
            at += 2
        places["code_edge", 0, 0] = (at, 2)
        at += 2
    return places, -(-at // 8) * 8


OWN_PLAN, OWN_ROWS = plan(False)
UP_PLAN, UP_ROWS = plan(True)


def first_pack(labels, potential, codes, cells, codes_out, edges, labels_in, codes_in, sems):
    copies = [
        pltpu.make_async_copy(labels, labels_in, sems.at[0]),
        pltpu.make_async_copy(potential, cells.at[1:3], sems.at[1]),
        pltpu.make_async_copy(codes, codes_in, sems.at[2]),
    ]
    for copy in copies:
        copy.start()
    lane = lanes()

    def packed(tiles, width, offset):
        total = jnp.zeros((8, 128), jnp.float32)
        for c, tile in enumerate(tiles):
            there = (lane >= width * c) & (lane < width * (c + 1))
            total = jnp.where(there, pltpu.roll(tile, (width * c + offset) % 128, 1), total)
        return total

    copies[0].wait()
    for p in range(32):
        cells[0, p] = labels_in[p].astype(jnp.float32)
    copies[2].wait()
    for e in range(SHIFT):
        codes_out[e] = codes_in[e].astype(jnp.float32)
    edges[9] = packed([codes_out[e] for e in range(SHIFT)], 8, 4)
    copies[1].wait()
    for f in range(3):
        for q in range(3):
            planes = range(PACK * q, min(PACK * q + PACK, 32))
            edges[3 * f + q] = packed([cells[f, p] for p in planes], 10, 5)


def put(lo, hi, place, tile):
    at, count = place
    if count:
        lo[at : at + count] = tile[0:count]
        hi[at : at + count] = tile[8 - count : 8]


def second_pack(cells, codes, across, own_lo, own_hi, grow):
    for f in range(3):
        for i in range(OWN):
            put(own_lo, own_hi, OWN_PLAN["cell", f, i], cells[f, i + 11])
            grow[f, i] = cells[f, i]
        for q in range(2):
            put(own_lo, own_hi, OWN_PLAN["edge", f, q], across[3 * f + q + 1])
            grow[f, OWN + q] = across[3 * f + q]
    for e in range(SHIFT):
        put(own_lo, own_hi, OWN_PLAN["code", 0, e], codes[e])
    put(own_lo, own_hi, OWN_PLAN["code_edge", 0, 0], across[9])
    for ref in (own_lo, own_hi):
        blank(ref, OWN_PLAN, OWN_ROWS)


def blank(ref, places, rows):
    used = max(at + count for at, count in places.values())
    ref[0:8] = jnp.zeros((8, 128), jnp.float32)
    ref[used:rows] = jnp.zeros((rows - used, 128), jnp.float32)


def third_pack(grow, up_lo, up_hi):
    for f in range(3):
        for i in range(OWN):
            put(up_lo, up_hi, UP_PLAN["cell", f, i], grow[f, i])
        for q in range(2):
            put(up_lo, up_hi, UP_PLAN["edge", f, q], grow[f, OWN + q])
    for ref in (up_lo, up_hi):
        blank(ref, UP_PLAN, UP_ROWS)


def react(phases, sums, chem, chem_sums, held):
    p0, p1, p2 = phases
    p3 = K - ((p0 + p1) + p2)
    n3 = 6.0 * K - ((sums[0] + sums[1]) + sums[2])
    ps = (p0, p1, p2, p3)
    ns = (sums[0], sums[1], sums[2], n3)
    squares = [p * p for p in ps]
    base = (0.28 / 0.12) - ((squares[0] + squares[1]) + (squares[2] + squares[3]))
    m0, m1 = chem
    both = BETA * (m0 + m1)
    w2 = both + DRIFT
    ws = (w2 + (7.0 * BETA) * m0, w2 + (7.0 * BETA) * m1, w2, 3.5 * both)
    moved = [
        ns[a] + ps[a] * ((base + squares[a]) + ws[a] * (K - ps[a])) for a in range(4)
    ]
    excess = 0.25 * ((moved[0] + moved[1]) + (moved[2] + moved[3])) - 0.25 * TOP
    clipped = [jnp.minimum(jnp.maximum(u - excess, 0.0), TOP) for u in moved]
    scale = K / ((clipped[0] + clipped[1]) + (clipped[2] + clipped[3]))
    new = [s * scale for s in clipped]
    h = [x * x * (1.5 * K - x) for x in new]
    shared = (h[0] + h[1]) + (h[2] + 3.5 * h[3])
    solute = (shared + 7.0 * h[0], shared + 7.0 * h[1])
    mobility = 0.0075 + (0.1425 / K) * p3
    new_held = [held[i] + mobility * (chem_sums[i] - 6.0 * chem[i]) for i in range(2)]
    new_chem = [new_held[i] - solute[i] for i in range(2)]
    return new, new_chem, new_held


class Half:
    def __init__(self, base, strip_base, n, cells, codes, across, own, up, grow, lane):
        self.base, self.strip_base, self.n = base, strip_base, n
        self.cells, self.codes, self.across = cells, codes, across
        self.own, self.up, self.grow, self.lane = own, up, grow, lane

    def source(self, p):
        up = p >= OWN
        i = p - OWN if up else p
        q, c = divmod(i, PACK)
        return up, i, q, c

    def store(self, dst, index, rows, label, m0, m1, mask=None):
        values = [jnp.where(label == a, K, 0.0) for a in range(3)]
        rest = jnp.where(label == 3.0, 3.5 * HALF, HALF)
        values += [ALPHA * m0, ALPHA * m1]
        values += [values[3 + i] + jnp.where(label == i, 8.0 * HALF, rest) for i in range(2)]
        for f, value in enumerate(values):
            if mask is not None:
                value = jnp.where(mask, value, dst[f, index, rows, :])
            dst[f, index, rows, :] = value

    def fill(self, dst, p):
        up, i, _, _ = self.source(p)
        body = [self.grow[f, i] if up else self.cells[f, i + 11] for f in range(3)]
        self.store(dst, p - self.base, slice(ROW0, ROW0 + 8), *body)
        for hi, ref in enumerate(self.up if up else self.own):
            count = reach(i, up)
            if count:
                places = UP_PLAN if up else OWN_PLAN
                body = []
                for f in range(3):
                    at, _ = places["cell", f, i]
                    body.append(ref[at : at + count])
                row = ROW0 - count if hi else ROW0 + 8
                self.store(dst, p - self.base, slice(row, row + count), *body)

    def pieces(self, p, f, block):
        up, i, q, _ = self.source(p)
        if block == 0:
            if up:
                return self.grow[f, i], self.grow[f, OWN + q]
            return self.cells[f, i + 11], self.across[3 * f + q + 1]
        places = UP_PLAN if up else OWN_PLAN
        ref = (self.up if up else self.own)[block - 1]
        at, count = places["cell", f, i]
        at = at if block == 1 else at + count - DEEP
        edge, _ = places["edge", f, q]
        return ref[at : at + DEEP], ref[edge : edge + DEEP]

    def joined(self, parts):
        rows = next(part for part in parts if part is not None)[0].shape[0]
        lane = lax.broadcasted_iota(jnp.int32, (rows, 128), 1)
        total = jnp.zeros((rows, 128), jnp.float32)
        for j, part in enumerate(parts):
            if part is None:
                continue
            value, edge, before, after = part
            at = 20 * j
            tile = jnp.where(
                lane < at + 10,
                jnp.where(lane < at + 5, pltpu.roll(edge, before % 128, 1), pltpu.roll(value, at + 5, 1)),
                jnp.where(lane < at + 15, pltpu.roll(value, (at + 15) % 128, 1), pltpu.roll(edge, after % 128, 1)),
            )
            total = jnp.where(lane >= at, tile, total)
        return total

    def fill_strips(self, dst, top):
        for index in range(self.n):
            for block, row, _ in BLOCKS:
                body = []
                for f in range(3):
                    parts = []
                    for j in range(6):
                        p = self.strip_base + self.n * j + index
                        if p >= top:
                            parts.append(None)
                            continue
                        c = self.source(p)[3]
                        parts.append(
                            (*self.pieces(p, f, block), 20 * j - 10 * c, 20 * j + 10 - 10 * c)
                        )
                    body.append(self.joined(parts))
                self.store(dst, index, slice(row, row + body[0].shape[0]), *body)

    def melt(self, dst, strips, table):
        def chem(code, i):
            value = jnp.zeros_like(code)
            for level in range(8):
                value = jnp.where(code == level, table[i, level], value)
            return value

        def rows(block, e):
            if block == 0:
                return self.codes[e], self.across[9]
            ref = self.own[block - 1]
            at, _ = OWN_PLAN["code", 0, e]
            edge, _ = OWN_PLAN["code_edge", 0, 0]
            return ref[at : at + 2], ref[edge : edge + 2]

        for e in range(SHIFT):
            for block, row, count in MELT_BLOCKS:
                code = rows(block, e)[0]
                label = jnp.full_like(code, 3.0)
                where = slice(row, row + count)
                self.store(dst, OWN + e - self.base, where, label, chem(code, 0), chem(code, 1))
        for index in range(self.n):
            for block, row, count in MELT_BLOCKS:
                parts, groups = [], []
                for j in range(6):
                    e = self.strip_base + self.n * j + index - OWN
                    if not 0 <= e < SHIFT:
                        parts.append(None)
                        continue
                    groups.append(j)
                    parts.append((*rows(block, e), 20 * j + 1 - 8 * e, 20 * j + 11 - 8 * e))
                code = self.joined(parts)
                lane = lax.broadcasted_iota(jnp.int32, code.shape, 1)
                mask = (lane >= 20 * groups[0]) & (lane < 20 * groups[-1] + 20)
                label = jnp.full_like(code, 3.0)
                where = slice(row, row + count)
                self.store(strips, index, where, label, chem(code, 0), chem(code, 1), mask)

    def repeat(self, dst, p, source):
        for f in range(5):
            dst[f, p - self.base, 7:25, :] = dst[f, source - self.base, 7:25, :]

    def repeat_strip(self, strips, p, source):
        j, index = divmod(p - self.strip_base, self.n)
        j_from, index_from = divmod(source - self.strip_base, self.n)
        lane = lax.broadcasted_iota(jnp.int32, (18, 128), 1)
        mask = (lane >= 20 * j) & (lane < 20 * j + 20)
        for f in range(5):
            value = strips[f, index_from, 7:25, :]
            if j != j_from:
                value = pltpu.roll(value, 20 * (j - j_from), 1)
            strips[f, index, 7:25, :] = jnp.where(mask, value, strips[f, index, 7:25, :])

    def advance(self, src, index, row, fetch, sides):
        here, sums = [], []
        for f in range(5):
            mid = src[f, index, row : row + 8, :]
            below, above = fetch(f)
            total = (below + above) + (
                src[f, index, row - 1 : row + 7, :] + src[f, index, row + 1 : row + 9, :]
            )
            left, right = sides(f, pltpu.roll(mid, 1, 1), pltpu.roll(mid, 127, 1))
            here.append(mid)
            sums.append(total + (left + right))
        held = [src[f, index, row : row + 8, :] for f in (5, 6)]
        return react(here[:3], sums[:3], here[3:], sums[3:], held)

    def plane_step(self, src, strips, p, row):
        index = p - self.base
        q = p - self.strip_base
        j = (q * 13) >> 6 if self.n == 5 else q >> 2
        at = q - self.n * j
        to_first, to_last = 124 - 20 * j, 112 - 20 * j
        rows = slice(row, row + 8)

        def fetch(f):
            return src[f, index - 1, rows, :], src[f, index + 1, rows, :]

        def sides(f, left, right):
            strip = strips[f, at, rows, :]
            left = jnp.where(self.lane == 0, pltpu.roll(strip, to_first, 1), left)
            return left, jnp.where(self.lane == 127, pltpu.roll(strip, to_last, 1), right)

        return self.advance(src, index, row, fetch, sides)

    def planes(self, first, count, body):
        whole = count - count % 4
        if whole:
            pl.loop(first, first + whole, unroll=4)(body)
        for p in range(first + whole, first + count):
            body(p)

    def sweep(self, src, dst, src_strips, dst_strips, first, count):
        def body(p):
            for row in (8, 16):
                new, chem, held = self.plane_step(src, src_strips, p, row)
                for f, value in enumerate((*new[:3], *chem, *held)):
                    dst[f, p - self.base, row : row + 8, :] = value

        self.planes(first, count, body)
        last = self.n - 1
        for index in range(self.n):
            for row in (8, 16):
                rows = slice(row, row + 8)

                def fetch(f, index=index, rows=rows):
                    if index:
                        below = src_strips[f, index - 1, rows, :]
                    else:
                        below = pltpu.roll(src_strips[f, last, rows, :], 20, 1)
                    if index < last:
                        above = src_strips[f, index + 1, rows, :]
                    else:
                        above = pltpu.roll(src_strips[f, 0, rows, :], 108, 1)
                    return below, above

                new, chem, held = self.advance(
                    src_strips, index, row, fetch, lambda f, left, right: (left, right)
                )
                for f, value in enumerate((*new[:3], *chem, *held)):
                    dst_strips[f, index, row : row + 8, :] = value

    def finish(self, src, strips, first, count, phases, chems):
        def body(p):
            new, chem, _ = self.plane_step(src, strips, p, ROW0)
            for a in range(4):
                phases[a, p - first] = new[a] * (1.0 / K)
            for i in range(2):
                chems[i, p - first] = chem[i] * (1.0 / ALPHA)

        self.planes(first, count, body)


BLOCKS = ((0, ROW0, 8), (1, ROW0 + 8, DEEP), (2, ROW0 - DEEP, DEEP))
MELT_BLOCKS = ((0, ROW0, 8), (1, ROW0 + 8, 2), (2, ROW0 - 2, 2))
LOWER = 11


def lower_half(
    where_ref, cells, codes, across, own_lo, own_hi, phases_out, chem_out, seam,
    one, two, strip_one, strip_two, phases, chems, sems,
):
    first = where_ref[0] == 0
    half = Half(0, 0, 4, cells, codes, across, (own_lo, own_hi), None, None, lanes())
    for p in range(OWN):
        half.fill(one, p)
    half.fill_strips(strip_one, OWN)
    src, dst, src_strips, dst_strips = one, two, strip_one, strip_two
    for s in range(1, 5):
        if s == 4:

            @pl.when(first)
            def _(src=src, src_strips=src_strips):
                half.repeat(src, 4, 5)
                half.repeat_strip(src_strips, 4, 5)

        half.sweep(src, dst, src_strips, dst_strips, s, OWN - 2 * s)
        for f in range(7):
            for i in range(2):
                seam[s - 1, f, i] = dst[f, OWN - 1 - s + i - 1, 8:24, :]
        src, dst, src_strips, dst_strips = dst, src, dst_strips, src_strips

    @pl.when(first)
    def _(src=src):
        half.repeat(src, 4, 5)

    half.finish(src, src_strips, 5, LOWER, phases, chems)
    deliver(phases, chems, phases_out, chem_out, 0, LOWER, sems)


def deliver(phases, chems, phases_out, chem_out, first, count, sems):
    copies = [
        pltpu.make_async_copy(phases, phases_out.at[:, pl.ds(first, count)], sems.at[0]),
        pltpu.make_async_copy(chems, chem_out.at[:, pl.ds(first, count)], sems.at[1]),
    ]
    for copy in copies:
        copy.start()
    for copy in copies:
        copy.wait()


def upper_half(
    where_ref, cells, codes, table_in, across, own_lo, own_hi, up_lo, up_hi, grow, seam,
    phases_in, chem_in, phases_out, chem_out,
    one, two, strip_one, strip_two, phases, chems, table, sem, sems,
):
    del phases_in, chem_in
    last = where_ref[0] == where_ref[1] - 1
    half = Half(
        15, 12, 5, cells, codes, across, (own_lo, own_hi), (up_lo, up_hi), grow, lanes()
    )
    for p in range(OWN - 2, PLANES):
        half.fill(one, p)
    half.fill_strips(strip_one, PLANES)
    src, dst, src_strips, dst_strips = one, two, strip_one, strip_two
    for s in range(1, 6):
        if s > 1:
            for f in range(7):
                for i in range(2):
                    src[f, OWN - 1 - s + i - half.base, 8:24, :] = seam[s - 2, f, i]
        if s < 4:

            @pl.when(last)
            def _(src=src, src_strips=src_strips):
                half.repeat(src, OWN, OWN - 1)
                half.repeat_strip(src_strips, OWN, OWN - 1)

        if s == 4:

            @pl.when(last)
            def _(src=src, src_strips=src_strips):
                copy = pltpu.make_async_copy(table_in, table, sem)
                copy.start()
                copy.wait()
                half.melt(src, src_strips, table)
                half.repeat_strip(src_strips, OWN + SHIFT, OWN + SHIFT - 1)

        if s >= 4:

            @pl.when(last)
            def _(src=src):
                half.repeat(src, OWN + SHIFT, OWN + SHIFT - 1)

        if s < 5:
            half.sweep(src, dst, src_strips, dst_strips, OWN - s, OWN)
            src, dst, src_strips, dst_strips = dst, src, dst_strips, src_strips
    half.finish(src, src_strips, OWN - 5, OWN, phases, chems)
    deliver(phases, chems, phases_out, chem_out, LOWER, OWN, sems)


def on_device(labels, potential, melt_codes, melt_table):
    n_grow, n_gy, n_gz = (lax.axis_size(a) for a in AXES)
    where = jnp.stack([lax.axis_index("grow"), n_grow]).astype(jnp.int32)

    def send(value, dg, dy, dz):
        pairs = []
        for g in range(max(0, -dg), n_grow):
            for y in range(n_gy):
                for z in range(n_gz):
                    to = ((g + dg) * n_gy + (y + dy) % n_gy) * n_gz + (z + dz) % n_gz
                    pairs.append(((g * n_gy + y) * n_gz + z, to))
        return lax.ppermute(value, AXES, pairs)

    def f32(*shape):
        return jax.ShapeDtypeStruct(shape, jnp.float32)

    params = pltpu.CompilerParams(vmem_limit_bytes=48 << 20)
    cells, codes, edges = pl.pallas_call(
        first_pack,
        in_specs=[HBM] * 3,
        out_specs=[VMEM] * 3,
        out_shape=[f32(3, 32, 8, 128), f32(SHIFT, 8, 128), f32(10, 8, 128)],
        scratch_shapes=[
            pltpu.VMEM((32, 8, 128), jnp.int32),
            pltpu.VMEM((SHIFT, 8, 128), jnp.int32),
            pltpu.SemaphoreType.DMA((3,)),
        ],
        compiler_params=params,
        name="first_pack",
    )(*(pltpu.with_memory_space_constraint(x, pltpu.MemorySpace.HBM) for x in (labels, potential, melt_codes)))
    across = send(edges, 0, 0, 1)
    own_lo, own_hi, grow = pl.pallas_call(
        second_pack,
        in_specs=[VMEM] * 3,
        out_specs=[VMEM] * 3,
        out_shape=[f32(OWN_ROWS, 128)] * 2 + [f32(3, OWN + 2, 8, 128)],
        compiler_params=params,
        name="second_pack",
    )(cells, codes, across)
    own_lo = send(own_lo, 0, -1, 0)
    own_hi = send(own_hi, 0, 1, 0)
    grow = send(grow, -1, 0, 0)
    up_lo, up_hi = pl.pallas_call(
        third_pack,
        in_specs=[VMEM],
        out_specs=[VMEM] * 2,
        out_shape=[f32(UP_ROWS, 128)] * 2,
        compiler_params=params,
        name="third_pack",
    )(grow)
    up_lo = send(up_lo, 0, -1, 0)
    up_hi = send(up_hi, 0, 1, 0)

    def buffers(planes, strips, count):
        return (
            [pltpu.VMEM((7, planes, PITCH, 128), jnp.float32)] * 2
            + [pltpu.VMEM((7, strips, PITCH, 128), jnp.float32)] * 2
            + [pltpu.VMEM((4, count, 8, 128), jnp.float32)]
            + [pltpu.VMEM((2, count, 8, 128), jnp.float32)]
        )

    outputs = [f32(4, 32, 8, 128), f32(2, 32, 8, 128)]
    phases, chems, seam = pl.pallas_call(
        lower_half,
        in_specs=[SMEM] + [VMEM] * 5,
        out_specs=[HBM, HBM, VMEM],
        out_shape=outputs + [f32(4, 7, 2, 16, 128)],
        scratch_shapes=buffers(OWN, 4, LOWER) + [pltpu.SemaphoreType.DMA((2,))],
        compiler_params=params,
        cost_estimate=pl.CostEstimate(
            flops=60_000_000, bytes_accessed=12_000_000, transcendentals=0
        ),
        name="lower_half",
    )(where, cells, codes, across, own_lo, own_hi)
    table = pltpu.with_memory_space_constraint(melt_table, pltpu.MemorySpace.HBM)
    return pl.pallas_call(
        upper_half,
        in_specs=[SMEM, VMEM, VMEM, HBM] + [VMEM] * 7 + [HBM, HBM],
        out_specs=[HBM, HBM],
        out_shape=outputs,
        scratch_shapes=buffers(27, 5, OWN)
        + [pltpu.SMEM((2, 8), jnp.float32), pltpu.SemaphoreType.DMA, pltpu.SemaphoreType.DMA((2,))],
        input_output_aliases={11: 0, 12: 1},
        compiler_params=params,
        name="upper_half",
    )(where, cells, codes, table, across, own_lo, own_hi, up_lo, up_hi, grow, seam, phases, chems)


def solution(mesh):
    return jax.shard_map(
        on_device,
        mesh=mesh,
        in_specs=(P("grow", "gy", "gz"), P(None, "grow", "gy", "gz"), P(None, "gy", "gz"), P()),
        out_specs=(P(None, "grow", "gy", "gz"), P(None, "grow", "gy", "gz")),
        check_vma=False,
    )
```

time: 47.4 us -> 40.8 us (0.86)
  starting transfers between devices: 18.1 us -> 13.2 us
  waiting for transfers between devices: 10.7 us -> 8.58 us
  Pallas kernels: 17.6 us -> 18.1 us
    ppermute x6, starting transfers between devices: 18.1 us -> 13.2 us  [send(): return lax.ppermute(value, AXES, pairs)]
    ppermute x6, waiting for transfers between devices: 10.7 us -> 8.58 us  [send(): return lax.ppermute(value, AXES, pairs)]
    pallas_call x2 -> x4, Pallas kernels: 16.3 us -> 16.8 us  [the longest x1 9.51 us: on_device(): pl.pallas_call(upper_half, in_specs=[SMEM, VMEM, VMEM, HBM] + [VMEM] * 7...]
  transfers between devices with their start and end apart: 6 -> 6, of which waited for: 3 -> 4; matrix products, arithmetic and copies ran while one was open for 0% -> 0% of each run, Pallas kernels for 0% -> 18%
where the time goes in v3:
time: 40.8 us; the launch traced here: 40.6 us
  Pallas kernels  18.1 us (44%)
  starting transfers between devices  13.2 us (32%)
  waiting for transfers between devices  8.58 us (21%)
  between operations  0.68 us (2%)
    ppermute x6, starting transfers between devices, send(): return lax.ppermute(value, AXES, pairs)  13.2 us
    pallas_call x1, Pallas kernels, on_device(): pl.pallas_call(upper_half, in_specs=[SMEM, VMEM, VMEM, HBM] + [VMEM] * 7...  9.51 us
    ppermute x6, waiting for transfers between devices, send(): return lax.ppermute(value, AXES, pairs)  8.58 us
    pallas_call x1, Pallas kernels, on_device(): pl.pallas_call(lower_half, in_specs=[SMEM] + [VMEM] * 5, out_specs=[HBM,...  7.18 us
    pallas_call x1, Pallas kernels, on_device(): pl.pallas_call(first_pack, in_specs=[HBM] * 3, out_specs=[VMEM] * 3, out_...  1.26 us
  transfers between devices with their start and end apart: 6, of which 4 were waited for; matrix products, arithmetic and copies ran while one was open for 0% of the time, Pallas kernels for 18%

profile of v3, /device:TPU:24, one launch (start us, length us, event | category | flops | bytes accessed | tf_op | source)
XLA Modules:
  0.0 40.6 jit_solution(3567015129288613635)
XLA Ops:
  0.6 1.3 %first_pack.1 = (f32[3,32,8,128]{3,2,1,0:T(8,128)S(1)}, f32[16,8,128]{2,1,0:T(8,128)S(1)}, f32[10,8,128]{2,1,0:T(8,128)S(1)}) custom-call(s32[32,8,128]{2,1,0:T(8,128)} %labels.1, f32[2,32,8,128]{3,2,1,0:T(8,128)} %potential.1, s32[16,8,128]{2,1,0:T(8,128)} %codes.1), custom_call_target="tpu_custom_call" | custom-call | tf_op jit(solution)/shard_map/first_pack/pallas_call | solution.py:487
  1.9 0.8 %collective-permute-start = (f32[10,8,128]{2,1,0:T(8,128)S(1)}, f32[10,8,128]{2,1,0:T(8,128)S(1)}, u32[]{:S(2)}, u32[]{:S(2)}) collective-permute-start(f32[10,8,128]{2,1,0:T(8,128)S(1)} %get-tuple-element.15), channel_id=1, source_target_pairs={{0,1},{1,0},{2,3},{3,2},{4,5},{5,4},{6,7},{7,6},{8,9},{9,8},{10,11... | collective-permute-start | bytes 122888 | tf_op jit(solution)/shard_map/ppermute | solution.py:481
  2.7 3.3 %collective-permute-done.across = f32[10,8,128]{2,1,0:T(8,128)S(1)} collective-permute-done((f32[10,8,128]{2,1,0:T(8,128)S(1)}, f32[10,8,128]{2,1,0:T(8,128)S(1)}, u32[]{:S(2)}, u32[]{:S(2)}) %collective-permute-start) | collective-permute-done | bytes 40992 | tf_op jit(solution)/shard_map/ppermute | solution.py:481
  6.0 0.1 second_pack.1
  6.1 6.7 %collective-permute-start.3 = (f32[3,23,8,128]{3,2,1,0:T(8,128)S(1)}, f32[3,23,8,128]{3,2,1,0:T(8,128)S(1)}, u32[]{:S(2)}, u32[]{:S(2)}) collective-permute-start(f32[3,23,8,128]{3,2,1,0:T(8,128)S(1)} %get-tuple-element.18), channel_id=1, source_target_pairs={{8,0},{9,1},{10,2},{11,3},{12,4},{13,5},{14,6},{15,7},{16,8},{17,9... | collective-permute-start | bytes 847880 | tf_op jit(solution)/shard_map/ppermute | solution.py:481
  12.8 2.8 %collective-permute-start.1 = (f32[344,128]{1,0:T(8,128)S(1)}, f32[344,128]{1,0:T(8,128)S(1)}, u32[]{:S(2)}, u32[]{:S(2)}) collective-permute-start(f32[344,128]{1,0:T(8,128)S(1)} %get-tuple-element.16), channel_id=1, source_target_pairs={{0,6},{1,7},{2,0},{3,1},{4,2},{5,3},{6,4},{7,5},{8,14},{9,15},{10,... | collective-permute-start | bytes 528392 | tf_op jit(solution)/shard_map/ppermute | solution.py:481
  15.6 0.0 collective-permute-start.2
  15.6 1.2 %collective-permute-done.3.grow = f32[3,23,8,128]{3,2,1,0:T(8,128)S(1)} collective-permute-done((f32[3,23,8,128]{3,2,1,0:T(8,128)S(1)}, f32[3,23,8,128]{3,2,1,0:T(8,128)S(1)}, u32[]{:S(2)}, u32[]{:S(2)}) %collective-permute-start.3) | collective-permute-done | bytes 282656 | tf_op jit(solution)/shard_map/ppermute | solution.py:481
  16.9 2.8 %collective-permute-start.4 = (f32[312,128]{1,0:T(8,128)S(1)}, f32[312,128]{1,0:T(8,128)S(1)}, u32[]{:S(2)}, u32[]{:S(2)}) collective-permute-start(f32[312,128]{1,0:T(8,128)S(1)} %get-tuple-element.19), channel_id=1, source_target_pairs={{0,6},{1,7},{2,0},{3,1},{4,2},{5,3},{6,4},{7,5},{8,14},{9,15},{10,... | collective-permute-start | bytes 479240 | tf_op jit(solution)/shard_map/ppermute | solution.py:481
  19.8 0.0 collective-permute-start.5
  19.8 0.1 pad_add_fusion.where_ref
  19.8 0.2 collective-permute-done.1.own_lo
  20.0 3.9 %collective-permute-done.2.own_hi = f32[344,128]{1,0:T(8,128)S(1)} collective-permute-done((f32[344,128]{1,0:T(8,128)S(1)}, f32[344,128]{1,0:T(8,128)S(1)}, u32[]{:S(2)}, u32[]{:S(2)}) %collective-permute-start.2) | collective-permute-done | bytes 176160 | tf_op jit(solution)/shard_map/ppermute | solution.py:481
  23.9 7.2 %lower_half.1 = (f32[4,32,8,128]{3,2,1,0:T(8,128)}, f32[2,32,8,128]{3,2,1,0:T(8,128)}, f32[4,7,2,16,128]{4,3,2,1,0:T(8,128)S(1)}) custom-call(s32[2]{0:T(128)S(1)} %pad_add_fusion.where_ref, f32[3,32,8,128]{3,2,1,0:T(8,128)S(1)} %get-tuple-element.13.cells, f32[16,8,128]{2,1,0:T(8,128)S(1)} %get-tuple-element.14.codes, ...), custom_call_target="tpu_custom_call" | custom-call | flops 60000000 | bytes 12000000 | tf_op jit(solution)/shard_map/lower_half/pallas_call | solution.py:532
  31.1 0.0 collective-permute-done.4.up_lo
  31.1 0.0 collective-permute-done.5.up_hi
  31.1 9.5 %upper_half.1 = (f32[4,32,8,128]{3,2,1,0:T(8,128)}, f32[2,32,8,128]{3,2,1,0:T(8,128)}) custom-call(s32[2]{0:T(128)S(1)} %pad_add_fusion.where_ref, f32[3,32,8,128]{3,2,1,0:T(8,128)S(1)} %get-tuple-element.13.cells, f32[16,8,128]{2,1,0:T(8,128)S(1)} %get-tuple-element.14.codes, f32[2,8]{1,0:T(2,128)} %table_in.1, ...), custom_call_target="tpu_custom_call", output_to_operand_aliasing={{0}: (11, {}), {1}: (12, {})} | custom-call | tf_op jit(solution)/shard_map/upper_half/pallas_call | solution.py:545
  (1 shorter events, 0.0 us)
Async XLA Ops:
  1.9 4.1 %collective-permute-start = (f32[10,8,128]{2,1,0:T(8,128)S(1)}, f32[10,8,128]{2,1,0:T(8,128)S(1)}, u32[]{:S(2)}, u32[]{:S(2)}) collective-permute-start(f32[10,8,128]{2,1,0:T(8,128)S(1)} %get-tuple-element.15), channel_id=1, source_target_pairs={{0,1},{1,0},{2,3},{3,2},{4,5},{5,4},{6,7},{7,6},{8,9},{9,8},{10,11... | collective-permute-start | bytes 122888 | tf_op jit(solution)/shard_map/ppermute | solution.py:481
  6.1 10.8 %collective-permute-start.3 = (f32[3,23,8,128]{3,2,1,0:T(8,128)S(1)}, f32[3,23,8,128]{3,2,1,0:T(8,128)S(1)}, u32[]{:S(2)}, u32[]{:S(2)}) collective-permute-start(f32[3,23,8,128]{3,2,1,0:T(8,128)S(1)} %get-tuple-element.18), channel_id=1, source_target_pairs={{8,0},{9,1},{10,2},{11,3},{12,4},{13,5},{14,6},{15,7},{16,8},{17,9... | collective-permute-start | bytes 847880 | tf_op jit(solution)/shard_map/ppermute | solution.py:481
  12.8 7.2 %collective-permute-start.1 = (f32[344,128]{1,0:T(8,128)S(1)}, f32[344,128]{1,0:T(8,128)S(1)}, u32[]{:S(2)}, u32[]{:S(2)}) collective-permute-start(f32[344,128]{1,0:T(8,128)S(1)} %get-tuple-element.16), channel_id=1, source_target_pairs={{0,6},{1,7},{2,0},{3,1},{4,2},{5,3},{6,4},{7,5},{8,14},{9,15},{10,... | collective-permute-start | bytes 528392 | tf_op jit(solution)/shard_map/ppermute | solution.py:481
  15.6 8.3 %collective-permute-start.2 = (f32[344,128]{1,0:T(8,128)S(1)}, f32[344,128]{1,0:T(8,128)S(1)}, u32[]{:S(2)}, u32[]{:S(2)}) collective-permute-start(f32[344,128]{1,0:T(8,128)S(1)} %get-tuple-element.17), channel_id=1, source_target_pairs={{0,2},{1,3},{2,4},{3,5},{4,6},{5,7},{6,0},{7,1},{8,10},{9,11},{10,... | collective-permute-start | bytes 528392 | tf_op jit(solution)/shard_map/ppermute | solution.py:481
  16.9 14.2 %collective-permute-start.4 = (f32[312,128]{1,0:T(8,128)S(1)}, f32[312,128]{1,0:T(8,128)S(1)}, u32[]{:S(2)}, u32[]{:S(2)}) collective-permute-start(f32[312,128]{1,0:T(8,128)S(1)} %get-tuple-element.19), channel_id=1, source_target_pairs={{0,6},{1,7},{2,0},{3,1},{4,2},{5,3},{6,4},{7,5},{8,14},{9,15},{10,... | collective-permute-start | bytes 479240 | tf_op jit(solution)/shard_map/ppermute | solution.py:481
  19.8 11.4 %collective-permute-start.5 = (f32[312,128]{1,0:T(8,128)S(1)}, f32[312,128]{1,0:T(8,128)S(1)}, u32[]{:S(2)}, u32[]{:S(2)}) collective-permute-start(f32[312,128]{1,0:T(8,128)S(1)} %get-tuple-element.20), channel_id=1, source_target_pairs={{0,2},{1,3},{2,4},{3,5},{4,6},{5,7},{6,0},{7,1},{8,10},{9,11},{10,... | collective-permute-start | bytes 479240 | tf_op jit(solution)/shard_map/ppermute | solution.py:481

commit v4 on v3

--- a/solution.py
+++ b/solution.py
@@ -125,8 +125,7 @@
 
 
 def react(phases, sums, chem, chem_sums, held):
-    p0, p1, p2 = phases
-    p3 = K - ((p0 + p1) + p2)
+    p0, p1, p2, p3 = phases
     n3 = 6.0 * K - ((sums[0] + sums[1]) + sums[2])
     ps = (p0, p1, p2, p3)
     ns = (sums[0], sums[1], sums[2], n3)
@@ -153,10 +152,10 @@
 
 
 class Half:
-    def __init__(self, base, strip_base, n, cells, codes, across, own, up, grow, lane):
+    def __init__(self, base, strip_base, n, cells, codes, across, own, up, grow, wing):
         self.base, self.strip_base, self.n = base, strip_base, n
         self.cells, self.codes, self.across = cells, codes, across
-        self.own, self.up, self.grow, self.lane = own, up, grow, lane
+        self.own, self.up, self.grow, self.wing, self.lane = own, up, grow, wing, lanes()
 
     def source(self, p):
         up = p >= OWN
@@ -169,6 +168,7 @@
         rest = jnp.where(label == 3.0, 3.5 * HALF, HALF)
         values += [ALPHA * m0, ALPHA * m1]
         values += [values[3 + i] + jnp.where(label == i, 8.0 * HALF, rest) for i in range(2)]
+        values.append(jnp.where(label == 3.0, K, 0.0))
         for f, value in enumerate(values):
             if mask is not None:
                 value = jnp.where(mask, value, dst[f, index, rows, :])
@@ -298,27 +298,40 @@
             total = (below + above) + (
                 src[f, index, row - 1 : row + 7, :] + src[f, index, row + 1 : row + 9, :]
             )
-            left, right = sides(f, pltpu.roll(mid, 1, 1), pltpu.roll(mid, 127, 1))
+            left, right = sides(f, mid)
             here.append(mid)
             sums.append(total + (left + right))
         held = [src[f, index, row : row + 8, :] for f in (5, 6)]
-        return react(here[:3], sums[:3], here[3:], sums[3:], held)
-
-    def plane_step(self, src, strips, p, row):
+        liquid = src[7, index, row : row + 8, :]
+        return react((*here[:3], liquid), sums[:3], here[3:], sums[3:], held)
+
+    def spread(self, strips, rows):
+        second = self.lane == 5
+        for j in range(1, 6):
+            second = second | (self.lane == 20 * j + 5)
+        for f in range(5):
+            for index in range(self.n):
+                for row in rows:
+                    tile = strips[f, index, row : row + 8, :]
+                    tile = jnp.where(second, pltpu.roll(tile, 118, 1), tile)
+                    self.wing[f, index, row : row + 8, :] = tile
+
+    def plane_step(self, src, p, row):
         index = p - self.base
         q = p - self.strip_base
         j = (q * 13) >> 6 if self.n == 5 else q >> 2
         at = q - self.n * j
-        to_first, to_last = 124 - 20 * j, 112 - 20 * j
+        turn = 123 - 20 * j
         rows = slice(row, row + 8)
 
         def fetch(f):
             return src[f, index - 1, rows, :], src[f, index + 1, rows, :]
 
-        def sides(f, left, right):
-            strip = strips[f, at, rows, :]
-            left = jnp.where(self.lane == 0, pltpu.roll(strip, to_first, 1), left)
-            return left, jnp.where(self.lane == 127, pltpu.roll(strip, to_last, 1), right)
+        def sides(f, mid):
+            beyond = pltpu.roll(self.wing[f, at, rows, :], turn, 1)
+            left = jnp.where(self.lane == 127, beyond, mid)
+            right = jnp.where(self.lane == 0, beyond, mid)
+            return pltpu.roll(left, 1, 1), pltpu.roll(right, 127, 1)
 
         return self.advance(src, index, row, fetch, sides)
 
@@ -330,14 +343,20 @@
             body(p)
 
     def sweep(self, src, dst, src_strips, dst_strips, first, count):
+        self.spread(src_strips, (8, 16))
+
         def body(p):
             for row in (8, 16):
-                new, chem, held = self.plane_step(src, src_strips, p, row)
-                for f, value in enumerate((*new[:3], *chem, *held)):
+                new, chem, held = self.plane_step(src, p, row)
+                for f, value in enumerate((*new[:3], *chem, *held, new[3])):
                     dst[f, p - self.base, row : row + 8, :] = value
 
         self.planes(first, count, body)
         last = self.n - 1
+
+        def inside(f, mid):
+            return pltpu.roll(mid, 1, 1), pltpu.roll(mid, 127, 1)
+
         for index in range(self.n):
             for row in (8, 16):
                 rows = slice(row, row + 8)
@@ -354,18 +373,18 @@
                     return below, above
 
                 new, chem, held = self.advance(
-                    src_strips, index, row, fetch, lambda f, left, right: (left, right)
+                    src_strips, index, row, fetch, inside
                 )
-                for f, value in enumerate((*new[:3], *chem, *held)):
+                for f, value in enumerate((*new[:3], *chem, *held, new[3])):
                     dst_strips[f, index, row : row + 8, :] = value
 
-    def finish(self, src, strips, first, count, phases, chems):
+    def finish(self, src, first, count, phases, chems, at=0):
         def body(p):
-            new, chem, _ = self.plane_step(src, strips, p, ROW0)
+            new, chem, _ = self.plane_step(src, p, ROW0)
             for a in range(4):
-                phases[a, p - first] = new[a] * (1.0 / K)
+                phases[a, p - first + at] = new[a] * (1.0 / K)
             for i in range(2):
-                chems[i, p - first] = chem[i] * (1.0 / ALPHA)
+                chems[i, p - first + at] = chem[i] * (1.0 / ALPHA)
 
         self.planes(first, count, body)
 
@@ -376,11 +395,11 @@
 
 
 def lower_half(
-    where_ref, cells, codes, across, own_lo, own_hi, phases_out, chem_out, seam,
-    one, two, strip_one, strip_two, phases, chems, sems,
+    where_ref, cells, codes, across, own_lo, own_hi, phases, chems, seam,
+    one, two, strip_one, strip_two, wing,
 ):
     first = where_ref[0] == 0
-    half = Half(0, 0, 4, cells, codes, across, (own_lo, own_hi), None, None, lanes())
+    half = Half(0, 0, 4, cells, codes, across, (own_lo, own_hi), None, None, wing)
     for p in range(OWN):
         half.fill(one, p)
     half.fill_strips(strip_one, OWN)
@@ -394,7 +413,7 @@
                 half.repeat_strip(src_strips, 4, 5)
 
         half.sweep(src, dst, src_strips, dst_strips, s, OWN - 2 * s)
-        for f in range(7):
+        for f in range(8):
             for i in range(2):
                 seam[s - 1, f, i] = dst[f, OWN - 1 - s + i - 1, 8:24, :]
         src, dst, src_strips, dst_strips = dst, src, dst_strips, src_strips
@@ -403,30 +422,31 @@
     def _(src=src):
         half.repeat(src, 4, 5)
 
-    half.finish(src, src_strips, 5, LOWER, phases, chems)
-    deliver(phases, chems, phases_out, chem_out, 0, LOWER, sems)
-
-
-def deliver(phases, chems, phases_out, chem_out, first, count, sems):
+    half.spread(src_strips, (ROW0,))
+    half.finish(src, 5, LOWER, phases, chems)
+
+
+def delivery(phases, chems, phases_out, chem_out, first, at, count, sems, s):
+    source, target = pl.ds(at, count), pl.ds(first, count)
     copies = [
-        pltpu.make_async_copy(phases, phases_out.at[:, pl.ds(first, count)], sems.at[0]),
-        pltpu.make_async_copy(chems, chem_out.at[:, pl.ds(first, count)], sems.at[1]),
+        pltpu.make_async_copy(phases.at[:, source], phases_out.at[:, target], sems.at[s]),
+        pltpu.make_async_copy(chems.at[:, source], chem_out.at[:, target], sems.at[s + 1]),
     ]
     for copy in copies:
         copy.start()
-    for copy in copies:
-        copy.wait()
+    return copies
 
 
 def upper_half(
     where_ref, cells, codes, table_in, across, own_lo, own_hi, up_lo, up_hi, grow, seam,
-    phases_in, chem_in, phases_out, chem_out,
-    one, two, strip_one, strip_two, phases, chems, table, sem, sems,
+    lower_phases, lower_chems, phases_out, chem_out,
+    one, two, strip_one, strip_two, wing, phases, chems, table, sem, sems,
 ):
-    del phases_in, chem_in
+    outs = (phases_out, chem_out)
+    copies = delivery(lower_phases, lower_chems, *outs, 0, 0, LOWER, sems, 0)
     last = where_ref[0] == where_ref[1] - 1
     half = Half(
-        15, 12, 5, cells, codes, across, (own_lo, own_hi), (up_lo, up_hi), grow, lanes()
+        15, 12, 5, cells, codes, across, (own_lo, own_hi), (up_lo, up_hi), grow, wing
     )
     for p in range(OWN - 2, PLANES):
         half.fill(one, p)
@@ -434,7 +454,7 @@
     src, dst, src_strips, dst_strips = one, two, strip_one, strip_two
     for s in range(1, 6):
         if s > 1:
-            for f in range(7):
+            for f in range(8):
                 for i in range(2):
                     src[f, OWN - 1 - s + i - half.base, 8:24, :] = seam[s - 2, f, i]
         if s < 4:
@@ -463,8 +483,13 @@
         if s < 5:
             half.sweep(src, dst, src_strips, dst_strips, OWN - s, OWN)
             src, dst, src_strips, dst_strips = dst, src, dst_strips, src_strips
-    half.finish(src, src_strips, OWN - 5, OWN, phases, chems)
-    deliver(phases, chems, phases_out, chem_out, LOWER, OWN, sems)
+    half.spread(src_strips, (ROW0,))
+    half.finish(src, OWN - 5, 12, phases, chems)
+    copies += delivery(phases, chems, *outs, LOWER, 0, 12, sems, 2)
+    half.finish(src, OWN + 7, 9, phases, chems, 12)
+    copies += delivery(phases, chems, *outs, LOWER + 12, 12, 9, sems, 4)
+    for copy in copies:
+        copy.wait()
 
 
 def on_device(labels, potential, melt_codes, melt_table):
@@ -520,21 +545,19 @@
     up_lo = send(up_lo, 0, -1, 0)
     up_hi = send(up_hi, 0, 1, 0)
 
-    def buffers(planes, strips, count):
+    def buffers(planes, strips):
         return (
-            [pltpu.VMEM((7, planes, PITCH, 128), jnp.float32)] * 2
-            + [pltpu.VMEM((7, strips, PITCH, 128), jnp.float32)] * 2
-            + [pltpu.VMEM((4, count, 8, 128), jnp.float32)]
-            + [pltpu.VMEM((2, count, 8, 128), jnp.float32)]
+            [pltpu.VMEM((8, planes, PITCH, 128), jnp.float32)] * 2
+            + [pltpu.VMEM((8, strips, PITCH, 128), jnp.float32)] * 2
+            + [pltpu.VMEM((5, strips, PITCH, 128), jnp.float32)]
         )
 
-    outputs = [f32(4, 32, 8, 128), f32(2, 32, 8, 128)]
     phases, chems, seam = pl.pallas_call(
         lower_half,
         in_specs=[SMEM] + [VMEM] * 5,
-        out_specs=[HBM, HBM, VMEM],
-        out_shape=outputs + [f32(4, 7, 2, 16, 128)],
-        scratch_shapes=buffers(OWN, 4, LOWER) + [pltpu.SemaphoreType.DMA((2,))],
+        out_specs=[VMEM] * 3,
+        out_shape=[f32(4, LOWER, 8, 128), f32(2, LOWER, 8, 128), f32(4, 8, 2, 16, 128)],
+        scratch_shapes=buffers(OWN, 4),
         compiler_params=params,
         cost_estimate=pl.CostEstimate(
             flops=60_000_000, bytes_accessed=12_000_000, transcendentals=0
@@ -544,12 +567,17 @@
     table = pltpu.with_memory_space_constraint(melt_table, pltpu.MemorySpace.HBM)
     return pl.pallas_call(
         upper_half,
-        in_specs=[SMEM, VMEM, VMEM, HBM] + [VMEM] * 7 + [HBM, HBM],
+        in_specs=[SMEM, VMEM, VMEM, HBM] + [VMEM] * 9,
         out_specs=[HBM, HBM],
-        out_shape=outputs,
-        scratch_shapes=buffers(27, 5, OWN)
-        + [pltpu.SMEM((2, 8), jnp.float32), pltpu.SemaphoreType.DMA, pltpu.SemaphoreType.DMA((2,))],
-        input_output_aliases={11: 0, 12: 1},
+        out_shape=[f32(4, 32, 8, 128), f32(2, 32, 8, 128)],
+        scratch_shapes=buffers(27, 5)
+        + [
+            pltpu.VMEM((4, OWN, 8, 128), jnp.float32),
+            pltpu.VMEM((2, OWN, 8, 128), jnp.float32),
+            pltpu.SMEM((2, 8), jnp.float32),
+            pltpu.SemaphoreType.DMA,
+            pltpu.SemaphoreType.DMA((6,)),
+        ],
         compiler_params=params,
         name="upper_half",
     )(where, cells, codes, table, across, own_lo, own_hi, up_lo, up_hi, grow, seam, phases, chems)

time: 40.8 us -> 43.4 us (1.064)
  Pallas kernels: 18.1 us -> 20.7 us
    pallas_call x2, Pallas kernels: 16.7 us -> 19.3 us  [the longest x1 10.8 us: on_device(): pl.pallas_call(upper_half, in_specs=[SMEM, VMEM, VMEM, HBM] + [VMEM] * 9,...]
  transfers between devices with their start and end apart: 6 -> 6, of which waited for: 4 -> 4; matrix products, arithmetic and copies ran while one was open for 0% -> 0% of each run, Pallas kernels for 18% -> 20%
where the time goes in v4:
time: 43.4 us; the launch traced here: 43.2 us
  Pallas kernels  20.7 us (48%)
  starting transfers between devices  13.2 us (30%)
  waiting for transfers between devices  8.58 us (20%)
  between operations  0.68 us (2%)
    ppermute x6, starting transfers between devices, send(): return lax.ppermute(value, AXES, pairs)  13.2 us
    pallas_call x1, Pallas kernels, on_device(): pl.pallas_call(upper_half, in_specs=[SMEM, VMEM, VMEM, HBM] + [VMEM] * 9,...  10.8 us
    ppermute x6, waiting for transfers between devices, send(): return lax.ppermute(value, AXES, pairs)  8.58 us
    pallas_call x1, Pallas kernels, on_device(): pl.pallas_call(lower_half, in_specs=[SMEM] + [VMEM] * 5, out_specs=[VMEM]...  8.48 us
    pallas_call x1, Pallas kernels, on_device(): pl.pallas_call(first_pack, in_specs=[HBM] * 3, out_specs=[VMEM] * 3, out_...  1.26 us
  transfers between devices with their start and end apart: 6, of which 4 were waited for; matrix products, arithmetic and copies ran while one was open for 0% of the time, Pallas kernels for 20%

profile of v4, /device:TPU:24, one launch (start us, length us, event | category | flops | bytes accessed | tf_op | source)
XLA Modules:
  0.0 43.2 jit_solution(3807580254448696087)
XLA Ops:
  0.6 1.3 %first_pack.1 = (f32[3,32,8,128]{3,2,1,0:T(8,128)S(1)}, f32[16,8,128]{2,1,0:T(8,128)S(1)}, f32[10,8,128]{2,1,0:T(8,128)S(1)}) custom-call(s32[32,8,128]{2,1,0:T(8,128)} %labels.1, f32[2,32,8,128]{3,2,1,0:T(8,128)} %potential.1, s32[16,8,128]{2,1,0:T(8,128)} %codes.1), custom_call_target="tpu_custom_call" | custom-call | tf_op jit(solution)/shard_map/first_pack/pallas_call | solution.py:512
  1.9 0.8 %collective-permute-start = (f32[10,8,128]{2,1,0:T(8,128)S(1)}, f32[10,8,128]{2,1,0:T(8,128)S(1)}, u32[]{:S(2)}, u32[]{:S(2)}) collective-permute-start(f32[10,8,128]{2,1,0:T(8,128)S(1)} %get-tuple-element.15), channel_id=1, source_target_pairs={{0,1},{1,0},{2,3},{3,2},{4,5},{5,4},{6,7},{7,6},{8,9},{9,8},{10,11... | collective-permute-start | bytes 122888 | tf_op jit(solution)/shard_map/ppermute | solution.py:506
  2.7 3.3 %collective-permute-done.across = f32[10,8,128]{2,1,0:T(8,128)S(1)} collective-permute-done((f32[10,8,128]{2,1,0:T(8,128)S(1)}, f32[10,8,128]{2,1,0:T(8,128)S(1)}, u32[]{:S(2)}, u32[]{:S(2)}) %collective-permute-start) | collective-permute-done | bytes 40992 | tf_op jit(solution)/shard_map/ppermute | solution.py:506
  6.0 0.1 second_pack.1
  6.1 6.7 %collective-permute-start.3 = (f32[3,23,8,128]{3,2,1,0:T(8,128)S(1)}, f32[3,23,8,128]{3,2,1,0:T(8,128)S(1)}, u32[]{:S(2)}, u32[]{:S(2)}) collective-permute-start(f32[3,23,8,128]{3,2,1,0:T(8,128)S(1)} %get-tuple-element.18), channel_id=1, source_target_pairs={{8,0},{9,1},{10,2},{11,3},{12,4},{13,5},{14,6},{15,7},{16,8},{17,9... | collective-permute-start | bytes 847880 | tf_op jit(solution)/shard_map/ppermute | solution.py:506
  12.8 2.8 %collective-permute-start.1 = (f32[344,128]{1,0:T(8,128)S(1)}, f32[344,128]{1,0:T(8,128)S(1)}, u32[]{:S(2)}, u32[]{:S(2)}) collective-permute-start(f32[344,128]{1,0:T(8,128)S(1)} %get-tuple-element.16), channel_id=1, source_target_pairs={{0,6},{1,7},{2,0},{3,1},{4,2},{5,3},{6,4},{7,5},{8,14},{9,15},{10,... | collective-permute-start | bytes 528392 | tf_op jit(solution)/shard_map/ppermute | solution.py:506
  15.6 0.0 collective-permute-start.2
  15.6 1.2 %collective-permute-done.3.grow = f32[3,23,8,128]{3,2,1,0:T(8,128)S(1)} collective-permute-done((f32[3,23,8,128]{3,2,1,0:T(8,128)S(1)}, f32[3,23,8,128]{3,2,1,0:T(8,128)S(1)}, u32[]{:S(2)}, u32[]{:S(2)}) %collective-permute-start.3) | collective-permute-done | bytes 282656 | tf_op jit(solution)/shard_map/ppermute | solution.py:506
  16.9 2.8 %collective-permute-start.4 = (f32[312,128]{1,0:T(8,128)S(1)}, f32[312,128]{1,0:T(8,128)S(1)}, u32[]{:S(2)}, u32[]{:S(2)}) collective-permute-start(f32[312,128]{1,0:T(8,128)S(1)} %get-tuple-element.19), channel_id=1, source_target_pairs={{0,6},{1,7},{2,0},{3,1},{4,2},{5,3},{6,4},{7,5},{8,14},{9,15},{10,... | collective-permute-start | bytes 479240 | tf_op jit(solution)/shard_map/ppermute | solution.py:506
  19.8 0.0 collective-permute-start.5
  19.8 0.1 pad_add_fusion.where_ref
  19.8 0.2 collective-permute-done.1.own_lo
  20.0 3.9 %collective-permute-done.2.own_hi = f32[344,128]{1,0:T(8,128)S(1)} collective-permute-done((f32[344,128]{1,0:T(8,128)S(1)}, f32[344,128]{1,0:T(8,128)S(1)}, u32[]{:S(2)}, u32[]{:S(2)}) %collective-permute-start.2) | collective-permute-done | bytes 176160 | tf_op jit(solution)/shard_map/ppermute | solution.py:506
  23.9 8.5 %lower_half.1 = (f32[4,11,8,128]{3,2,1,0:T(8,128)S(1)}, f32[2,11,8,128]{3,2,1,0:T(8,128)S(1)}, f32[4,8,2,16,128]{4,3,2,1,0:T(8,128)S(1)}) custom-call(s32[2]{0:T(128)S(1)} %pad_add_fusion.where_ref, f32[3,32,8,128]{3,2,1,0:T(8,128)S(1)} %get-tuple-element.13.cells, f32[16,8,128]{2,1,0:T(8,128)S(1)} %get-tuple-element.14.codes, ...), custom_call_target="tpu_custom_call" | custom-call | flops 60000000 | bytes 12000000 | tf_op jit(solution)/shard_map/lower_half/pallas_call | solution.py:555
  32.4 0.0 collective-permute-done.4.up_lo
  32.4 0.0 collective-permute-done.5.up_hi
  32.4 10.8 %upper_half.1 = (f32[4,32,8,128]{3,2,1,0:T(8,128)}, f32[2,32,8,128]{3,2,1,0:T(8,128)}) custom-call(s32[2]{0:T(128)S(1)} %pad_add_fusion.where_ref, f32[3,32,8,128]{3,2,1,0:T(8,128)S(1)} %get-tuple-element.13.cells, f32[16,8,128]{2,1,0:T(8,128)S(1)} %get-tuple-element.14.codes, f32[2,8]{1,0:T(2,128)} %table_in.1, ...), custom_call_target="tpu_custom_call" | custom-call | tf_op jit(solution)/shard_map/upper_half/pallas_call | solution.py:568
  (1 shorter events, 0.0 us)
Async XLA Ops:
  1.9 4.1 %collective-permute-start = (f32[10,8,128]{2,1,0:T(8,128)S(1)}, f32[10,8,128]{2,1,0:T(8,128)S(1)}, u32[]{:S(2)}, u32[]{:S(2)}) collective-permute-start(f32[10,8,128]{2,1,0:T(8,128)S(1)} %get-tuple-element.15), channel_id=1, source_target_pairs={{0,1},{1,0},{2,3},{3,2},{4,5},{5,4},{6,7},{7,6},{8,9},{9,8},{10,11... | collective-permute-start | bytes 122888 | tf_op jit(solution)/shard_map/ppermute | solution.py:506
  6.1 10.8 %collective-permute-start.3 = (f32[3,23,8,128]{3,2,1,0:T(8,128)S(1)}, f32[3,23,8,128]{3,2,1,0:T(8,128)S(1)}, u32[]{:S(2)}, u32[]{:S(2)}) collective-permute-start(f32[3,23,8,128]{3,2,1,0:T(8,128)S(1)} %get-tuple-element.18), channel_id=1, source_target_pairs={{8,0},{9,1},{10,2},{11,3},{12,4},{13,5},{14,6},{15,7},{16,8},{17,9... | collective-permute-start | bytes 847880 | tf_op jit(solution)/shard_map/ppermute | solution.py:506
  12.8 7.2 %collective-permute-start.1 = (f32[344,128]{1,0:T(8,128)S(1)}, f32[344,128]{1,0:T(8,128)S(1)}, u32[]{:S(2)}, u32[]{:S(2)}) collective-permute-start(f32[344,128]{1,0:T(8,128)S(1)} %get-tuple-element.16), channel_id=1, source_target_pairs={{0,6},{1,7},{2,0},{3,1},{4,2},{5,3},{6,4},{7,5},{8,14},{9,15},{10,... | collective-permute-start | bytes 528392 | tf_op jit(solution)/shard_map/ppermute | solution.py:506
  15.6 8.3 %collective-permute-start.2 = (f32[344,128]{1,0:T(8,128)S(1)}, f32[344,128]{1,0:T(8,128)S(1)}, u32[]{:S(2)}, u32[]{:S(2)}) collective-permute-start(f32[344,128]{1,0:T(8,128)S(1)} %get-tuple-element.17), channel_id=1, source_target_pairs={{0,2},{1,3},{2,4},{3,5},{4,6},{5,7},{6,0},{7,1},{8,10},{9,11},{10,... | collective-permute-start | bytes 528392 | tf_op jit(solution)/shard_map/ppermute | solution.py:506
  16.9 15.5 %collective-permute-start.4 = (f32[312,128]{1,0:T(8,128)S(1)}, f32[312,128]{1,0:T(8,128)S(1)}, u32[]{:S(2)}, u32[]{:S(2)}) collective-permute-start(f32[312,128]{1,0:T(8,128)S(1)} %get-tuple-element.19), channel_id=1, source_target_pairs={{0,6},{1,7},{2,0},{3,1},{4,2},{5,3},{6,4},{7,5},{8,14},{9,15},{10,... | collective-permute-start | bytes 479240 | tf_op jit(solution)/shard_map/ppermute | solution.py:506
  19.8 12.7 %collective-permute-start.5 = (f32[312,128]{1,0:T(8,128)S(1)}, f32[312,128]{1,0:T(8,128)S(1)}, u32[]{:S(2)}, u32[]{:S(2)}) collective-permute-start(f32[312,128]{1,0:T(8,128)S(1)} %get-tuple-element.20), channel_id=1, source_target_pairs={{0,2},{1,3},{2,4},{3,5},{4,6},{5,7},{6,0},{7,1},{8,10},{9,11},{10,... | collective-permute-start | bytes 479240 | tf_op jit(solution)/shard_map/ppermute | solution.py:506

commit v5 on v4

--- a/solution.py
+++ b/solution.py
@@ -125,7 +125,8 @@
 
 
 def react(phases, sums, chem, chem_sums, held):
-    p0, p1, p2, p3 = phases
+    p0, p1, p2 = phases
+    p3 = K - ((p0 + p1) + p2)
     n3 = 6.0 * K - ((sums[0] + sums[1]) + sums[2])
     ps = (p0, p1, p2, p3)
     ns = (sums[0], sums[1], sums[2], n3)
@@ -168,7 +169,6 @@
         rest = jnp.where(label == 3.0, 3.5 * HALF, HALF)
         values += [ALPHA * m0, ALPHA * m1]
         values += [values[3 + i] + jnp.where(label == i, 8.0 * HALF, rest) for i in range(2)]
-        values.append(jnp.where(label == 3.0, K, 0.0))
         for f, value in enumerate(values):
             if mask is not None:
                 value = jnp.where(mask, value, dst[f, index, rows, :])
@@ -302,18 +302,17 @@
             here.append(mid)
             sums.append(total + (left + right))
         held = [src[f, index, row : row + 8, :] for f in (5, 6)]
-        liquid = src[7, index, row : row + 8, :]
-        return react((*here[:3], liquid), sums[:3], here[3:], sums[3:], held)
+        return react(here[:3], sums[:3], here[3:], sums[3:], held)
 
     def spread(self, strips, rows):
-        second = self.lane == 5
+        second = self.lane == 3
         for j in range(1, 6):
-            second = second | (self.lane == 20 * j + 5)
+            second = second | (self.lane == 20 * j + 3)
         for f in range(5):
             for index in range(self.n):
                 for row in rows:
                     tile = strips[f, index, row : row + 8, :]
-                    tile = jnp.where(second, pltpu.roll(tile, 118, 1), tile)
+                    tile = jnp.where(second, pltpu.roll(tile, 116, 1), tile)
                     self.wing[f, index, row : row + 8, :] = tile
 
     def plane_step(self, src, p, row):
@@ -321,7 +320,7 @@
         q = p - self.strip_base
         j = (q * 13) >> 6 if self.n == 5 else q >> 2
         at = q - self.n * j
-        turn = 123 - 20 * j
+        turn = 124 - 20 * j
         rows = slice(row, row + 8)
 
         def fetch(f):
@@ -329,16 +328,15 @@
 
         def sides(f, mid):
             beyond = pltpu.roll(self.wing[f, at, rows, :], turn, 1)
-            left = jnp.where(self.lane == 127, beyond, mid)
-            right = jnp.where(self.lane == 0, beyond, mid)
-            return pltpu.roll(left, 1, 1), pltpu.roll(right, 127, 1)
+            left = jnp.where(self.lane == 0, beyond, pltpu.roll(mid, 1, 1))
+            return left, jnp.where(self.lane == 127, beyond, pltpu.roll(mid, 127, 1))
 
         return self.advance(src, index, row, fetch, sides)
 
     def planes(self, first, count, body):
-        whole = count - count % 4
+        whole = count - count % 8
         if whole:
-            pl.loop(first, first + whole, unroll=4)(body)
+            pl.loop(first, first + whole, unroll=8)(body)
         for p in range(first + whole, first + count):
             body(p)
 
@@ -348,7 +346,7 @@
         def body(p):
             for row in (8, 16):
                 new, chem, held = self.plane_step(src, p, row)
-                for f, value in enumerate((*new[:3], *chem, *held, new[3])):
+                for f, value in enumerate((*new[:3], *chem, *held)):
                     dst[f, p - self.base, row : row + 8, :] = value
 
         self.planes(first, count, body)
@@ -375,7 +373,7 @@
                 new, chem, held = self.advance(
                     src_strips, index, row, fetch, inside
                 )
-                for f, value in enumerate((*new[:3], *chem, *held, new[3])):
+                for f, value in enumerate((*new[:3], *chem, *held)):
                     dst_strips[f, index, row : row + 8, :] = value
 
     def finish(self, src, first, count, phases, chems, at=0):
@@ -413,7 +411,7 @@
                 half.repeat_strip(src_strips, 4, 5)
 
         half.sweep(src, dst, src_strips, dst_strips, s, OWN - 2 * s)
-        for f in range(8):
+        for f in range(7):
             for i in range(2):
                 seam[s - 1, f, i] = dst[f, OWN - 1 - s + i - 1, 8:24, :]
         src, dst, src_strips, dst_strips = dst, src, dst_strips, src_strips
@@ -454,7 +452,7 @@
     src, dst, src_strips, dst_strips = one, two, strip_one, strip_two
     for s in range(1, 6):
         if s > 1:
-            for f in range(8):
+            for f in range(7):
                 for i in range(2):
                     src[f, OWN - 1 - s + i - half.base, 8:24, :] = seam[s - 2, f, i]
         if s < 4:
@@ -547,8 +545,8 @@
 
     def buffers(planes, strips):
         return (
-            [pltpu.VMEM((8, planes, PITCH, 128), jnp.float32)] * 2
-            + [pltpu.VMEM((8, strips, PITCH, 128), jnp.float32)] * 2
+            [pltpu.VMEM((7, planes, PITCH, 128), jnp.float32)] * 2
+            + [pltpu.VMEM((7, strips, PITCH, 128), jnp.float32)] * 2
             + [pltpu.VMEM((5, strips, PITCH, 128), jnp.float32)]
         )
 
@@ -556,7 +554,7 @@
         lower_half,
         in_specs=[SMEM] + [VMEM] * 5,
         out_specs=[VMEM] * 3,
-        out_shape=[f32(4, LOWER, 8, 128), f32(2, LOWER, 8, 128), f32(4, 8, 2, 16, 128)],
+        out_shape=[f32(4, LOWER, 8, 128), f32(2, LOWER, 8, 128), f32(4, 7, 2, 16, 128)],
         scratch_shapes=buffers(OWN, 4),
         compiler_params=params,
         cost_estimate=pl.CostEstimate(

time: 43.4 us -> 38.4 us (0.88)
  Pallas kernels: 20.7 us -> 15.5 us
    pallas_call x1, Pallas kernels: 8.48 us -> 5.7 us  [on_device(): pl.pallas_call(lower_half, in_specs=[SMEM] + [VMEM] * 5, out_specs=[VMEM]...]
    pallas_call x1, Pallas kernels: 10.8 us -> 8.43 us  [on_device(): pl.pallas_call(upper_half, in_specs=[SMEM, VMEM, VMEM, HBM] + [VMEM] * 9,...]
  transfers between devices with their start and end apart: 6 -> 6, of which waited for: 4 -> 4; matrix products, arithmetic and copies ran while one was open for 0% -> 0% of each run, Pallas kernels for 20% -> 15%
where the time goes in v5:
time: 38.4 us; the launch traced here: 38.2 us
  Pallas kernels  15.5 us (40%)
  starting transfers between devices  13.2 us (34%)
  waiting for transfers between devices  8.58 us (22%)
  between operations  0.84 us (2%)
    ppermute x6, starting transfers between devices, send(): return lax.ppermute(value, AXES, pairs)  13.2 us
    ppermute x6, waiting for transfers between devices, send(): return lax.ppermute(value, AXES, pairs)  8.58 us
    pallas_call x1, Pallas kernels, on_device(): pl.pallas_call(upper_half, in_specs=[SMEM, VMEM, VMEM, HBM] + [VMEM] * 9,...  8.43 us
    pallas_call x1, Pallas kernels, on_device(): pl.pallas_call(lower_half, in_specs=[SMEM] + [VMEM] * 5, out_specs=[VMEM]...  5.7 us
    pallas_call x1, Pallas kernels, on_device(): pl.pallas_call(first_pack, in_specs=[HBM] * 3, out_specs=[VMEM] * 3, out_...  1.26 us
  transfers between devices with their start and end apart: 6, of which 4 were waited for; matrix products, arithmetic and copies ran while one was open for 0% of the time, Pallas kernels for 15%

profile of v5, /device:TPU:24, one launch (start us, length us, event | category | flops | bytes accessed | tf_op | source)
XLA Modules:
  0.0 38.2 jit_solution(742340882791994528)
XLA Ops:
  0.6 1.3 %first_pack.1 = (f32[3,32,8,128]{3,2,1,0:T(8,128)S(1)}, f32[16,8,128]{2,1,0:T(8,128)S(1)}, f32[10,8,128]{2,1,0:T(8,128)S(1)}) custom-call(s32[32,8,128]{2,1,0:T(8,128)} %labels.1, f32[2,32,8,128]{3,2,1,0:T(8,128)} %potential.1, s32[16,8,128]{2,1,0:T(8,128)} %codes.1), custom_call_target="tpu_custom_call" | custom-call | tf_op jit(solution)/shard_map/first_pack/pallas_call | solution.py:510
  1.9 0.8 %collective-permute-start = (f32[10,8,128]{2,1,0:T(8,128)S(1)}, f32[10,8,128]{2,1,0:T(8,128)S(1)}, u32[]{:S(2)}, u32[]{:S(2)}) collective-permute-start(f32[10,8,128]{2,1,0:T(8,128)S(1)} %get-tuple-element.15), channel_id=1, source_target_pairs={{0,1},{1,0},{2,3},{3,2},{4,5},{5,4},{6,7},{7,6},{8,9},{9,8},{10,11... | collective-permute-start | bytes 122888 | tf_op jit(solution)/shard_map/ppermute | solution.py:504
  2.7 3.3 %collective-permute-done.across = f32[10,8,128]{2,1,0:T(8,128)S(1)} collective-permute-done((f32[10,8,128]{2,1,0:T(8,128)S(1)}, f32[10,8,128]{2,1,0:T(8,128)S(1)}, u32[]{:S(2)}, u32[]{:S(2)}) %collective-permute-start) | collective-permute-done | bytes 40992 | tf_op jit(solution)/shard_map/ppermute | solution.py:504
  6.0 0.1 second_pack.1
  6.1 6.7 %collective-permute-start.3 = (f32[3,23,8,128]{3,2,1,0:T(8,128)S(1)}, f32[3,23,8,128]{3,2,1,0:T(8,128)S(1)}, u32[]{:S(2)}, u32[]{:S(2)}) collective-permute-start(f32[3,23,8,128]{3,2,1,0:T(8,128)S(1)} %get-tuple-element.18), channel_id=1, source_target_pairs={{8,0},{9,1},{10,2},{11,3},{12,4},{13,5},{14,6},{15,7},{16,8},{17,9... | collective-permute-start | bytes 847880 | tf_op jit(solution)/shard_map/ppermute | solution.py:504
  12.8 2.8 %collective-permute-start.1 = (f32[344,128]{1,0:T(8,128)S(1)}, f32[344,128]{1,0:T(8,128)S(1)}, u32[]{:S(2)}, u32[]{:S(2)}) collective-permute-start(f32[344,128]{1,0:T(8,128)S(1)} %get-tuple-element.16), channel_id=1, source_target_pairs={{0,6},{1,7},{2,0},{3,1},{4,2},{5,3},{6,4},{7,5},{8,14},{9,15},{10,... | collective-permute-start | bytes 528392 | tf_op jit(solution)/shard_map/ppermute | solution.py:504
  15.6 0.0 collective-permute-start.2
  15.6 1.2 %collective-permute-done.3.grow = f32[3,23,8,128]{3,2,1,0:T(8,128)S(1)} collective-permute-done((f32[3,23,8,128]{3,2,1,0:T(8,128)S(1)}, f32[3,23,8,128]{3,2,1,0:T(8,128)S(1)}, u32[]{:S(2)}, u32[]{:S(2)}) %collective-permute-start.3) | collective-permute-done | bytes 282656 | tf_op jit(solution)/shard_map/ppermute | solution.py:504
  16.9 2.8 %collective-permute-start.4 = (f32[312,128]{1,0:T(8,128)S(1)}, f32[312,128]{1,0:T(8,128)S(1)}, u32[]{:S(2)}, u32[]{:S(2)}) collective-permute-start(f32[312,128]{1,0:T(8,128)S(1)} %get-tuple-element.19), channel_id=1, source_target_pairs={{0,6},{1,7},{2,0},{3,1},{4,2},{5,3},{6,4},{7,5},{8,14},{9,15},{10,... | collective-permute-start | bytes 479240 | tf_op jit(solution)/shard_map/ppermute | solution.py:504
  19.8 0.0 collective-permute-start.5
  19.8 0.1 pad_add_fusion.where_ref
  19.8 0.2 collective-permute-done.1.own_lo
  20.0 3.9 %collective-permute-done.2.own_hi = f32[344,128]{1,0:T(8,128)S(1)} collective-permute-done((f32[344,128]{1,0:T(8,128)S(1)}, f32[344,128]{1,0:T(8,128)S(1)}, u32[]{:S(2)}, u32[]{:S(2)}) %collective-permute-start.2) | collective-permute-done | bytes 176160 | tf_op jit(solution)/shard_map/ppermute | solution.py:504
  23.9 5.7 %lower_half.1 = (f32[4,11,8,128]{3,2,1,0:T(8,128)S(1)}, f32[2,11,8,128]{3,2,1,0:T(8,128)S(1)}, f32[4,7,2,16,128]{4,3,2,1,0:T(8,128)S(1)}) custom-call(s32[2]{0:T(128)S(1)} %pad_add_fusion.where_ref, f32[3,32,8,128]{3,2,1,0:T(8,128)S(1)} %get-tuple-element.13.cells, f32[16,8,128]{2,1,0:T(8,128)S(1)} %get-tuple-element.14.codes, ...), custom_call_target="tpu_custom_call" | custom-call | flops 60000000 | bytes 12000000 | tf_op jit(solution)/shard_map/lower_half/pallas_call | solution.py:553
  29.6 0.0 collective-permute-done.4.up_lo
  29.6 0.0 collective-permute-done.5.up_hi
  29.6 8.4 %upper_half.1 = (f32[4,32,8,128]{3,2,1,0:T(8,128)}, f32[2,32,8,128]{3,2,1,0:T(8,128)}) custom-call(s32[2]{0:T(128)S(1)} %pad_add_fusion.where_ref, f32[3,32,8,128]{3,2,1,0:T(8,128)S(1)} %get-tuple-element.13.cells, f32[16,8,128]{2,1,0:T(8,128)S(1)} %get-tuple-element.14.codes, f32[2,8]{1,0:T(2,128)} %table_in.1, ...), custom_call_target="tpu_custom_call" | custom-call | tf_op jit(solution)/shard_map/upper_half/pallas_call | solution.py:566
  (1 shorter events, 0.0 us)
Async XLA Ops:
  1.9 4.1 %collective-permute-start = (f32[10,8,128]{2,1,0:T(8,128)S(1)}, f32[10,8,128]{2,1,0:T(8,128)S(1)}, u32[]{:S(2)}, u32[]{:S(2)}) collective-permute-start(f32[10,8,128]{2,1,0:T(8,128)S(1)} %get-tuple-element.15), channel_id=1, source_target_pairs={{0,1},{1,0},{2,3},{3,2},{4,5},{5,4},{6,7},{7,6},{8,9},{9,8},{10,11... | collective-permute-start | bytes 122888 | tf_op jit(solution)/shard_map/ppermute | solution.py:504
  6.1 10.8 %collective-permute-start.3 = (f32[3,23,8,128]{3,2,1,0:T(8,128)S(1)}, f32[3,23,8,128]{3,2,1,0:T(8,128)S(1)}, u32[]{:S(2)}, u32[]{:S(2)}) collective-permute-start(f32[3,23,8,128]{3,2,1,0:T(8,128)S(1)} %get-tuple-element.18), channel_id=1, source_target_pairs={{8,0},{9,1},{10,2},{11,3},{12,4},{13,5},{14,6},{15,7},{16,8},{17,9... | collective-permute-start | bytes 847880 | tf_op jit(solution)/shard_map/ppermute | solution.py:504
  12.8 7.2 %collective-permute-start.1 = (f32[344,128]{1,0:T(8,128)S(1)}, f32[344,128]{1,0:T(8,128)S(1)}, u32[]{:S(2)}, u32[]{:S(2)}) collective-permute-start(f32[344,128]{1,0:T(8,128)S(1)} %get-tuple-element.16), channel_id=1, source_target_pairs={{0,6},{1,7},{2,0},{3,1},{4,2},{5,3},{6,4},{7,5},{8,14},{9,15},{10,... | collective-permute-start | bytes 528392 | tf_op jit(solution)/shard_map/ppermute | solution.py:504
  15.6 8.3 %collective-permute-start.2 = (f32[344,128]{1,0:T(8,128)S(1)}, f32[344,128]{1,0:T(8,128)S(1)}, u32[]{:S(2)}, u32[]{:S(2)}) collective-permute-start(f32[344,128]{1,0:T(8,128)S(1)} %get-tuple-element.17), channel_id=1, source_target_pairs={{0,2},{1,3},{2,4},{3,5},{4,6},{5,7},{6,0},{7,1},{8,10},{9,11},{10,... | collective-permute-start | bytes 528392 | tf_op jit(solution)/shard_map/ppermute | solution.py:504
  16.9 12.7 %collective-permute-start.4 = (f32[312,128]{1,0:T(8,128)S(1)}, f32[312,128]{1,0:T(8,128)S(1)}, u32[]{:S(2)}, u32[]{:S(2)}) collective-permute-start(f32[312,128]{1,0:T(8,128)S(1)} %get-tuple-element.19), channel_id=1, source_target_pairs={{0,6},{1,7},{2,0},{3,1},{4,2},{5,3},{6,4},{7,5},{8,14},{9,15},{10,... | collective-permute-start | bytes 479240 | tf_op jit(solution)/shard_map/ppermute | solution.py:504
  19.8 9.9 %collective-permute-start.5 = (f32[312,128]{1,0:T(8,128)S(1)}, f32[312,128]{1,0:T(8,128)S(1)}, u32[]{:S(2)}, u32[]{:S(2)}) collective-permute-start(f32[312,128]{1,0:T(8,128)S(1)} %get-tuple-element.20), channel_id=1, source_target_pairs={{0,2},{1,3},{2,4},{3,5},{4,6},{5,7},{6,0},{7,1},{8,10},{9,11},{10,... | collective-permute-start | bytes 479240 | tf_op jit(solution)/shard_map/ppermute | solution.py:504

commit v6 on v5

--- a/solution.py
+++ b/solution.py
@@ -21,6 +21,7 @@
 PACK = 11
 AXES = ("grow", "gy", "gz")
 VMEM = pl.BlockSpec(memory_space=pltpu.VMEM)
+ANY = pl.BlockSpec(memory_space=pl.ANY)
 HBM = pl.BlockSpec(memory_space=pltpu.MemorySpace.HBM)
 SMEM = pl.BlockSpec(memory_space=pltpu.SMEM)
 
@@ -42,17 +43,13 @@
         for q in range(2):
             places["edge", f, q] = (at, DEEP)
             at += DEEP
-    if not up:
-        for e in range(SHIFT):
-            places["code", 0, e] = (at, 2)
-            at += 2
-        places["code_edge", 0, 0] = (at, 2)
-        at += 2
     return places, -(-at // 8) * 8
 
 
 OWN_PLAN, OWN_ROWS = plan(False)
 UP_PLAN, UP_ROWS = plan(True)
+CODE_PLAN = {("code", 0, e): (8 + 2 * e, 2) for e in range(SHIFT)}
+CODE_PLAN["code_edge", 0, 0] = (8 + 2 * SHIFT, 2)
 
 
 def first_pack(labels, potential, codes, cells, codes_out, edges, labels_in, codes_in, sems):
@@ -93,35 +90,50 @@
         hi[at : at + count] = tile[8 - count : 8]
 
 
-def second_pack(cells, codes, across, own_lo, own_hi, grow):
+def second_pack(cells, across, own_lo, own_hi):
     for f in range(3):
         for i in range(OWN):
             put(own_lo, own_hi, OWN_PLAN["cell", f, i], cells[f, i + 11])
-            grow[f, i] = cells[f, i]
         for q in range(2):
             put(own_lo, own_hi, OWN_PLAN["edge", f, q], across[3 * f + q + 1])
-            grow[f, OWN + q] = across[3 * f + q]
-    for e in range(SHIFT):
-        put(own_lo, own_hi, OWN_PLAN["code", 0, e], codes[e])
-    put(own_lo, own_hi, OWN_PLAN["code_edge", 0, 0], across[9])
     for ref in (own_lo, own_hi):
         blank(ref, OWN_PLAN, OWN_ROWS)
+
+
+def grow_pack(cells, across, after_lo, after_hi, grow):
+    del after_lo, after_hi
+    for f in range(3):
+        grow[f, 0:OWN] = cells[f, 0:OWN]
+        grow[f, OWN : OWN + 2] = across[3 * f : 3 * f + 2]
 
 
 def blank(ref, places, rows):
     used = max(at + count for at, count in places.values())
     ref[0:8] = jnp.zeros((8, 128), jnp.float32)
-    ref[used:rows] = jnp.zeros((rows - used, 128), jnp.float32)
-
-
-def third_pack(grow, up_lo, up_hi):
-    for f in range(3):
-        for i in range(OWN):
-            put(up_lo, up_hi, UP_PLAN["cell", f, i], grow[f, i])
-        for q in range(2):
-            put(up_lo, up_hi, UP_PLAN["edge", f, q], grow[f, OWN + q])
+    if used < rows:
+        ref[used:rows] = jnp.zeros((rows - used, 128), jnp.float32)
+
+
+def third_pack(where_ref, grow, codes, across, up_lo, up_hi):
+    last = where_ref[0] == where_ref[1] - 1
     for ref in (up_lo, up_hi):
         blank(ref, UP_PLAN, UP_ROWS)
+
+    @pl.when(jnp.logical_not(last))
+    def _():
+        for f in range(3):
+            for i in range(OWN):
+                put(up_lo, up_hi, UP_PLAN["cell", f, i], grow[f, i])
+            for q in range(2):
+                put(up_lo, up_hi, UP_PLAN["edge", f, q], grow[f, OWN + q])
+
+    @pl.when(last)
+    def _():
+        for ref in (up_lo, up_hi):
+            ref[...] = jnp.zeros((UP_ROWS, 128), jnp.float32)
+        for e in range(SHIFT):
+            put(up_lo, up_hi, CODE_PLAN["code", 0, e], codes[e])
+        put(up_lo, up_hi, CODE_PLAN["code_edge", 0, 0], across[9])
 
 
 def react(phases, sums, chem, chem_sums, held):
@@ -247,9 +259,9 @@
         def rows(block, e):
             if block == 0:
                 return self.codes[e], self.across[9]
-            ref = self.own[block - 1]
-            at, _ = OWN_PLAN["code", 0, e]
-            edge, _ = OWN_PLAN["code_edge", 0, 0]
+            ref = self.up[block - 1]
+            at, _ = CODE_PLAN["code", 0, e]
+            edge, _ = CODE_PLAN["code_edge", 0, 0]
             return ref[at : at + 2], ref[edge : edge + 2]
 
         for e in range(SHIFT):
@@ -393,11 +405,24 @@
 
 
 def lower_half(
-    where_ref, cells, codes, across, own_lo, own_hi, phases, chems, seam,
+    where_ref, cells, across, own_lo, own_hi, middle_lo, middle_hi,
+    phases, chems, seam, rows_lo, rows_hi,
     one, two, strip_one, strip_two, wing,
 ):
     first = where_ref[0] == 0
-    half = Half(0, 0, 4, cells, codes, across, (own_lo, own_hi), None, None, wing)
+    middle = where_ref[0] == where_ref[1] // 2
+
+    @pl.when(middle)
+    def _():
+        rows_lo[...] = middle_lo[...]
+        rows_hi[...] = middle_hi[...]
+
+    @pl.when(jnp.logical_not(middle))
+    def _():
+        rows_lo[...] = own_lo[...]
+        rows_hi[...] = own_hi[...]
+
+    half = Half(0, 0, 4, cells, None, across, (rows_lo, rows_hi), None, None, wing)
     for p in range(OWN):
         half.fill(one, p)
     half.fill_strips(strip_one, OWN)
@@ -494,9 +519,9 @@
     n_grow, n_gy, n_gz = (lax.axis_size(a) for a in AXES)
     where = jnp.stack([lax.axis_index("grow"), n_grow]).astype(jnp.int32)
 
-    def send(value, dg, dy, dz):
+    def send(value, dg, dy, dz, planes=None):
         pairs = []
-        for g in range(max(0, -dg), n_grow):
+        for g in planes or range(max(0, -dg), n_grow):
             for y in range(n_gy):
                 for z in range(n_gz):
                     to = ((g + dg) * n_gy + (y + dy) % n_gy) * n_gz + (z + dz) % n_gz
@@ -521,25 +546,37 @@
         name="first_pack",
     )(*(pltpu.with_memory_space_constraint(x, pltpu.MemorySpace.HBM) for x in (labels, potential, melt_codes)))
     across = send(edges, 0, 0, 1)
-    own_lo, own_hi, grow = pl.pallas_call(
+    own_lo, own_hi = pl.pallas_call(
         second_pack,
-        in_specs=[VMEM] * 3,
-        out_specs=[VMEM] * 3,
-        out_shape=[f32(OWN_ROWS, 128)] * 2 + [f32(3, OWN + 2, 8, 128)],
+        in_specs=[VMEM] * 2,
+        out_specs=[VMEM] * 2,
+        out_shape=[f32(OWN_ROWS, 128)] * 2,
         compiler_params=params,
         name="second_pack",
-    )(cells, codes, across)
-    own_lo = send(own_lo, 0, -1, 0)
-    own_hi = send(own_hi, 0, 1, 0)
+    )(cells, across)
+    middle = n_grow // 2
+    others = [g for g in range(n_grow) if g != middle]
+    middle_lo = send(own_lo, 0, -1, 0, [middle])
+    middle_hi = send(own_hi, 0, 1, 0, [middle])
+    own_lo = send(own_lo, 0, -1, 0, others)
+    own_hi = send(own_hi, 0, 1, 0, others)
+    grow = pl.pallas_call(
+        grow_pack,
+        in_specs=[VMEM, VMEM, ANY, ANY],
+        out_specs=VMEM,
+        out_shape=f32(3, OWN + 2, 8, 128),
+        compiler_params=params,
+        name="grow_pack",
+    )(cells, across, middle_lo, middle_hi)
     grow = send(grow, -1, 0, 0)
     up_lo, up_hi = pl.pallas_call(
         third_pack,
-        in_specs=[VMEM],
+        in_specs=[SMEM] + [VMEM] * 3,
         out_specs=[VMEM] * 2,
         out_shape=[f32(UP_ROWS, 128)] * 2,
         compiler_params=params,
         name="third_pack",
-    )(grow)
+    )(where, grow, codes, across)
     up_lo = send(up_lo, 0, -1, 0)
     up_hi = send(up_hi, 0, 1, 0)
 
@@ -550,18 +587,19 @@
             + [pltpu.VMEM((5, strips, PITCH, 128), jnp.float32)]
         )
 
-    phases, chems, seam = pl.pallas_call(
+    phases, chems, seam, own_lo, own_hi = pl.pallas_call(
         lower_half,
-        in_specs=[SMEM] + [VMEM] * 5,
-        out_specs=[VMEM] * 3,
-        out_shape=[f32(4, LOWER, 8, 128), f32(2, LOWER, 8, 128), f32(4, 7, 2, 16, 128)],
+        in_specs=[SMEM] + [VMEM] * 6,
+        out_specs=[VMEM] * 5,
+        out_shape=[f32(4, LOWER, 8, 128), f32(2, LOWER, 8, 128), f32(4, 7, 2, 16, 128)]
+        + [f32(OWN_ROWS, 128)] * 2,
         scratch_shapes=buffers(OWN, 4),
         compiler_params=params,
         cost_estimate=pl.CostEstimate(
             flops=60_000_000, bytes_accessed=12_000_000, transcendentals=0
         ),
         name="lower_half",
-    )(where, cells, codes, across, own_lo, own_hi)
+    )(where, cells, across, own_lo, own_hi, middle_lo, middle_hi)
     table = pltpu.with_memory_space_constraint(melt_table, pltpu.MemorySpace.HBM)
     return pl.pallas_call(
         upper_half,

time: 38.4 us -> 45.6 us (1.19)
  the two profiles are of different devices: /device:TPU:24 before, /device:TPU:17 now
where the time goes in v6:
time: 45.6 us; the launch traced here: 45.4 us
  starting transfers between devices  24.7 us (54%)
  Pallas kernels  15.9 us (35%)
  waiting for transfers between devices  3.95 us (9%)
  between operations  0.74 us (2%)
    ppermute x8, starting transfers between devices, send(): return lax.ppermute(value, AXES, pairs)  24.7 us
    pallas_call x1, Pallas kernels, on_device(): pl.pallas_call(upper_half, in_specs=[SMEM, VMEM, VMEM, HBM] + [VMEM] * 9,...  8.27 us
    pallas_call x1, Pallas kernels, on_device(): pl.pallas_call(lower_half, in_specs=[SMEM] + [VMEM] * 6, out_specs=[VMEM]...  5.74 us
    ppermute x8, waiting for transfers between devices, send(): return lax.ppermute(value, AXES, pairs)  3.95 us
    pallas_call x1, Pallas kernels, on_device(): pl.pallas_call(first_pack, in_specs=[HBM] * 3, out_specs=[VMEM] * 3, out_...  1.26 us
  transfers between devices with their start and end apart: 8, of which 2 were waited for; matrix products, arithmetic and copies ran while one was open for 0% of the time, Pallas kernels for 14%

profile of v6, /device:TPU:17, one launch (start us, length us, event | category | flops | bytes accessed | tf_op | source)
XLA Modules:
  0.0 45.4 jit_solution(17705875802597467764)
XLA Ops:
  0.6 1.3 %first_pack.1 = (f32[3,32,8,128]{3,2,1,0:T(8,128)S(1)}, f32[16,8,128]{2,1,0:T(8,128)S(1)}, f32[10,8,128]{2,1,0:T(8,128)S(1)}) custom-call(s32[32,8,128]{2,1,0:T(8,128)} %labels.1, f32[2,32,8,128]{3,2,1,0:T(8,128)} %potential.1, s32[16,8,128]{2,1,0:T(8,128)} %codes.1), custom_call_target="tpu_custom_call" | custom-call | tf_op jit(solution)/shard_map/first_pack/pallas_call | solution.py:535
  1.9 1.1 %collective-permute-start = (f32[10,8,128]{2,1,0:T(8,128)S(1)}, f32[10,8,128]{2,1,0:T(8,128)S(1)}, u32[]{:S(2)}, u32[]{:S(2)}) collective-permute-start(f32[10,8,128]{2,1,0:T(8,128)S(1)} %get-tuple-element.16), channel_id=1, source_target_pairs={{0,1},{1,0},{2,3},{3,2},{4,5},{5,4},{6,7},{7,6},{8,9},{9,8},{10,11... | collective-permute-start | bytes 122888 | tf_op jit(solution)/shard_map/ppermute | solution.py:529
  3.0 1.8 %collective-permute-done.across = f32[10,8,128]{2,1,0:T(8,128)S(1)} collective-permute-done((f32[10,8,128]{2,1,0:T(8,128)S(1)}, f32[10,8,128]{2,1,0:T(8,128)S(1)}, u32[]{:S(2)}, u32[]{:S(2)}) %collective-permute-start) | collective-permute-done | bytes 40992 | tf_op jit(solution)/shard_map/ppermute | solution.py:529
  4.9 0.7 %collective-permute-start.3 = (f32[312,128]{1,0:T(8,128)S(1)}, f32[312,128]{1,0:T(8,128)S(1)}, u32[]{:S(2)}, u32[]{:S(2)}) collective-permute-start(f32[312,128]{1,0:T(8,128)S(1)} %get-tuple-element.17), channel_id=1, source_target_pairs={{128,134},{129,135},{130,128},{131,129},{132,130},{133,131},{134,1... | collective-permute-start | bytes 479240 | tf_op jit(solution)/shard_map/ppermute | solution.py:529
  5.6 0.7 %collective-permute-start.4 = (f32[312,128]{1,0:T(8,128)S(1)}, f32[312,128]{1,0:T(8,128)S(1)}, u32[]{:S(2)}, u32[]{:S(2)}) collective-permute-start(f32[312,128]{1,0:T(8,128)S(1)} %get-tuple-element.18), channel_id=1, source_target_pairs={{128,130},{129,131},{130,132},{131,133},{132,134},{133,135},{134,1... | collective-permute-start | bytes 479240 | tf_op jit(solution)/shard_map/ppermute | solution.py:529
  6.2 0.0 collective-permute-done.3.middle_lo.after_lo
  6.3 0.0 collective-permute-done.4.middle_hi.after_hi
  6.3 15.4 %collective-permute-start.5 = (f32[3,23,8,128]{3,2,1,0:T(8,128)S(1)}, f32[3,23,8,128]{3,2,1,0:T(8,128)S(1)}, u32[]{:S(2)}, u32[]{:S(2)}) collective-permute-start(f32[3,23,8,128]{3,2,1,0:T(8,128)S(1)} %grow_pack.1), channel_id=1, source_target_pairs={{8,0},{9,1},{10,2},{11,3},{12,4},{13,5},{14,6},{15,7},{16,8},{17,9... | collective-permute-start | bytes 847880 | tf_op jit(solution)/shard_map/ppermute | solution.py:529
  21.7 1.9 %collective-permute-start.1 = (f32[312,128]{1,0:T(8,128)S(1)}, f32[312,128]{1,0:T(8,128)S(1)}, u32[]{:S(2)}, u32[]{:S(2)}) collective-permute-start(f32[312,128]{1,0:T(8,128)S(1)} %get-tuple-element.17), channel_id=1, source_target_pairs={{0,6},{1,7},{2,0},{3,1},{4,2},{5,3},{6,4},{7,5},{8,14},{9,15},{10,... | collective-permute-start | bytes 479240 | tf_op jit(solution)/shard_map/ppermute | solution.py:529
  23.6 3.4 %collective-permute-start.2 = (f32[312,128]{1,0:T(8,128)S(1)}, f32[312,128]{1,0:T(8,128)S(1)}, u32[]{:S(2)}, u32[]{:S(2)}) collective-permute-start(f32[312,128]{1,0:T(8,128)S(1)} %get-tuple-element.18), channel_id=1, source_target_pairs={{0,2},{1,3},{2,4},{3,5},{4,6},{5,7},{6,0},{7,1},{8,10},{9,11},{10,... | collective-permute-start | bytes 479240 | tf_op jit(solution)/shard_map/ppermute | solution.py:529
  27.0 0.1 pad_add_fusion.where_ref
  27.1 0.0 collective-permute-done.5.grow
  27.1 0.6 %third_pack.1 = (f32[312,128]{1,0:T(8,128)S(1)}, f32[312,128]{1,0:T(8,128)S(1)}) custom-call(s32[2]{0:T(128)S(1)} %pad_add_fusion.where_ref, f32[3,23,8,128]{3,2,1,0:T(8,128)S(1)} %collective-permute-done.5.grow, f32[16,8,128]{2,1,0:T(8,128)S(1)} %get-tuple-element.15.codes, f32[10,8,128]{2,1,0:T(8,128)S(1)} %collective-permute-done.across), custom_call_target="tpu_custom_call" | custom-call | tf_op jit(solution)/shard_map/third_pack/pallas_call | solution.py:572
  27.7 1.3 %collective-permute-start.6 = (f32[312,128]{1,0:T(8,128)S(1)}, f32[312,128]{1,0:T(8,128)S(1)}, u32[]{:S(2)}, u32[]{:S(2)}) collective-permute-start(f32[312,128]{1,0:T(8,128)S(1)} %get-tuple-element.21), channel_id=1, source_target_pairs={{0,6},{1,7},{2,0},{3,1},{4,2},{5,3},{6,4},{7,5},{8,14},{9,15},{10,... | collective-permute-start | bytes 479240 | tf_op jit(solution)/shard_map/ppermute | solution.py:529
  29.0 0.2 collective-permute-start.7
  29.2 0.0 collective-permute-done.1.own_lo
  29.2 2.1 %collective-permute-done.2.own_hi = f32[312,128]{1,0:T(8,128)S(1)} collective-permute-done((f32[312,128]{1,0:T(8,128)S(1)}, f32[312,128]{1,0:T(8,128)S(1)}, u32[]{:S(2)}, u32[]{:S(2)}) %collective-permute-start.2) | collective-permute-done | bytes 159776 | tf_op jit(solution)/shard_map/ppermute | solution.py:529
  31.3 5.7 %lower_half.1 = (f32[4,11,8,128]{3,2,1,0:T(8,128)S(1)}, f32[2,11,8,128]{3,2,1,0:T(8,128)S(1)}, f32[4,7,2,16,128]{4,3,2,1,0:T(8,128)S(1)}, f32[312,128]{1,0:T(8,128)S(1)}, f32[312,128]{1,0:T(8,128)S(1)}) custom-call(s32[2]{0:T(128)S(1)} %pad_add_fusion.where_ref, f32[3,32,8,128]{3,2,1,0:T(8,128)S(1)} %get-tuple-element.14.cells, ...), custom_call_target="tpu_custom_call" | custom-call | flops 60000000 | bytes 12000000 | tf_op jit(solution)/shard_map/lower_half/pallas_call | solution.py:590
  37.1 0.0 collective-permute-done.6.up_lo
  37.1 0.0 collective-permute-done.7.up_hi
  37.1 8.3 %upper_half.1 = (f32[4,32,8,128]{3,2,1,0:T(8,128)}, f32[2,32,8,128]{3,2,1,0:T(8,128)}) custom-call(s32[2]{0:T(128)S(1)} %pad_add_fusion.where_ref, f32[3,32,8,128]{3,2,1,0:T(8,128)S(1)} %get-tuple-element.14.cells, f32[16,8,128]{2,1,0:T(8,128)S(1)} %get-tuple-element.15.codes, f32[2,8]{1,0:T(2,128)} %table_in.1, ...), custom_call_target="tpu_custom_call" | custom-call | tf_op jit(solution)/shard_map/upper_half/pallas_call | solution.py:604
  (2 shorter events, 0.1 us)
Async XLA Ops:
  1.9 2.9 %collective-permute-start = (f32[10,8,128]{2,1,0:T(8,128)S(1)}, f32[10,8,128]{2,1,0:T(8,128)S(1)}, u32[]{:S(2)}, u32[]{:S(2)}) collective-permute-start(f32[10,8,128]{2,1,0:T(8,128)S(1)} %get-tuple-element.16), channel_id=1, source_target_pairs={{0,1},{1,0},{2,3},{3,2},{4,5},{5,4},{6,7},{7,6},{8,9},{9,8},{10,11... | collective-permute-start | bytes 122888 | tf_op jit(solution)/shard_map/ppermute | solution.py:529
  4.9 1.4 %collective-permute-start.3 = (f32[312,128]{1,0:T(8,128)S(1)}, f32[312,128]{1,0:T(8,128)S(1)}, u32[]{:S(2)}, u32[]{:S(2)}) collective-permute-start(f32[312,128]{1,0:T(8,128)S(1)} %get-tuple-element.17), channel_id=1, source_target_pairs={{128,134},{129,135},{130,128},{131,129},{132,130},{133,131},{134,1... | collective-permute-start | bytes 479240 | tf_op jit(solution)/shard_map/ppermute | solution.py:529
  5.6 0.7 %collective-permute-start.4 = (f32[312,128]{1,0:T(8,128)S(1)}, f32[312,128]{1,0:T(8,128)S(1)}, u32[]{:S(2)}, u32[]{:S(2)}) collective-permute-start(f32[312,128]{1,0:T(8,128)S(1)} %get-tuple-element.18), channel_id=1, source_target_pairs={{128,130},{129,131},{130,132},{131,133},{132,134},{133,135},{134,1... | collective-permute-start | bytes 479240 | tf_op jit(solution)/shard_map/ppermute | solution.py:529
  6.3 20.8 %collective-permute-start.5 = (f32[3,23,8,128]{3,2,1,0:T(8,128)S(1)}, f32[3,23,8,128]{3,2,1,0:T(8,128)S(1)}, u32[]{:S(2)}, u32[]{:S(2)}) collective-permute-start(f32[3,23,8,128]{3,2,1,0:T(8,128)S(1)} %grow_pack.1), channel_id=1, source_target_pairs={{8,0},{9,1},{10,2},{11,3},{12,4},{13,5},{14,6},{15,7},{16,8},{17,9... | collective-permute-start | bytes 847880 | tf_op jit(solution)/shard_map/ppermute | solution.py:529
  21.7 7.5 %collective-permute-start.1 = (f32[312,128]{1,0:T(8,128)S(1)}, f32[312,128]{1,0:T(8,128)S(1)}, u32[]{:S(2)}, u32[]{:S(2)}) collective-permute-start(f32[312,128]{1,0:T(8,128)S(1)} %get-tuple-element.17), channel_id=1, source_target_pairs={{0,6},{1,7},{2,0},{3,1},{4,2},{5,3},{6,4},{7,5},{8,14},{9,15},{10,... | collective-permute-start | bytes 479240 | tf_op jit(solution)/shard_map/ppermute | solution.py:529
  23.6 7.7 %collective-permute-start.2 = (f32[312,128]{1,0:T(8,128)S(1)}, f32[312,128]{1,0:T(8,128)S(1)}, u32[]{:S(2)}, u32[]{:S(2)}) collective-permute-start(f32[312,128]{1,0:T(8,128)S(1)} %get-tuple-element.18), channel_id=1, source_target_pairs={{0,2},{1,3},{2,4},{3,5},{4,6},{5,7},{6,0},{7,1},{8,10},{9,11},{10,... | collective-permute-start | bytes 479240 | tf_op jit(solution)/shard_map/ppermute | solution.py:529
  27.7 9.4 %collective-permute-start.6 = (f32[312,128]{1,0:T(8,128)S(1)}, f32[312,128]{1,0:T(8,128)S(1)}, u32[]{:S(2)}, u32[]{:S(2)}) collective-permute-start(f32[312,128]{1,0:T(8,128)S(1)} %get-tuple-element.21), channel_id=1, source_target_pairs={{0,6},{1,7},{2,0},{3,1},{4,2},{5,3},{6,4},{7,5},{8,14},{9,15},{10,... | collective-permute-start | bytes 479240 | tf_op jit(solution)/shard_map/ppermute | solution.py:529
  29.0 8.1 %collective-permute-start.7 = (f32[312,128]{1,0:T(8,128)S(1)}, f32[312,128]{1,0:T(8,128)S(1)}, u32[]{:S(2)}, u32[]{:S(2)}) collective-permute-start(f32[312,128]{1,0:T(8,128)S(1)} %get-tuple-element.22), channel_id=1, source_target_pairs={{0,2},{1,3},{2,4},{3,5},{4,6},{5,7},{6,0},{7,1},{8,10},{9,11},{10,... | collective-permute-start | bytes 479240 | tf_op jit(solution)/shard_map/ppermute | solution.py:529

commit v7 on v6

--- a/solution.py
+++ b/solution.py
@@ -21,9 +21,7 @@
 PACK = 11
 AXES = ("grow", "gy", "gz")
 VMEM = pl.BlockSpec(memory_space=pltpu.VMEM)
-ANY = pl.BlockSpec(memory_space=pl.ANY)
 HBM = pl.BlockSpec(memory_space=pltpu.MemorySpace.HBM)
-SMEM = pl.BlockSpec(memory_space=pltpu.SMEM)
 
 
 def lanes():
@@ -90,7 +88,20 @@
         hi[at : at + count] = tile[8 - count : 8]
 
 
-def second_pack(cells, across, own_lo, own_hi):
+def by_parity(body):
+    even = lax.rem(lax.axis_index("gy"), 2) == 0
+    pl.when(even)(lambda: body(True))
+    pl.when(jnp.logical_not(even))(lambda: body(False))
+
+
+def second_pack(cells, across, one, two, grow):
+    by_parity(lambda even: own_rows(cells, across, *((one, two) if even else (two, one))))
+    for f in range(3):
+        grow[f, 0:OWN] = cells[f, 0:OWN]
+        grow[f, OWN : OWN + 2] = across[3 * f : 3 * f + 2]
+
+
+def own_rows(cells, across, own_lo, own_hi):
     for f in range(3):
         for i in range(OWN):
             put(own_lo, own_hi, OWN_PLAN["cell", f, i], cells[f, i + 11])
@@ -100,13 +111,6 @@
         blank(ref, OWN_PLAN, OWN_ROWS)
 
 
-def grow_pack(cells, across, after_lo, after_hi, grow):
-    del after_lo, after_hi
-    for f in range(3):
-        grow[f, 0:OWN] = cells[f, 0:OWN]
-        grow[f, OWN : OWN + 2] = across[3 * f : 3 * f + 2]
-
-
 def blank(ref, places, rows):
     used = max(at + count for at, count in places.values())
     ref[0:8] = jnp.zeros((8, 128), jnp.float32)
@@ -114,8 +118,17 @@
         ref[used:rows] = jnp.zeros((rows - used, 128), jnp.float32)
 
 
-def third_pack(where_ref, grow, codes, across, up_lo, up_hi):
-    last = where_ref[0] == where_ref[1] - 1
+def third_pack(grow, codes, across, one, two):
+    by_parity(lambda even: up_rows(grow, codes, across, *((one, two) if even else (two, one))))
+
+
+def place():
+    index = lax.axis_index("grow")
+    return index == 0, index == lax.axis_size("grow") - 1
+
+
+def up_rows(grow, codes, across, up_lo, up_hi):
+    _, last = place()
     for ref in (up_lo, up_hi):
         blank(ref, UP_PLAN, UP_ROWS)
 
@@ -405,23 +418,17 @@
 
 
 def lower_half(
-    where_ref, cells, across, own_lo, own_hi, middle_lo, middle_hi,
+    cells, across, swap_one, swap_two,
     phases, chems, seam, rows_lo, rows_hi,
     one, two, strip_one, strip_two, wing,
 ):
-    first = where_ref[0] == 0
-    middle = where_ref[0] == where_ref[1] // 2
-
-    @pl.when(middle)
-    def _():
-        rows_lo[...] = middle_lo[...]
-        rows_hi[...] = middle_hi[...]
-
-    @pl.when(jnp.logical_not(middle))
-    def _():
-        rows_lo[...] = own_lo[...]
-        rows_hi[...] = own_hi[...]
-
+    first, _ = place()
+
+    def sort_rows(even):
+        rows_lo[...] = (swap_two if even else swap_one)[...]
+        rows_hi[...] = (swap_one if even else swap_two)[...]
+
+    by_parity(sort_rows)
     half = Half(0, 0, 4, cells, None, across, (rows_lo, rows_hi), None, None, wing)
     for p in range(OWN):
         half.fill(one, p)
@@ -461,13 +468,19 @@
 
 
 def upper_half(
-    where_ref, cells, codes, table_in, across, own_lo, own_hi, up_lo, up_hi, grow, seam,
+    cells, codes, table_in, across, own_lo, own_hi, swap_one, swap_two, grow, seam,
     lower_phases, lower_chems, phases_out, chem_out,
-    one, two, strip_one, strip_two, wing, phases, chems, table, sem, sems,
+    one, two, strip_one, strip_two, wing, phases, chems, up_lo, up_hi, table, sem, sems,
 ):
     outs = (phases_out, chem_out)
     copies = delivery(lower_phases, lower_chems, *outs, 0, 0, LOWER, sems, 0)
-    last = where_ref[0] == where_ref[1] - 1
+    _, last = place()
+
+    def sort_rows(even):
+        up_lo[...] = (swap_two if even else swap_one)[...]
+        up_hi[...] = (swap_one if even else swap_two)[...]
+
+    by_parity(sort_rows)
     half = Half(
         15, 12, 5, cells, codes, across, (own_lo, own_hi), (up_lo, up_hi), grow, wing
     )
@@ -517,11 +530,10 @@
 
 def on_device(labels, potential, melt_codes, melt_table):
     n_grow, n_gy, n_gz = (lax.axis_size(a) for a in AXES)
-    where = jnp.stack([lax.axis_index("grow"), n_grow]).astype(jnp.int32)
-
-    def send(value, dg, dy, dz, planes=None):
+
+    def send(value, dg, dy, dz):
         pairs = []
-        for g in planes or range(max(0, -dg), n_grow):
+        for g in range(max(0, -dg), n_grow):
             for y in range(n_gy):
                 for z in range(n_gz):
                     to = ((g + dg) * n_gy + (y + dy) % n_gy) * n_gz + (z + dz) % n_gz
@@ -546,39 +558,31 @@
         name="first_pack",
     )(*(pltpu.with_memory_space_constraint(x, pltpu.MemorySpace.HBM) for x in (labels, potential, melt_codes)))
     across = send(edges, 0, 0, 1)
-    own_lo, own_hi = pl.pallas_call(
+    own_one, own_two, grow = pl.pallas_call(
         second_pack,
         in_specs=[VMEM] * 2,
-        out_specs=[VMEM] * 2,
-        out_shape=[f32(OWN_ROWS, 128)] * 2,
+        out_specs=[VMEM] * 3,
+        out_shape=[f32(OWN_ROWS, 128)] * 2 + [f32(3, OWN + 2, 8, 128)],
         compiler_params=params,
         name="second_pack",
     )(cells, across)
-    middle = n_grow // 2
-    others = [g for g in range(n_grow) if g != middle]
-    middle_lo = send(own_lo, 0, -1, 0, [middle])
-    middle_hi = send(own_hi, 0, 1, 0, [middle])
-    own_lo = send(own_lo, 0, -1, 0, others)
-    own_hi = send(own_hi, 0, 1, 0, others)
-    grow = pl.pallas_call(
-        grow_pack,
-        in_specs=[VMEM, VMEM, ANY, ANY],
-        out_specs=VMEM,
-        out_shape=f32(3, OWN + 2, 8, 128),
-        compiler_params=params,
-        name="grow_pack",
-    )(cells, across, middle_lo, middle_hi)
+
+    def swap(one, two):
+        below = [(y, (y + (1 if y % 2 else -1)) % n_gy) for y in range(n_gy)]
+        above = [(y, (y + (-1 if y % 2 else 1)) % n_gy) for y in range(n_gy)]
+        return lax.ppermute(one, "gy", below), lax.ppermute(two, "gy", above)
+
+    own_one, own_two = swap(own_one, own_two)
     grow = send(grow, -1, 0, 0)
-    up_lo, up_hi = pl.pallas_call(
+    up_one, up_two = pl.pallas_call(
         third_pack,
-        in_specs=[SMEM] + [VMEM] * 3,
+        in_specs=[VMEM] * 3,
         out_specs=[VMEM] * 2,
         out_shape=[f32(UP_ROWS, 128)] * 2,
         compiler_params=params,
         name="third_pack",
-    )(where, grow, codes, across)
-    up_lo = send(up_lo, 0, -1, 0)
-    up_hi = send(up_hi, 0, 1, 0)
+    )(grow, codes, across)
+    up_one, up_two = swap(up_one, up_two)
 
     def buffers(planes, strips):
         return (
@@ -589,7 +593,7 @@
 
     phases, chems, seam, own_lo, own_hi = pl.pallas_call(
         lower_half,
-        in_specs=[SMEM] + [VMEM] * 6,
+        in_specs=[VMEM] * 4,
         out_specs=[VMEM] * 5,
         out_shape=[f32(4, LOWER, 8, 128), f32(2, LOWER, 8, 128), f32(4, 7, 2, 16, 128)]
         + [f32(OWN_ROWS, 128)] * 2,
@@ -599,24 +603,26 @@
             flops=60_000_000, bytes_accessed=12_000_000, transcendentals=0
         ),
         name="lower_half",
-    )(where, cells, across, own_lo, own_hi, middle_lo, middle_hi)
+    )(cells, across, own_one, own_two)
     table = pltpu.with_memory_space_constraint(melt_table, pltpu.MemorySpace.HBM)
     return pl.pallas_call(
         upper_half,
-        in_specs=[SMEM, VMEM, VMEM, HBM] + [VMEM] * 9,
+        in_specs=[VMEM, VMEM, HBM] + [VMEM] * 9,
         out_specs=[HBM, HBM],
         out_shape=[f32(4, 32, 8, 128), f32(2, 32, 8, 128)],
         scratch_shapes=buffers(27, 5)
         + [
             pltpu.VMEM((4, OWN, 8, 128), jnp.float32),
             pltpu.VMEM((2, OWN, 8, 128), jnp.float32),
+            pltpu.VMEM((UP_ROWS, 128), jnp.float32),
+            pltpu.VMEM((UP_ROWS, 128), jnp.float32),
             pltpu.SMEM((2, 8), jnp.float32),
             pltpu.SemaphoreType.DMA,
             pltpu.SemaphoreType.DMA((6,)),
         ],
         compiler_params=params,
         name="upper_half",
-    )(where, cells, codes, table, across, own_lo, own_hi, up_lo, up_hi, grow, seam, phases, chems)
+    )(cells, codes, table, across, own_lo, own_hi, up_one, up_two, grow, seam, phases, chems)
 
 
 def solution(mesh):

time: 45.6 us -> 35.5 us (0.78)
  the two profiles are of different devices: /device:TPU:17 before, /device:TPU:24 now
where the time goes in v7:
time: 35.5 us; the launch traced here: 35.3 us
  Pallas kernels  14.3 us (40%)
  starting transfers between devices  13.7 us (39%)
  waiting for transfers between devices  6.63 us (19%)
  between operations  0.69 us (2%)
    pallas_call x1, Pallas kernels, on_device(): pl.pallas_call(upper_half, in_specs=[VMEM, VMEM, HBM] + [VMEM] * 9, out_s...  7.76 us
    ppermute x2, starting transfers between devices, send(): return lax.ppermute(value, AXES, pairs)  7.56 us
    ppermute x4, starting transfers between devices, swap(): return (lax.ppermute(one, 'gy', below), lax.ppermute(two, 'gy', above))  6.14 us
    pallas_call x1, Pallas kernels, on_device(): pl.pallas_call(lower_half, in_specs=[VMEM] * 4, out_specs=[VMEM] * 5, out...  5.19 us
    ppermute x2, waiting for transfers between devices, send(): return lax.ppermute(value, AXES, pairs)  4.28 us
    ppermute x4, waiting for transfers between devices, swap(): return (lax.ppermute(one, 'gy', below), lax.ppermute(two, 'gy', above))  2.35 us
    pallas_call x1, Pallas kernels, on_device(): pl.pallas_call(first_pack, in_specs=[HBM] * 3, out_specs=[VMEM] * 3, out_...  1.26 us
  transfers between devices with their start and end apart: 6, of which 4 were waited for; matrix products, arithmetic and copies ran while one was open for 0% of the time, Pallas kernels for 15%

profile of v7, /device:TPU:24, one launch (start us, length us, event | category | flops | bytes accessed | tf_op | source)
XLA Modules:
  0.0 35.3 jit_solution(6643576203182235242)
XLA Ops:
  0.6 1.3 %first_pack.1 = (f32[3,32,8,128]{3,2,1,0:T(8,128)S(1)}, f32[16,8,128]{2,1,0:T(8,128)S(1)}, f32[10,8,128]{2,1,0:T(8,128)S(1)}) custom-call(s32[32,8,128]{2,1,0:T(8,128)} %labels.1, f32[2,32,8,128]{3,2,1,0:T(8,128)} %potential.1, s32[16,8,128]{2,1,0:T(8,128)} %codes.1), custom_call_target="tpu_custom_call" | custom-call | tf_op jit(solution)/shard_map/first_pack/pallas_call | solution.py:547
  1.9 0.8 %collective-permute-start = (f32[10,8,128]{2,1,0:T(8,128)S(1)}, f32[10,8,128]{2,1,0:T(8,128)S(1)}, u32[]{:S(2)}, u32[]{:S(2)}) collective-permute-start(f32[10,8,128]{2,1,0:T(8,128)S(1)} %get-tuple-element.17), channel_id=1, source_target_pairs={{0,1},{1,0},{2,3},{3,2},{4,5},{5,4},{6,7},{7,6},{8,9},{9,8},{10,11... | collective-permute-start | bytes 122888 | tf_op jit(solution)/shard_map/ppermute | solution.py:541
  2.7 3.3 %collective-permute-done.across = f32[10,8,128]{2,1,0:T(8,128)S(1)} collective-permute-done((f32[10,8,128]{2,1,0:T(8,128)S(1)}, f32[10,8,128]{2,1,0:T(8,128)S(1)}, u32[]{:S(2)}, u32[]{:S(2)}) %collective-permute-start) | collective-permute-done | bytes 40992 | tf_op jit(solution)/shard_map/ppermute | solution.py:541
  6.0 0.1 second_pack.1
  6.1 6.7 %collective-permute-start.3 = (f32[3,23,8,128]{3,2,1,0:T(8,128)S(1)}, f32[3,23,8,128]{3,2,1,0:T(8,128)S(1)}, u32[]{:S(2)}, u32[]{:S(2)}) collective-permute-start(f32[3,23,8,128]{3,2,1,0:T(8,128)S(1)} %get-tuple-element.22), channel_id=1, source_target_pairs={{8,0},{9,1},{10,2},{11,3},{12,4},{13,5},{14,6},{15,7},{16,8},{17,9... | collective-permute-start | bytes 847880 | tf_op jit(solution)/shard_map/ppermute | solution.py:541
  12.8 2.8 %collective-permute-start.1 = (f32[312,128]{1,0:T(8,128)S(1)}, f32[312,128]{1,0:T(8,128)S(1)}, u32[]{:S(2)}, u32[]{:S(2)}) collective-permute-start(f32[312,128]{1,0:T(8,128)S(1)} %get-tuple-element.18), channel_id=1, source_target_pairs={{0,6},{2,4},{4,2},{6,0},{1,7},{3,5},{5,3},{7,1},{8,14},{10,12},{12... | collective-permute-start | bytes 479240 | tf_op jit(solution)/shard_map/ppermute | solution.py:573
  15.6 0.2 collective-permute-start.2
  15.9 1.0 %collective-permute-done.3.grow = f32[3,23,8,128]{3,2,1,0:T(8,128)S(1)} collective-permute-done((f32[3,23,8,128]{3,2,1,0:T(8,128)S(1)}, f32[3,23,8,128]{3,2,1,0:T(8,128)S(1)}, u32[]{:S(2)}, u32[]{:S(2)}) %collective-permute-start.3) | collective-permute-done | bytes 282656 | tf_op jit(solution)/shard_map/ppermute | solution.py:541
  16.9 2.8 %collective-permute-start.4 = (f32[312,128]{1,0:T(8,128)S(1)}, f32[312,128]{1,0:T(8,128)S(1)}, u32[]{:S(2)}, u32[]{:S(2)}) collective-permute-start(f32[312,128]{1,0:T(8,128)S(1)} %get-tuple-element.23), channel_id=1, source_target_pairs={{0,6},{2,4},{4,2},{6,0},{1,7},{3,5},{5,3},{7,1},{8,14},{10,12},{12... | collective-permute-start | bytes 479240 | tf_op jit(solution)/shard_map/ppermute | solution.py:573
  19.8 0.2 collective-permute-start.5
  20.0 0.6 %collective-permute-done.1.swap_one = f32[312,128]{1,0:T(8,128)S(1)} collective-permute-done((f32[312,128]{1,0:T(8,128)S(1)}, f32[312,128]{1,0:T(8,128)S(1)}, u32[]{:S(2)}, u32[]{:S(2)}) %collective-permute-start.1) | collective-permute-done | bytes 159776 | tf_op jit(solution)/shard_map/ppermute | solution.py:573
  20.6 1.8 %collective-permute-done.2.swap_two = f32[312,128]{1,0:T(8,128)S(1)} collective-permute-done((f32[312,128]{1,0:T(8,128)S(1)}, f32[312,128]{1,0:T(8,128)S(1)}, u32[]{:S(2)}, u32[]{:S(2)}) %collective-permute-start.2) | collective-permute-done | bytes 159776 | tf_op jit(solution)/shard_map/ppermute | solution.py:573
  22.3 5.2 %lower_half.1 = (f32[4,11,8,128]{3,2,1,0:T(8,128)S(1)}, f32[2,11,8,128]{3,2,1,0:T(8,128)S(1)}, f32[4,7,2,16,128]{4,3,2,1,0:T(8,128)S(1)}, f32[312,128]{1,0:T(8,128)S(1)}, f32[312,128]{1,0:T(8,128)S(1)}) custom-call(f32[3,32,8,128]{3,2,1,0:T(8,128)S(1)} %get-tuple-element.15.cells, f32[10,8,128]{2,1,0:T(8,128)S(1)} %collective-permute-done.across, ...), custom_call_target="tpu_custom_call" | custom-call | flops 60000000 | bytes 12000000 | tf_op jit(solution)/shard_map/lower_half/pallas_call | solution.py:594
  27.5 0.0 collective-permute-done.4.swap_one
  27.6 0.0 collective-permute-done.5.swap_two
  27.6 7.8 %upper_half.1 = (f32[4,32,8,128]{3,2,1,0:T(8,128)}, f32[2,32,8,128]{3,2,1,0:T(8,128)}) custom-call(f32[3,32,8,128]{3,2,1,0:T(8,128)S(1)} %get-tuple-element.15.cells, f32[16,8,128]{2,1,0:T(8,128)S(1)} %get-tuple-element.16.codes, f32[2,8]{1,0:T(2,128)} %table_in.1, f32[10,8,128]{2,1,0:T(8,128)S(1)} %collective-permute-done.across, ...), custom_call_target="tpu_custom_call" | custom-call | tf_op jit(solution)/shard_map/upper_half/pallas_call | solution.py:608
  (1 shorter events, 0.0 us)
Async XLA Ops:
  1.9 4.1 %collective-permute-start = (f32[10,8,128]{2,1,0:T(8,128)S(1)}, f32[10,8,128]{2,1,0:T(8,128)S(1)}, u32[]{:S(2)}, u32[]{:S(2)}) collective-permute-start(f32[10,8,128]{2,1,0:T(8,128)S(1)} %get-tuple-element.17), channel_id=1, source_target_pairs={{0,1},{1,0},{2,3},{3,2},{4,5},{5,4},{6,7},{7,6},{8,9},{9,8},{10,11... | collective-permute-start | bytes 122888 | tf_op jit(solution)/shard_map/ppermute | solution.py:541
  6.1 10.8 %collective-permute-start.3 = (f32[3,23,8,128]{3,2,1,0:T(8,128)S(1)}, f32[3,23,8,128]{3,2,1,0:T(8,128)S(1)}, u32[]{:S(2)}, u32[]{:S(2)}) collective-permute-start(f32[3,23,8,128]{3,2,1,0:T(8,128)S(1)} %get-tuple-element.22), channel_id=1, source_target_pairs={{8,0},{9,1},{10,2},{11,3},{12,4},{13,5},{14,6},{15,7},{16,8},{17,9... | collective-permute-start | bytes 847880 | tf_op jit(solution)/shard_map/ppermute | solution.py:541
  12.8 7.8 %collective-permute-start.1 = (f32[312,128]{1,0:T(8,128)S(1)}, f32[312,128]{1,0:T(8,128)S(1)}, u32[]{:S(2)}, u32[]{:S(2)}) collective-permute-start(f32[312,128]{1,0:T(8,128)S(1)} %get-tuple-element.18), channel_id=1, source_target_pairs={{0,6},{2,4},{4,2},{6,0},{1,7},{3,5},{5,3},{7,1},{8,14},{10,12},{12... | collective-permute-start | bytes 479240 | tf_op jit(solution)/shard_map/ppermute | solution.py:573
  15.6 6.7 %collective-permute-start.2 = (f32[312,128]{1,0:T(8,128)S(1)}, f32[312,128]{1,0:T(8,128)S(1)}, u32[]{:S(2)}, u32[]{:S(2)}) collective-permute-start(f32[312,128]{1,0:T(8,128)S(1)} %get-tuple-element.19), channel_id=1, source_target_pairs={{0,2},{2,0},{4,6},{6,4},{1,3},{3,1},{5,7},{7,5},{8,10},{10,8},{12,... | collective-permute-start | bytes 479240 | tf_op jit(solution)/shard_map/ppermute | solution.py:573
  16.9 10.6 %collective-permute-start.4 = (f32[312,128]{1,0:T(8,128)S(1)}, f32[312,128]{1,0:T(8,128)S(1)}, u32[]{:S(2)}, u32[]{:S(2)}) collective-permute-start(f32[312,128]{1,0:T(8,128)S(1)} %get-tuple-element.23), channel_id=1, source_target_pairs={{0,6},{2,4},{4,2},{6,0},{1,7},{3,5},{5,3},{7,1},{8,14},{10,12},{12... | collective-permute-start | bytes 479240 | tf_op jit(solution)/shard_map/ppermute | solution.py:573
  19.8 7.8 %collective-permute-start.5 = (f32[312,128]{1,0:T(8,128)S(1)}, f32[312,128]{1,0:T(8,128)S(1)}, u32[]{:S(2)}, u32[]{:S(2)}) collective-permute-start(f32[312,128]{1,0:T(8,128)S(1)} %get-tuple-element.24), channel_id=1, source_target_pairs={{0,2},{2,0},{4,6},{6,4},{1,3},{3,1},{5,7},{7,5},{8,10},{10,8},{12,... | collective-permute-start | bytes 479240 | tf_op jit(solution)/shard_map/ppermute | solution.py:573

commit v8 on v7

--- a/solution.py
+++ b/solution.py
@@ -533,10 +533,11 @@
 
     def send(value, dg, dy, dz):
         pairs = []
-        for g in range(max(0, -dg), n_grow):
+        for g in range(n_grow):
             for y in range(n_gy):
                 for z in range(n_gz):
-                    to = ((g + dg) * n_gy + (y + dy) % n_gy) * n_gz + (z + dz) % n_gz
+                    side = (z + dz + (not 0 <= g + dg < n_grow)) % n_gz
+                    to = ((g + dg) % n_grow * n_gy + (y + dy) % n_gy) * n_gz + side
                     pairs.append(((g * n_gy + y) * n_gz + z, to))
         return lax.ppermute(value, AXES, pairs)
 

time: 35.5 us -> 34.4 us (0.969)
  the two profiles are of different devices: /device:TPU:24 before, /device:TPU:8 now
where the time goes in v8:
time: 34.4 us; the launch traced here: 34.3 us
  Pallas kernels  14.5 us (42%)
  starting transfers between devices  13.4 us (39%)
  waiting for transfers between devices  5.58 us (16%)
  between operations  0.84 us (2%)
    pallas_call x1, Pallas kernels, on_device(): pl.pallas_call(upper_half, in_specs=[VMEM, VMEM, HBM] + [VMEM] * 9, out_s...  7.94 us
    ppermute x2, starting transfers between devices, send(): return lax.ppermute(value, AXES, pairs)  7.34 us
    ppermute x4, starting transfers between devices, swap(): return (lax.ppermute(one, 'gy', below), lax.ppermute(two, 'gy', above))  6.05 us
    pallas_call x1, Pallas kernels, on_device(): pl.pallas_call(lower_half, in_specs=[VMEM] * 4, out_specs=[VMEM] * 5, out...  5.2 us
    ppermute x2, waiting for transfers between devices, send(): return lax.ppermute(value, AXES, pairs)  3.11 us
    ppermute x4, waiting for transfers between devices, swap(): return (lax.ppermute(one, 'gy', below), lax.ppermute(two, 'gy', above))  2.48 us
    pallas_call x1, Pallas kernels, on_device(): pl.pallas_call(first_pack, in_specs=[HBM] * 3, out_specs=[VMEM] * 3, out_...  1.26 us
  transfers between devices with their start and end apart: 6, of which 4 were waited for; matrix products, arithmetic and copies ran while one was open for 0% of the time, Pallas kernels for 15%

profile of v8, /device:TPU:8, one launch (start us, length us, event | category | flops | bytes accessed | tf_op | source)
XLA Modules:
  0.0 34.3 jit_solution(10227620251950755509)
XLA Ops:
  0.6 1.3 %first_pack.1 = (f32[3,32,8,128]{3,2,1,0:T(8,128)S(1)}, f32[16,8,128]{2,1,0:T(8,128)S(1)}, f32[10,8,128]{2,1,0:T(8,128)S(1)}) custom-call(s32[32,8,128]{2,1,0:T(8,128)} %labels.1, f32[2,32,8,128]{3,2,1,0:T(8,128)} %potential.1, s32[16,8,128]{2,1,0:T(8,128)} %codes.1), custom_call_target="tpu_custom_call" | custom-call | tf_op jit(solution)/shard_map/first_pack/pallas_call | solution.py:548
  1.9 2.3 %collective-permute-start = (f32[10,8,128]{2,1,0:T(8,128)S(1)}, f32[10,8,128]{2,1,0:T(8,128)S(1)}, u32[]{:S(2)}, u32[]{:S(2)}) collective-permute-start(f32[10,8,128]{2,1,0:T(8,128)S(1)} %get-tuple-element.17), channel_id=1, source_target_pairs={{0,1},{1,0},{2,3},{3,2},{4,5},{5,4},{6,7},{7,6},{8,9},{9,8},{10,11... | collective-permute-start | bytes 122888 | tf_op jit(solution)/shard_map/ppermute | solution.py:542
  4.2 2.0 %collective-permute-done.across = f32[10,8,128]{2,1,0:T(8,128)S(1)} collective-permute-done((f32[10,8,128]{2,1,0:T(8,128)S(1)}, f32[10,8,128]{2,1,0:T(8,128)S(1)}, u32[]{:S(2)}, u32[]{:S(2)}) %collective-permute-start) | collective-permute-done | bytes 40992 | tf_op jit(solution)/shard_map/ppermute | solution.py:542
  6.2 0.1 second_pack.1
  6.2 5.1 %collective-permute-start.3 = (f32[3,23,8,128]{3,2,1,0:T(8,128)S(1)}, f32[3,23,8,128]{3,2,1,0:T(8,128)S(1)}, u32[]{:S(2)}, u32[]{:S(2)}) collective-permute-start(f32[3,23,8,128]{3,2,1,0:T(8,128)S(1)} %get-tuple-element.22), channel_id=1, source_target_pairs={{0,249},{1,248},{2,251},{3,250},{4,253},{5,252},{6,255},{7,254},{8... | collective-permute-start | bytes 847880 | tf_op jit(solution)/shard_map/ppermute | solution.py:542
  11.3 2.8 %collective-permute-start.1 = (f32[312,128]{1,0:T(8,128)S(1)}, f32[312,128]{1,0:T(8,128)S(1)}, u32[]{:S(2)}, u32[]{:S(2)}) collective-permute-start(f32[312,128]{1,0:T(8,128)S(1)} %get-tuple-element.18), channel_id=1, source_target_pairs={{0,6},{2,4},{4,2},{6,0},{1,7},{3,5},{5,3},{7,1},{8,14},{10,12},{12... | collective-permute-start | bytes 479240 | tf_op jit(solution)/shard_map/ppermute | solution.py:574
  14.0 0.2 collective-permute-start.2
  14.3 1.1 %collective-permute-done.3.grow = f32[3,23,8,128]{3,2,1,0:T(8,128)S(1)} collective-permute-done((f32[3,23,8,128]{3,2,1,0:T(8,128)S(1)}, f32[3,23,8,128]{3,2,1,0:T(8,128)S(1)}, u32[]{:S(2)}, u32[]{:S(2)}) %collective-permute-start.3) | collective-permute-done | bytes 282656 | tf_op jit(solution)/shard_map/ppermute | solution.py:542
  15.5 2.8 %collective-permute-start.4 = (f32[312,128]{1,0:T(8,128)S(1)}, f32[312,128]{1,0:T(8,128)S(1)}, u32[]{:S(2)}, u32[]{:S(2)}) collective-permute-start(f32[312,128]{1,0:T(8,128)S(1)} %get-tuple-element.23), channel_id=1, source_target_pairs={{0,6},{2,4},{4,2},{6,0},{1,7},{3,5},{5,3},{7,1},{8,14},{10,12},{12... | collective-permute-start | bytes 479240 | tf_op jit(solution)/shard_map/ppermute | solution.py:574
  18.3 0.2 collective-permute-start.5
  18.5 0.6 %collective-permute-done.1.swap_one = f32[312,128]{1,0:T(8,128)S(1)} collective-permute-done((f32[312,128]{1,0:T(8,128)S(1)}, f32[312,128]{1,0:T(8,128)S(1)}, u32[]{:S(2)}, u32[]{:S(2)}) %collective-permute-start.1) | collective-permute-done | bytes 159776 | tf_op jit(solution)/shard_map/ppermute | solution.py:574
  19.2 1.8 %collective-permute-done.2.swap_two = f32[312,128]{1,0:T(8,128)S(1)} collective-permute-done((f32[312,128]{1,0:T(8,128)S(1)}, f32[312,128]{1,0:T(8,128)S(1)}, u32[]{:S(2)}, u32[]{:S(2)}) %collective-permute-start.2) | collective-permute-done | bytes 159776 | tf_op jit(solution)/shard_map/ppermute | solution.py:574
  21.0 5.2 %lower_half.1 = (f32[4,11,8,128]{3,2,1,0:T(8,128)S(1)}, f32[2,11,8,128]{3,2,1,0:T(8,128)S(1)}, f32[4,7,2,16,128]{4,3,2,1,0:T(8,128)S(1)}, f32[312,128]{1,0:T(8,128)S(1)}, f32[312,128]{1,0:T(8,128)S(1)}) custom-call(f32[3,32,8,128]{3,2,1,0:T(8,128)S(1)} %get-tuple-element.15.cells, f32[10,8,128]{2,1,0:T(8,128)S(1)} %collective-permute-done.across, ...), custom_call_target="tpu_custom_call" | custom-call | flops 60000000 | bytes 12000000 | tf_op jit(solution)/shard_map/lower_half/pallas_call | solution.py:595
  26.2 0.0 collective-permute-done.4.swap_one
  26.2 0.0 collective-permute-done.5.swap_two
  26.2 7.9 %upper_half.1 = (f32[4,32,8,128]{3,2,1,0:T(8,128)}, f32[2,32,8,128]{3,2,1,0:T(8,128)}) custom-call(f32[3,32,8,128]{3,2,1,0:T(8,128)S(1)} %get-tuple-element.15.cells, f32[16,8,128]{2,1,0:T(8,128)S(1)} %get-tuple-element.16.codes, f32[2,8]{1,0:T(2,128)} %table_in.1, f32[10,8,128]{2,1,0:T(8,128)S(1)} %collective-permute-done.across, ...), custom_call_target="tpu_custom_call" | custom-call | tf_op jit(solution)/shard_map/upper_half/pallas_call | solution.py:609
  (1 shorter events, 0.0 us)
Async XLA Ops:
  1.9 4.3 %collective-permute-start = (f32[10,8,128]{2,1,0:T(8,128)S(1)}, f32[10,8,128]{2,1,0:T(8,128)S(1)}, u32[]{:S(2)}, u32[]{:S(2)}) collective-permute-start(f32[10,8,128]{2,1,0:T(8,128)S(1)} %get-tuple-element.17), channel_id=1, source_target_pairs={{0,1},{1,0},{2,3},{3,2},{4,5},{5,4},{6,7},{7,6},{8,9},{9,8},{10,11... | collective-permute-start | bytes 122888 | tf_op jit(solution)/shard_map/ppermute | solution.py:542
  6.2 9.2 %collective-permute-start.3 = (f32[3,23,8,128]{3,2,1,0:T(8,128)S(1)}, f32[3,23,8,128]{3,2,1,0:T(8,128)S(1)}, u32[]{:S(2)}, u32[]{:S(2)}) collective-permute-start(f32[3,23,8,128]{3,2,1,0:T(8,128)S(1)} %get-tuple-element.22), channel_id=1, source_target_pairs={{0,249},{1,248},{2,251},{3,250},{4,253},{5,252},{6,255},{7,254},{8... | collective-permute-start | bytes 847880 | tf_op jit(solution)/shard_map/ppermute | solution.py:542
  11.3 7.9 %collective-permute-start.1 = (f32[312,128]{1,0:T(8,128)S(1)}, f32[312,128]{1,0:T(8,128)S(1)}, u32[]{:S(2)}, u32[]{:S(2)}) collective-permute-start(f32[312,128]{1,0:T(8,128)S(1)} %get-tuple-element.18), channel_id=1, source_target_pairs={{0,6},{2,4},{4,2},{6,0},{1,7},{3,5},{5,3},{7,1},{8,14},{10,12},{12... | collective-permute-start | bytes 479240 | tf_op jit(solution)/shard_map/ppermute | solution.py:574
  14.0 6.9 %collective-permute-start.2 = (f32[312,128]{1,0:T(8,128)S(1)}, f32[312,128]{1,0:T(8,128)S(1)}, u32[]{:S(2)}, u32[]{:S(2)}) collective-permute-start(f32[312,128]{1,0:T(8,128)S(1)} %get-tuple-element.19), channel_id=1, source_target_pairs={{0,2},{2,0},{4,6},{6,4},{1,3},{3,1},{5,7},{7,5},{8,10},{10,8},{12,... | collective-permute-start | bytes 479240 | tf_op jit(solution)/shard_map/ppermute | solution.py:574
  15.5 10.8 %collective-permute-start.4 = (f32[312,128]{1,0:T(8,128)S(1)}, f32[312,128]{1,0:T(8,128)S(1)}, u32[]{:S(2)}, u32[]{:S(2)}) collective-permute-start(f32[312,128]{1,0:T(8,128)S(1)} %get-tuple-element.23), channel_id=1, source_target_pairs={{0,6},{2,4},{4,2},{6,0},{1,7},{3,5},{5,3},{7,1},{8,14},{10,12},{12... | collective-permute-start | bytes 479240 | tf_op jit(solution)/shard_map/ppermute | solution.py:574
  18.3 7.9 %collective-permute-start.5 = (f32[312,128]{1,0:T(8,128)S(1)}, f32[312,128]{1,0:T(8,128)S(1)}, u32[]{:S(2)}, u32[]{:S(2)}) collective-permute-start(f32[312,128]{1,0:T(8,128)S(1)} %get-tuple-element.24), channel_id=1, source_target_pairs={{0,2},{2,0},{4,6},{6,4},{1,3},{3,1},{5,7},{7,5},{8,10},{10,8},{12,... | collective-permute-start | bytes 479240 | tf_op jit(solution)/shard_map/ppermute | solution.py:574

commit v9 on v8

--- a/solution.py
+++ b/solution.py
@@ -244,9 +244,9 @@
             total = jnp.where(lane >= at, tile, total)
         return total
 
-    def fill_strips(self, dst, top):
+    def fill_strips(self, dst, top, blocks):
         for index in range(self.n):
-            for block, row, _ in BLOCKS:
+            for block, row, _ in blocks:
                 body = []
                 for f in range(3):
                     parts = []
@@ -417,8 +417,13 @@
 LOWER = 11
 
 
+def strip_pack(cells, across, own_strips):
+    half = Half(0, 0, 4, cells, None, across, None, None, None, None)
+    half.fill_strips(own_strips, OWN, ((0, 0, 8),))
+
+
 def lower_half(
-    cells, across, swap_one, swap_two,
+    cells, across, own_strips, swap_one, swap_two,
     phases, chems, seam, rows_lo, rows_hi,
     one, two, strip_one, strip_two, wing,
 ):
@@ -432,7 +437,8 @@
     half = Half(0, 0, 4, cells, None, across, (rows_lo, rows_hi), None, None, wing)
     for p in range(OWN):
         half.fill(one, p)
-    half.fill_strips(strip_one, OWN)
+    strip_one[:, :, ROW0 : ROW0 + 8, :] = own_strips[...]
+    half.fill_strips(strip_one, OWN, BLOCKS[1:])
     src, dst, src_strips, dst_strips = one, two, strip_one, strip_two
     for s in range(1, 5):
         if s == 4:
@@ -486,7 +492,7 @@
     )
     for p in range(OWN - 2, PLANES):
         half.fill(one, p)
-    half.fill_strips(strip_one, PLANES)
+    half.fill_strips(strip_one, PLANES, BLOCKS)
     src, dst, src_strips, dst_strips = one, two, strip_one, strip_two
     for s in range(1, 6):
         if s > 1:
@@ -592,9 +598,17 @@
             + [pltpu.VMEM((5, strips, PITCH, 128), jnp.float32)]
         )
 
+    own_strips = pl.pallas_call(
+        strip_pack,
+        in_specs=[VMEM] * 2,
+        out_specs=VMEM,
+        out_shape=f32(7, 4, 8, 128),
+        compiler_params=params,
+        name="strip_pack",
+    )(cells, across)
     phases, chems, seam, own_lo, own_hi = pl.pallas_call(
         lower_half,
-        in_specs=[VMEM] * 4,
+        in_specs=[VMEM] * 5,
         out_specs=[VMEM] * 5,
         out_shape=[f32(4, LOWER, 8, 128), f32(2, LOWER, 8, 128), f32(4, 7, 2, 16, 128)]
         + [f32(OWN_ROWS, 128)] * 2,
@@ -604,7 +618,7 @@
             flops=60_000_000, bytes_accessed=12_000_000, transcendentals=0
         ),
         name="lower_half",
-    )(cells, across, own_one, own_two)
+    )(cells, across, own_strips, own_one, own_two)
     table = pltpu.with_memory_space_constraint(melt_table, pltpu.MemorySpace.HBM)
     return pl.pallas_call(
         upper_half,

time: 34.4 us -> 34.2 us (level)
    pallas_call x1 -> x2, Pallas kernels: 5.2 us -> 5.27 us  [the longest x1 4.94 us: on_device(): pl.pallas_call(lower_half, in_specs=[VMEM] * 5, out_specs=[VMEM] * 5, out...]
  transfers between devices with their start and end apart: 6 -> 6, of which waited for: 4 -> 4; matrix products, arithmetic and copies ran while one was open for 0% -> 0% of each run, Pallas kernels for 15% -> 16%
where the time goes in v9:
time: 34.2 us; the launch traced here: 34.1 us
  Pallas kernels  14.6 us (43%)
  starting transfers between devices  13.4 us (39%)
  waiting for transfers between devices  5.26 us (15%)
  between operations  0.85 us (2%)
    pallas_call x1, Pallas kernels, on_device(): pl.pallas_call(upper_half, in_specs=[VMEM, VMEM, HBM] + [VMEM] * 9, out_s...  7.94 us
    ppermute x2, starting transfers between devices, send(): return lax.ppermute(value, AXES, pairs)  7.34 us
    ppermute x4, starting transfers between devices, swap(): return (lax.ppermute(one, 'gy', below), lax.ppermute(two, 'gy', above))  6.05 us
    pallas_call x1, Pallas kernels, on_device(): pl.pallas_call(lower_half, in_specs=[VMEM] * 5, out_specs=[VMEM] * 5, out...  4.94 us
    ppermute x2, waiting for transfers between devices, send(): return lax.ppermute(value, AXES, pairs)  3.11 us
    ppermute x4, waiting for transfers between devices, swap(): return (lax.ppermute(one, 'gy', below), lax.ppermute(two, 'gy', above))  2.15 us
    pallas_call x1, Pallas kernels, on_device(): pl.pallas_call(first_pack, in_specs=[HBM] * 3, out_specs=[VMEM] * 3, out_...  1.26 us
  transfers between devices with their start and end apart: 6, of which 4 were waited for; matrix products, arithmetic and copies ran while one was open for 0% of the time, Pallas kernels for 16%

profile of v9, /device:TPU:8, one launch (start us, length us, event | category | flops | bytes accessed | tf_op | source)
XLA Modules:
  0.0 34.1 jit_solution(13630013544648102339)
XLA Ops:
  0.6 1.3 %first_pack.1 = (f32[3,32,8,128]{3,2,1,0:T(8,128)S(1)}, f32[16,8,128]{2,1,0:T(8,128)S(1)}, f32[10,8,128]{2,1,0:T(8,128)S(1)}) custom-call(s32[32,8,128]{2,1,0:T(8,128)} %labels.1, f32[2,32,8,128]{3,2,1,0:T(8,128)} %potential.1, s32[16,8,128]{2,1,0:T(8,128)} %codes.1), custom_call_target="tpu_custom_call" | custom-call | tf_op jit(solution)/shard_map/first_pack/pallas_call | solution.py:554
  1.9 2.3 %collective-permute-start = (f32[10,8,128]{2,1,0:T(8,128)S(1)}, f32[10,8,128]{2,1,0:T(8,128)S(1)}, u32[]{:S(2)}, u32[]{:S(2)}) collective-permute-start(f32[10,8,128]{2,1,0:T(8,128)S(1)} %get-tuple-element.17), channel_id=1, source_target_pairs={{0,1},{1,0},{2,3},{3,2},{4,5},{5,4},{6,7},{7,6},{8,9},{9,8},{10,11... | collective-permute-start | bytes 122888 | tf_op jit(solution)/shard_map/ppermute | solution.py:548
  4.2 2.0 %collective-permute-done.across = f32[10,8,128]{2,1,0:T(8,128)S(1)} collective-permute-done((f32[10,8,128]{2,1,0:T(8,128)S(1)}, f32[10,8,128]{2,1,0:T(8,128)S(1)}, u32[]{:S(2)}, u32[]{:S(2)}) %collective-permute-start) | collective-permute-done | bytes 40992 | tf_op jit(solution)/shard_map/ppermute | solution.py:548
  6.2 0.1 second_pack.1
  6.2 5.1 %collective-permute-start.3 = (f32[3,23,8,128]{3,2,1,0:T(8,128)S(1)}, f32[3,23,8,128]{3,2,1,0:T(8,128)S(1)}, u32[]{:S(2)}, u32[]{:S(2)}) collective-permute-start(f32[3,23,8,128]{3,2,1,0:T(8,128)S(1)} %get-tuple-element.22), channel_id=1, source_target_pairs={{0,249},{1,248},{2,251},{3,250},{4,253},{5,252},{6,255},{7,254},{8... | collective-permute-start | bytes 847880 | tf_op jit(solution)/shard_map/ppermute | solution.py:548
  11.3 2.8 %collective-permute-start.1 = (f32[312,128]{1,0:T(8,128)S(1)}, f32[312,128]{1,0:T(8,128)S(1)}, u32[]{:S(2)}, u32[]{:S(2)}) collective-permute-start(f32[312,128]{1,0:T(8,128)S(1)} %get-tuple-element.18), channel_id=1, source_target_pairs={{0,6},{2,4},{4,2},{6,0},{1,7},{3,5},{5,3},{7,1},{8,14},{10,12},{12... | collective-permute-start | bytes 479240 | tf_op jit(solution)/shard_map/ppermute | solution.py:580
  14.0 0.2 collective-permute-start.2
  14.3 1.1 %collective-permute-done.3.grow = f32[3,23,8,128]{3,2,1,0:T(8,128)S(1)} collective-permute-done((f32[3,23,8,128]{3,2,1,0:T(8,128)S(1)}, f32[3,23,8,128]{3,2,1,0:T(8,128)S(1)}, u32[]{:S(2)}, u32[]{:S(2)}) %collective-permute-start.3) | collective-permute-done | bytes 282656 | tf_op jit(solution)/shard_map/ppermute | solution.py:548
  15.5 2.8 %collective-permute-start.4 = (f32[312,128]{1,0:T(8,128)S(1)}, f32[312,128]{1,0:T(8,128)S(1)}, u32[]{:S(2)}, u32[]{:S(2)}) collective-permute-start(f32[312,128]{1,0:T(8,128)S(1)} %get-tuple-element.23), channel_id=1, source_target_pairs={{0,6},{2,4},{4,2},{6,0},{1,7},{3,5},{5,3},{7,1},{8,14},{10,12},{12... | collective-permute-start | bytes 479240 | tf_op jit(solution)/shard_map/ppermute | solution.py:580
  18.3 0.2 collective-permute-start.5
  18.5 0.3 strip_pack.1.own_strips
  18.9 0.3 collective-permute-done.1.swap_one
  19.2 1.8 %collective-permute-done.2.swap_two = f32[312,128]{1,0:T(8,128)S(1)} collective-permute-done((f32[312,128]{1,0:T(8,128)S(1)}, f32[312,128]{1,0:T(8,128)S(1)}, u32[]{:S(2)}, u32[]{:S(2)}) %collective-permute-start.2) | collective-permute-done | bytes 159776 | tf_op jit(solution)/shard_map/ppermute | solution.py:580
  21.0 4.9 %lower_half.1 = (f32[4,11,8,128]{3,2,1,0:T(8,128)S(1)}, f32[2,11,8,128]{3,2,1,0:T(8,128)S(1)}, f32[4,7,2,16,128]{4,3,2,1,0:T(8,128)S(1)}, f32[312,128]{1,0:T(8,128)S(1)}, f32[312,128]{1,0:T(8,128)S(1)}) custom-call(f32[3,32,8,128]{3,2,1,0:T(8,128)S(1)} %get-tuple-element.15.cells, f32[10,8,128]{2,1,0:T(8,128)S(1)} %collective-permute-done.across, ...), custom_call_target="tpu_custom_call" | custom-call | flops 60000000 | bytes 12000000 | tf_op jit(solution)/shard_map/lower_half/pallas_call | solution.py:609
  25.9 0.0 collective-permute-done.4.swap_one
  26.0 0.0 collective-permute-done.5.swap_two
  26.0 7.9 %upper_half.1 = (f32[4,32,8,128]{3,2,1,0:T(8,128)}, f32[2,32,8,128]{3,2,1,0:T(8,128)}) custom-call(f32[3,32,8,128]{3,2,1,0:T(8,128)S(1)} %get-tuple-element.15.cells, f32[16,8,128]{2,1,0:T(8,128)S(1)} %get-tuple-element.16.codes, f32[2,8]{1,0:T(2,128)} %table_in.1, f32[10,8,128]{2,1,0:T(8,128)S(1)} %collective-permute-done.across, ...), custom_call_target="tpu_custom_call" | custom-call | tf_op jit(solution)/shard_map/upper_half/pallas_call | solution.py:623
  (1 shorter events, 0.0 us)
Async XLA Ops:
  1.9 4.3 %collective-permute-start = (f32[10,8,128]{2,1,0:T(8,128)S(1)}, f32[10,8,128]{2,1,0:T(8,128)S(1)}, u32[]{:S(2)}, u32[]{:S(2)}) collective-permute-start(f32[10,8,128]{2,1,0:T(8,128)S(1)} %get-tuple-element.17), channel_id=1, source_target_pairs={{0,1},{1,0},{2,3},{3,2},{4,5},{5,4},{6,7},{7,6},{8,9},{9,8},{10,11... | collective-permute-start | bytes 122888 | tf_op jit(solution)/shard_map/ppermute | solution.py:548
  6.2 9.2 %collective-permute-start.3 = (f32[3,23,8,128]{3,2,1,0:T(8,128)S(1)}, f32[3,23,8,128]{3,2,1,0:T(8,128)S(1)}, u32[]{:S(2)}, u32[]{:S(2)}) collective-permute-start(f32[3,23,8,128]{3,2,1,0:T(8,128)S(1)} %get-tuple-element.22), channel_id=1, source_target_pairs={{0,249},{1,248},{2,251},{3,250},{4,253},{5,252},{6,255},{7,254},{8... | collective-permute-start | bytes 847880 | tf_op jit(solution)/shard_map/ppermute | solution.py:548
  11.3 7.9 %collective-permute-start.1 = (f32[312,128]{1,0:T(8,128)S(1)}, f32[312,128]{1,0:T(8,128)S(1)}, u32[]{:S(2)}, u32[]{:S(2)}) collective-permute-start(f32[312,128]{1,0:T(8,128)S(1)} %get-tuple-element.18), channel_id=1, source_target_pairs={{0,6},{2,4},{4,2},{6,0},{1,7},{3,5},{5,3},{7,1},{8,14},{10,12},{12... | collective-permute-start | bytes 479240 | tf_op jit(solution)/shard_map/ppermute | solution.py:580
  14.0 6.9 %collective-permute-start.2 = (f32[312,128]{1,0:T(8,128)S(1)}, f32[312,128]{1,0:T(8,128)S(1)}, u32[]{:S(2)}, u32[]{:S(2)}) collective-permute-start(f32[312,128]{1,0:T(8,128)S(1)} %get-tuple-element.19), channel_id=1, source_target_pairs={{0,2},{2,0},{4,6},{6,4},{1,3},{3,1},{5,7},{7,5},{8,10},{10,8},{12,... | collective-permute-start | bytes 479240 | tf_op jit(solution)/shard_map/ppermute | solution.py:580
  15.5 10.5 %collective-permute-start.4 = (f32[312,128]{1,0:T(8,128)S(1)}, f32[312,128]{1,0:T(8,128)S(1)}, u32[]{:S(2)}, u32[]{:S(2)}) collective-permute-start(f32[312,128]{1,0:T(8,128)S(1)} %get-tuple-element.23), channel_id=1, source_target_pairs={{0,6},{2,4},{4,2},{6,0},{1,7},{3,5},{5,3},{7,1},{8,14},{10,12},{12... | collective-permute-start | bytes 479240 | tf_op jit(solution)/shard_map/ppermute | solution.py:580
  18.3 7.7 %collective-permute-start.5 = (f32[312,128]{1,0:T(8,128)S(1)}, f32[312,128]{1,0:T(8,128)S(1)}, u32[]{:S(2)}, u32[]{:S(2)}) collective-permute-start(f32[312,128]{1,0:T(8,128)S(1)} %get-tuple-element.24), channel_id=1, source_target_pairs={{0,2},{2,0},{4,6},{6,4},{1,3},{3,1},{5,7},{7,5},{8,10},{10,8},{12,... | collective-permute-start | bytes 479240 | tf_op jit(solution)/shard_map/ppermute | solution.py:580

commit v10 on v9

--- a/solution.py
+++ b/solution.py
@@ -526,10 +526,10 @@
             half.sweep(src, dst, src_strips, dst_strips, OWN - s, OWN)
             src, dst, src_strips, dst_strips = dst, src, dst_strips, src_strips
     half.spread(src_strips, (ROW0,))
-    half.finish(src, OWN - 5, 12, phases, chems)
-    copies += delivery(phases, chems, *outs, LOWER, 0, 12, sems, 2)
-    half.finish(src, OWN + 7, 9, phases, chems, 12)
-    copies += delivery(phases, chems, *outs, LOWER + 12, 12, 9, sems, 4)
+    half.finish(src, OWN - 5, 16, phases, chems)
+    copies += delivery(phases, chems, *outs, LOWER, 0, 16, sems, 2)
+    half.finish(src, OWN + 11, 5, phases, chems, 16)
+    copies += delivery(phases, chems, *outs, LOWER + 16, 16, 5, sems, 4)
     for copy in copies:
         copy.wait()
 

time: 34.2 us -> 34.2 us (level)
  no operation moved by 1% of the time
where the time goes in v10:
time: 34.2 us; the launch traced here: 34.1 us
  Pallas kernels  14.6 us (43%)
  starting transfers between devices  13.4 us (39%)
  waiting for transfers between devices  5.26 us (15%)
  between operations  0.85 us (2%)
    pallas_call x1, Pallas kernels, on_device(): pl.pallas_call(upper_half, in_specs=[VMEM, VMEM, HBM] + [VMEM] * 9, out_s...  7.95 us
    ppermute x2, starting transfers between devices, send(): return lax.ppermute(value, AXES, pairs)  7.34 us
    ppermute x4, starting transfers between devices, swap(): return (lax.ppermute(one, 'gy', below), lax.ppermute(two, 'gy', above))  6.05 us
    pallas_call x1, Pallas kernels, on_device(): pl.pallas_call(lower_half, in_specs=[VMEM] * 5, out_specs=[VMEM] * 5, out...  4.94 us
    ppermute x2, waiting for transfers between devices, send(): return lax.ppermute(value, AXES, pairs)  3.11 us
    ppermute x4, waiting for transfers between devices, swap(): return (lax.ppermute(one, 'gy', below), lax.ppermute(two, 'gy', above))  2.15 us
    pallas_call x1, Pallas kernels, on_device(): pl.pallas_call(first_pack, in_specs=[HBM] * 3, out_specs=[VMEM] * 3, out_...  1.26 us
  transfers between devices with their start and end apart: 6, of which 4 were waited for; matrix products, arithmetic and copies ran while one was open for 0% of the time, Pallas kernels for 16%

profile of v10, /device:TPU:8, one launch (start us, length us, event | category | flops | bytes accessed | tf_op | source)
XLA Modules:
  0.0 34.1 jit_solution(5720613858878356528)
XLA Ops:
  0.6 1.3 %first_pack.1 = (f32[3,32,8,128]{3,2,1,0:T(8,128)S(1)}, f32[16,8,128]{2,1,0:T(8,128)S(1)}, f32[10,8,128]{2,1,0:T(8,128)S(1)}) custom-call(s32[32,8,128]{2,1,0:T(8,128)} %labels.1, f32[2,32,8,128]{3,2,1,0:T(8,128)} %potential.1, s32[16,8,128]{2,1,0:T(8,128)} %codes.1), custom_call_target="tpu_custom_call" | custom-call | tf_op jit(solution)/shard_map/first_pack/pallas_call | solution.py:554
  1.9 2.3 %collective-permute-start = (f32[10,8,128]{2,1,0:T(8,128)S(1)}, f32[10,8,128]{2,1,0:T(8,128)S(1)}, u32[]{:S(2)}, u32[]{:S(2)}) collective-permute-start(f32[10,8,128]{2,1,0:T(8,128)S(1)} %get-tuple-element.17), channel_id=1, source_target_pairs={{0,1},{1,0},{2,3},{3,2},{4,5},{5,4},{6,7},{7,6},{8,9},{9,8},{10,11... | collective-permute-start | bytes 122888 | tf_op jit(solution)/shard_map/ppermute | solution.py:548
  4.2 2.0 %collective-permute-done.across = f32[10,8,128]{2,1,0:T(8,128)S(1)} collective-permute-done((f32[10,8,128]{2,1,0:T(8,128)S(1)}, f32[10,8,128]{2,1,0:T(8,128)S(1)}, u32[]{:S(2)}, u32[]{:S(2)}) %collective-permute-start) | collective-permute-done | bytes 40992 | tf_op jit(solution)/shard_map/ppermute | solution.py:548
  6.2 0.1 second_pack.1
  6.2 5.1 %collective-permute-start.3 = (f32[3,23,8,128]{3,2,1,0:T(8,128)S(1)}, f32[3,23,8,128]{3,2,1,0:T(8,128)S(1)}, u32[]{:S(2)}, u32[]{:S(2)}) collective-permute-start(f32[3,23,8,128]{3,2,1,0:T(8,128)S(1)} %get-tuple-element.22), channel_id=1, source_target_pairs={{0,249},{1,248},{2,251},{3,250},{4,253},{5,252},{6,255},{7,254},{8... | collective-permute-start | bytes 847880 | tf_op jit(solution)/shard_map/ppermute | solution.py:548
  11.3 2.8 %collective-permute-start.1 = (f32[312,128]{1,0:T(8,128)S(1)}, f32[312,128]{1,0:T(8,128)S(1)}, u32[]{:S(2)}, u32[]{:S(2)}) collective-permute-start(f32[312,128]{1,0:T(8,128)S(1)} %get-tuple-element.18), channel_id=1, source_target_pairs={{0,6},{2,4},{4,2},{6,0},{1,7},{3,5},{5,3},{7,1},{8,14},{10,12},{12... | collective-permute-start | bytes 479240 | tf_op jit(solution)/shard_map/ppermute | solution.py:580
  14.0 0.2 collective-permute-start.2
  14.3 1.1 %collective-permute-done.3.grow = f32[3,23,8,128]{3,2,1,0:T(8,128)S(1)} collective-permute-done((f32[3,23,8,128]{3,2,1,0:T(8,128)S(1)}, f32[3,23,8,128]{3,2,1,0:T(8,128)S(1)}, u32[]{:S(2)}, u32[]{:S(2)}) %collective-permute-start.3) | collective-permute-done | bytes 282656 | tf_op jit(solution)/shard_map/ppermute | solution.py:548
  15.5 2.8 %collective-permute-start.4 = (f32[312,128]{1,0:T(8,128)S(1)}, f32[312,128]{1,0:T(8,128)S(1)}, u32[]{:S(2)}, u32[]{:S(2)}) collective-permute-start(f32[312,128]{1,0:T(8,128)S(1)} %get-tuple-element.23), channel_id=1, source_target_pairs={{0,6},{2,4},{4,2},{6,0},{1,7},{3,5},{5,3},{7,1},{8,14},{10,12},{12... | collective-permute-start | bytes 479240 | tf_op jit(solution)/shard_map/ppermute | solution.py:580
  18.3 0.2 collective-permute-start.5
  18.5 0.3 strip_pack.1.own_strips
  18.9 0.3 collective-permute-done.1.swap_one
  19.2 1.8 %collective-permute-done.2.swap_two = f32[312,128]{1,0:T(8,128)S(1)} collective-permute-done((f32[312,128]{1,0:T(8,128)S(1)}, f32[312,128]{1,0:T(8,128)S(1)}, u32[]{:S(2)}, u32[]{:S(2)}) %collective-permute-start.2) | collective-permute-done | bytes 159776 | tf_op jit(solution)/shard_map/ppermute | solution.py:580
  21.0 4.9 %lower_half.1 = (f32[4,11,8,128]{3,2,1,0:T(8,128)S(1)}, f32[2,11,8,128]{3,2,1,0:T(8,128)S(1)}, f32[4,7,2,16,128]{4,3,2,1,0:T(8,128)S(1)}, f32[312,128]{1,0:T(8,128)S(1)}, f32[312,128]{1,0:T(8,128)S(1)}) custom-call(f32[3,32,8,128]{3,2,1,0:T(8,128)S(1)} %get-tuple-element.15.cells, f32[10,8,128]{2,1,0:T(8,128)S(1)} %collective-permute-done.across, ...), custom_call_target="tpu_custom_call" | custom-call | flops 60000000 | bytes 12000000 | tf_op jit(solution)/shard_map/lower_half/pallas_call | solution.py:609
  25.9 0.0 collective-permute-done.4.swap_one
  26.0 0.0 collective-permute-done.5.swap_two
  26.0 8.0 %upper_half.1 = (f32[4,32,8,128]{3,2,1,0:T(8,128)}, f32[2,32,8,128]{3,2,1,0:T(8,128)}) custom-call(f32[3,32,8,128]{3,2,1,0:T(8,128)S(1)} %get-tuple-element.15.cells, f32[16,8,128]{2,1,0:T(8,128)S(1)} %get-tuple-element.16.codes, f32[2,8]{1,0:T(2,128)} %table_in.1, f32[10,8,128]{2,1,0:T(8,128)S(1)} %collective-permute-done.across, ...), custom_call_target="tpu_custom_call" | custom-call | tf_op jit(solution)/shard_map/upper_half/pallas_call | solution.py:623
  (1 shorter events, 0.0 us)
Async XLA Ops:
  1.9 4.3 %collective-permute-start = (f32[10,8,128]{2,1,0:T(8,128)S(1)}, f32[10,8,128]{2,1,0:T(8,128)S(1)}, u32[]{:S(2)}, u32[]{:S(2)}) collective-permute-start(f32[10,8,128]{2,1,0:T(8,128)S(1)} %get-tuple-element.17), channel_id=1, source_target_pairs={{0,1},{1,0},{2,3},{3,2},{4,5},{5,4},{6,7},{7,6},{8,9},{9,8},{10,11... | collective-permute-start | bytes 122888 | tf_op jit(solution)/shard_map/ppermute | solution.py:548
  6.2 9.2 %collective-permute-start.3 = (f32[3,23,8,128]{3,2,1,0:T(8,128)S(1)}, f32[3,23,8,128]{3,2,1,0:T(8,128)S(1)}, u32[]{:S(2)}, u32[]{:S(2)}) collective-permute-start(f32[3,23,8,128]{3,2,1,0:T(8,128)S(1)} %get-tuple-element.22), channel_id=1, source_target_pairs={{0,249},{1,248},{2,251},{3,250},{4,253},{5,252},{6,255},{7,254},{8... | collective-permute-start | bytes 847880 | tf_op jit(solution)/shard_map/ppermute | solution.py:548
  11.3 7.9 %collective-permute-start.1 = (f32[312,128]{1,0:T(8,128)S(1)}, f32[312,128]{1,0:T(8,128)S(1)}, u32[]{:S(2)}, u32[]{:S(2)}) collective-permute-start(f32[312,128]{1,0:T(8,128)S(1)} %get-tuple-element.18), channel_id=1, source_target_pairs={{0,6},{2,4},{4,2},{6,0},{1,7},{3,5},{5,3},{7,1},{8,14},{10,12},{12... | collective-permute-start | bytes 479240 | tf_op jit(solution)/shard_map/ppermute | solution.py:580
  14.0 6.9 %collective-permute-start.2 = (f32[312,128]{1,0:T(8,128)S(1)}, f32[312,128]{1,0:T(8,128)S(1)}, u32[]{:S(2)}, u32[]{:S(2)}) collective-permute-start(f32[312,128]{1,0:T(8,128)S(1)} %get-tuple-element.19), channel_id=1, source_target_pairs={{0,2},{2,0},{4,6},{6,4},{1,3},{3,1},{5,7},{7,5},{8,10},{10,8},{12,... | collective-permute-start | bytes 479240 | tf_op jit(solution)/shard_map/ppermute | solution.py:580
  15.5 10.5 %collective-permute-start.4 = (f32[312,128]{1,0:T(8,128)S(1)}, f32[312,128]{1,0:T(8,128)S(1)}, u32[]{:S(2)}, u32[]{:S(2)}) collective-permute-start(f32[312,128]{1,0:T(8,128)S(1)} %get-tuple-element.23), channel_id=1, source_target_pairs={{0,6},{2,4},{4,2},{6,0},{1,7},{3,5},{5,3},{7,1},{8,14},{10,12},{12... | collective-permute-start | bytes 479240 | tf_op jit(solution)/shard_map/ppermute | solution.py:580
  18.3 7.7 %collective-permute-start.5 = (f32[312,128]{1,0:T(8,128)S(1)}, f32[312,128]{1,0:T(8,128)S(1)}, u32[]{:S(2)}, u32[]{:S(2)}) collective-permute-start(f32[312,128]{1,0:T(8,128)S(1)} %get-tuple-element.24), channel_id=1, source_target_pairs={{0,2},{2,0},{4,6},{6,4},{1,3},{3,1},{5,7},{7,5},{8,10},{10,8},{12,... | collective-permute-start | bytes 479240 | tf_op jit(solution)/shard_map/ppermute | solution.py:580
